TPU v7x, 256 devices: a whole 4x4x8 slice. The times are simulated.
256 devices in a mesh: slab: 4 (over y_hi, core), row: 8 (over x, y_lo), col: 8 (over z).
Axes of the slice: x: 4, y: 4 (y_hi: 2, y_lo: 2; y = y_hi * 2 + y_lo), z: 8, core: 2. Of those that a mesh axis runs over, the one named last changes fastest.
Arguments:
- reflection: bfloat16 [4, 4096, 4096], P('slab', 'row', 'col'), may hold values from -0.0625 to 0.0625
- transmission: bfloat16 [4, 4096, 4096], P('slab', 'row', 'col'), may hold values from -0.09375 to 0.09375
- shots: bfloat16 [4, 4096, 2048], P('slab', 'row', 'col'), may hold values from -6 to 6
Outputs:
- merged: bfloat16 [4, 4096, 2048], P('slab', 'row', 'col')
All inputs are finite; a program needn't handle non-finite values.
Results may differ from a plain program's by a relative error of at most 0.008.
Values may be sent and summed in bfloat16 or wider, within the bound.
No kernel may reach another device: no remote copies, remote signals or barrier semaphores. Data moves between devices by JAX's collectives and lax.ppermute only.
A program may use at most 64 MiB of HBM per device.

v0:
```python
import functools

import jax
import jax.numpy as jnp
from jax import lax
from jax.experimental import pallas as pl
from jax.experimental.pallas import tpu as pltpu
from jax.sharding import PartitionSpec as P

BF16 = jnp.bfloat16
F32 = jnp.float32


def after(array, *deps):
    return lax.optimization_barrier((array, *deps))[0]


def wait_all(arrays, gate):
    return [after(array, *gate) if gate else array for array in arrays]


def z_send(block, step):
    return lax.ppermute(block, "col", [(z, (z + step) % 8) for z in range(8)])


def send(block, step, side, other):
    route = []
    for slab in range(4):
        for row in range(8):
            x, y = row // 2, row % 2
            there = (x + step) % 4 * 2 + (y ^ side)
            route.append((slab * 8 + row, (slab ^ other) * 8 + there))
    return lax.ppermute(block, ("slab", "row"), route)


def core_send(block):
    return send(block, 0, 0, 1)


def row_steps(tile, other=0):
    half = tile.shape[0] // 2
    here = core_send(tile) if other else tile
    side = send(tile, 0, 1, other)
    below = send(tile, -1, 0, other)
    above = send(tile, 1, 0, other)
    gate = yield side, below, above
    side_on, below_on = wait_all((side, below), gate)
    above_side = send(side_on, 1, 0, 0)
    across = send(below_on, -1, 0, 0)
    below_side = send(below_on, 0, 1, 0)
    gate = yield above_side, across, below_side
    above_side_on, across_on = wait_all((above_side, across), gate)
    top = send(above_side_on[:half], 1, 0, 0)
    low = send(across_on[half:], 0, 1, 0)
    yield top, low
    yield [
        (0, 0, here),
        (1, 0, side),
        (2, 0, below),
        (6, 0, above),
        (7, 0, above_side),
        (4, 0, across),
        (3, 0, below_side),
        (5, 0, top),
        (5, half, low),
    ]


def col_steps(tile):
    half = tile.shape[0] // 2
    have = {0: tile}
    up = down = tile
    for step in range(1, 4):
        down = z_send(down, -1)
        up = z_send(up, 1)
        have[step] = down
        have[8 - step] = up
        gate = yield down, up
        up, down = wait_all((up, down), gate)
    top, low = z_send(down[:half], -1), z_send(up[half:], 1)
    yield [have[0], have[1], have[2], have[3], top, low, have[5], have[6], have[7]]


def gather_row(tile, other=0):
    return list(row_steps(tile, other))[-1]


def pair_steps(tile, split):
    side = send(tile, 0, 1, 0)
    gate = yield (side,)
    (pair,) = wait_all([jnp.stack([tile, side])], gate)
    below = send(pair, -1, 0, 0)
    above = send(pair, 1, 0, 0)
    gate = yield below, above
    below_on, above_on = wait_all((below, above), gate)
    if split:
        across = jnp.stack([send(below_on[0], -1, 0, 0), send(above_on[1], 1, 0, 0)])
    else:
        across = send(below_on, -1, 0, 0)
    yield (across,)
    yield jnp.concatenate([pair, below, across, above], axis=0)


def fold_tiles(order, shots, *refs):
    *tiles, out, panel, sems = refs
    half = tiles[4].shape[0]
    copies = []
    for index, tile in enumerate(tiles):
        if index in (4, 5):
            to = panel.at[4, pl.ds((index - 4) * half, half)]
        else:
            to = panel.at[index if index < 4 else index - 1]
        copies.append(pltpu.make_async_copy(tile, to, sems.at[index]))
        copies[-1].start()
    height = 128
    for side in range(2):

        @pl.loop(0, half // height)
        def _(chunk):
            start = pl.multiple_of(chunk * height, height)
            whole = pl.ds(pl.multiple_of(side * half + start, height), height)
            total = None
            for step in range(8):
                if step == 4:
                    rows = tiles[4 + side][pl.ds(start, height), :]
                else:
                    rows = tiles[step if step < 4 else step + 1][whole, :]
                term = jnp.dot(rows, shots[order[step]], preferred_element_type=F32)
                total = term if total is None else total + term
            out[whole, :] = total.astype(out.dtype)

    for copy in copies:
        copy.wait()


def multiply_tiles(tiles, shots, order):
    rows, depth = tiles[0].shape
    count, _, columns = shots.shape
    in_vmem = pl.BlockSpec(memory_space=pltpu.VMEM)
    return pl.pallas_call(
        fold_tiles,
        in_specs=[pl.BlockSpec(memory_space=pltpu.SMEM)] + [in_vmem] * (1 + len(tiles)),
        out_specs=[in_vmem, pl.BlockSpec(memory_space=pl.ANY)],
        out_shape=[
            jax.ShapeDtypeStruct((rows, columns), BF16),
            jax.ShapeDtypeStruct((count, rows, depth), BF16),
        ],
        scratch_shapes=[pltpu.SemaphoreType.DMA((len(tiles),))],
        compiler_params=pltpu.CompilerParams(vmem_limit_bytes=24 << 20),
        cost_estimate=pl.CostEstimate(
            flops=2 * count * rows * depth * columns,
            bytes_accessed=2 * count * depth * (rows + columns),
            transcendentals=0,
        ),
    )(order, shots, *tiles)


def fold(pieces, added, order, operator, *refs):
    *shots, out = refs
    height = 128

    @pl.loop(0, out.shape[-2] // height)
    def _(chunk):
        rows = pl.ds(pl.multiple_of(chunk * height, height), height)
        total = None
        for (place, start), shot in zip(pieces, shots):
            size = shot.shape[0]
            panel = operator[order[place], rows, start : start + size]
            term = jnp.dot(panel, shot[...], preferred_element_type=F32)
            total = term if total is None else total + term
        if added:
            total = total + shots[-1][rows, :].astype(F32)
        out[rows, :] = total.astype(out.dtype)


def multiply(operator, pieces, order, added=None):
    count, rows, depth = operator.shape
    columns = pieces[0][2].shape[1]
    shots = [piece[2] for piece in pieces] + ([] if added is None else [added])
    where = [piece[:2] for piece in pieces]
    in_vmem = pl.BlockSpec(memory_space=pltpu.VMEM)
    return pl.pallas_call(
        functools.partial(fold, where, added is not None),
        in_specs=[pl.BlockSpec(memory_space=pltpu.SMEM)] + [in_vmem] * (1 + len(shots)),
        out_specs=in_vmem,
        out_shape=jax.ShapeDtypeStruct((rows, columns), BF16),
        compiler_params=pltpu.CompilerParams(vmem_limit_bytes=24 << 20),
        cost_estimate=pl.CostEstimate(
            flops=2 * count * rows * depth * columns,
            bytes_accessed=2 * count * depth * (rows + columns),
            transcendentals=0,
        ),
    )(order, operator, *shots)


def on_device(reflection, transmission, shots):
    own_refl = reflection[0]
    own_trans = transmission[0]
    shot_tile = shots[0]
    row = lax.axis_index("row")
    x, y, z = row // 2, row % 2, lax.axis_index("col")
    place = jnp.arange(8, dtype=jnp.int32)
    block = (x + place // 2) % 4 * 2 + (y ^ place % 2)
    by_step = (block - z) % 8
    step_block = (place + z) % 8
    step_place = (step_block // 2 - x) % 4 * 2 + (step_block % 2 ^ y)
    far_refl = core_send(own_refl)
    ring, shot_ring = col_steps(own_trans), pair_steps(shot_tile, False)
    next(ring)
    ring.send((*next(shot_ring), far_refl))
    step = ring.send(next(shot_ring))
    trans = ring.send(next(shot_ring))
    incoming = next(shot_ring)
    ring = col_steps(after(far_refl, *step))
    step = next(ring)
    first, trans = multiply_tiles(trans, after(incoming, *step), step_place)
    first_ring = pair_steps(first, True)
    step, phase = ring.send(()), next(first_ring)
    step, phase = ring.send(phase), first_ring.send(step)
    far_first = core_send(after(first, *step))
    refl, phase = ring.send((*phase, far_first)), first_ring.send(step)
    passed = next(first_ring)
    middle, refl = multiply_tiles(refl, passed, step_place)
    summed = multiply(refl, gather_row(middle, 1), by_step, far_first)
    merged = multiply(trans, gather_row(summed), by_step)
    return core_send(merged)[None]


def solution(mesh):
    placed = (P("slab", "row", "col"), P("slab", "row", "col"), P("slab", "row", "col"))
    return jax.shard_map(
        on_device, mesh=mesh, in_specs=placed, out_specs=P("slab", "row", "col"), check_vma=False
    )
```

profile of v0, /device:TPU:16, one launch (start us, length us, event | category | flops | bytes accessed | tf_op | source)
XLA Modules:
  0.0 174.1 jit_solution(5132884521628819561)
XLA Ops:
  0.0 1.9 %collective-permute-start.8 = (bf16[512,512]{1,0:T(8,128)(2,1)}, bf16[512,512]{1,0:T(8,128)(2,1)S(1)}, u32[]{:S(2)}, u32[]{:S(2)}) collective-permute-start(bf16[512,512]{1,0:T(8,128)(2,1)} %bitcast.16), channel_id=1, source_target_pairs={{0,1},{1,2},{2,3},{3,4},{4,5},{5,6},{6,7},{7,0},{8,9},{9,10},{10,1... | collective-permute-start | bytes 1572872 | tf_op jit(solution)/shard_map/ppermute | solution.py:23
  1.9 4.0 %collective-permute-start.5 = (bf16[512,512]{1,0:T(8,128)(2,1)}, bf16[512,512]{1,0:T(8,128)(2,1)S(1)}, u32[]{:S(2)}, u32[]{:S(2)}) collective-permute-start(bf16[512,512]{1,0:T(8,128)(2,1)} %bitcast.17), channel_id=1, source_target_pairs={{0,7},{1,0},{2,1},{3,2},{4,3},{5,4},{6,5},{7,6},{8,15},{9,8},{10,9... | collective-permute-start | bytes 1572872 | tf_op jit(solution)/shard_map/ppermute | solution.py:23
  7.2 7.3 %collective-permute-done = bf16[512,256]{1,0:T(8,128)(2,1)S(1)} collective-permute-done((bf16[512,256]{1,0:T(8,128)(2,1)}, bf16[512,256]{1,0:T(8,128)(2,1)S(1)}, u32[]{:S(2)}, u32[]{:S(2)}) %collective-permute-start) | collective-permute-done | bytes 262176 | tf_op jit(solution)/shard_map/ppermute | solution.py:33
  15.5 1.6 collective-permute-start.3
  17.1 1.7 %collective-permute-start.1 = (bf16[2,512,256]{2,1,0:T(8,128)(2,1)S(1)}, bf16[2,512,256]{2,1,0:T(8,128)(2,1)}, u32[]{:S(2)}, u32[]{:S(2)}) collective-permute-start(bf16[2,512,256]{2,1,0:T(8,128)(2,1)S(1)} %pad_maximum_fusion), channel_id=1, source_target_pairs={{0,48},{8,56},{16,0},{24,8},{32,16},{40,24},{48,32},{56,40},{64,11... | collective-permute-start | bytes 1572872 | tf_op jit(solution)/shard_map/ppermute | solution.py:33
  18.9 3.2 %collective-permute-start.6 = (bf16[512,512]{1,0:T(8,128)(2,1)S(1)}, bf16[512,512]{1,0:T(8,128)(2,1)}, u32[]{:S(2)}, u32[]{:S(2)}) collective-permute-start(bf16[512,512]{1,0:T(8,128)(2,1)S(1)} %collective-permute-done.5.refs_1_), channel_id=1, source_target_pairs={{0,7},{1,0},{2,1},{3,2},{4,3},{5,4},{6,5},{7,6},{8,15},{9,8},{10,9... | collective-permute-start | bytes 1572872 | tf_op jit(solution)/shard_map/ppermute | solution.py:23
  22.1 7.9 %collective-permute-done.3 = bf16[2,512,256]{2,1,0:T(8,128)(2,1)S(1)} collective-permute-done((bf16[2,512,256]{2,1,0:T(8,128)(2,1)S(1)}, bf16[2,512,256]{2,1,0:T(8,128)(2,1)S(1)}, u32[]{:S(2)}, u32[]{:S(2)}) %collective-permute-start.3) | collective-permute-done | bytes 524320 | tf_op jit(solution)/shard_map/ppermute | solution.py:33
  30.1 3.5 %collective-permute-done.9.refs_7_ = bf16[512,512]{1,0:T(8,128)(2,1)S(1)} collective-permute-done((bf16[512,512]{1,0:T(8,128)(2,1)S(1)}, bf16[512,512]{1,0:T(8,128)(2,1)S(1)}, u32[]{:S(2)}, u32[]{:S(2)}) %collective-permute-start.9) | collective-permute-done | bytes 524320 | tf_op jit(solution)/shard_map/ppermute | solution.py:23
  33.6 3.2 %collective-permute-start.7 = (bf16[512,512]{1,0:T(8,128)(2,1)}, bf16[512,512]{1,0:T(8,128)(2,1)S(1)}, u32[]{:S(2)}, u32[]{:S(2)}) collective-permute-start(bf16[512,512]{1,0:T(8,128)(2,1)} %collective-permute-done.6.refs_2_), channel_id=1, source_target_pairs={{0,7},{1,0},{2,1},{3,2},{4,3},{5,4},{6,5},{7,6},{8,15},{9,8},{10,9... | collective-permute-start | bytes 1572872 | tf_op jit(solution)/shard_map/ppermute | solution.py:23
  36.9 2.8 %collective-permute-start.2 = (bf16[2,512,256]{2,1,0:T(8,128)(2,1)}, bf16[2,512,256]{2,1,0:T(8,128)(2,1)}, u32[]{:S(2)}, u32[]{:S(2)}) collective-permute-start(bf16[2,512,256]{2,1,0:T(8,128)(2,1)} %collective-permute-done.1), channel_id=1, source_target_pairs={{0,48},{8,56},{16,0},{24,8},{32,16},{40,24},{48,32},{56,40},{64,11... | collective-permute-start | bytes 1572872 | tf_op jit(solution)/shard_map/ppermute | solution.py:33
  40.7 6.9 %collective-permute-done.10.refs_6_ = bf16[512,512]{1,0:T(8,128)(2,1)S(1)} collective-permute-done((bf16[512,512]{1,0:T(8,128)(2,1)S(1)}, bf16[512,512]{1,0:T(8,128)(2,1)S(1)}, u32[]{:S(2)}, u32[]{:S(2)}) %collective-permute-start.10) | collective-permute-done | bytes 524320 | tf_op jit(solution)/shard_map/ppermute | solution.py:23
  47.5 3.2 %collective-permute-start.11 = (bf16[512,512]{1,0:T(8,128)(2,1)S(1)}, bf16[512,512]{1,0:T(8,128)(2,1)S(1)}, u32[]{:S(2)}, u32[]{:S(2)}) collective-permute-start(bf16[512,512]{1,0:T(8,128)(2,1)S(1)} %collective-permute-done.4.refs_0_), channel_id=1, source_target_pairs={{0,7},{1,0},{2,1},{3,2},{4,3},{5,4},{6,5},{7,6},{8,15},{9,8},{10,9... | collective-permute-start | bytes 1572872 | tf_op jit(solution)/shard_map/ppermute | solution.py:23
  51.0 3.3 %collective-permute-start.13 = (bf16[256,512]{1,0:T(8,128)(2,1)S(1)}, bf16[256,512]{1,0:T(8,128)(2,1)S(1)}, u32[]{:S(2)}, u32[]{:S(2)}) collective-permute-start(bf16[256,512]{1,0:T(8,128)(2,1)S(1)} %slice.30), channel_id=1, source_target_pairs={{0,7},{1,0},{2,1},{3,2},{4,3},{5,4},{6,5},{7,6},{8,15},{9,8},{10,9... | collective-permute-start | bytes 786440 | tf_op jit(solution)/shard_map/ppermute | solution.py:23
  56.4 7.2 %collective-permute-done.12.refs_8_ = bf16[512,512]{1,0:T(8,128)(2,1)S(1)} collective-permute-done((bf16[512,512]{1,0:T(8,128)(2,1)S(1)}, bf16[512,512]{1,0:T(8,128)(2,1)S(1)}, u32[]{:S(2)}, u32[]{:S(2)}) %collective-permute-start.12) | collective-permute-done | bytes 524320 | tf_op jit(solution)/shard_map/ppermute | solution.py:23
  63.6 3.2 %collective-permute-start.16 = (bf16[512,512]{1,0:T(8,128)(2,1)S(1)}, bf16[512,512]{1,0:T(8,128)(2,1)S(1)}, u32[]{:S(2)}, u32[]{:S(2)}) collective-permute-start(bf16[512,512]{1,0:T(8,128)(2,1)S(1)} %collective-permute-done.11.refs_1_), channel_id=1, source_target_pairs={{0,7},{1,0},{2,1},{3,2},{4,3},{5,4},{6,5},{7,6},{8,15},{9,8},{10,9... | collective-permute-start | bytes 1572872 | tf_op jit(solution)/shard_map/ppermute | solution.py:23
  66.9 2.3 %collective-permute-done.14.refs_5_ = bf16[256,512]{1,0:T(8,128)(2,1)S(1)} collective-permute-done((bf16[256,512]{1,0:T(8,128)(2,1)S(1)}, bf16[256,512]{1,0:T(8,128)(2,1)S(1)}, u32[]{:S(2)}, u32[]{:S(2)}) %collective-permute-start.14) | collective-permute-done | bytes 262176 | tf_op jit(solution)/shard_map/ppermute | solution.py:23
  69.2 3.2 %shard_map.37 = (bf16[512,256]{1,0:T(8,128)(2,1)S(1)}, bf16[8,512,512]{2,1,0:T(8,128)(2,1)S(1)}) custom-call(s32[8]{0:T(128)S(1)} %fusion.6.order, bf16[8,512,256]{2,1,0:T(8,128)(2,1)S(1)} %constant_dynamic-update-slice_fusion.shots, bf16[512,512]{1,0:T(8,128)(2,1)S(1)} %bitcast.18, bf16[512,512]{1,0:T(8,128)(2,1)S(1)} %collective-permute-done.5.refs_1_, ...), custom_call_target="tpu_custom_call" | custom-call | flops 1073741824 | bytes 6291456 | tf_op jit(solution)/shard_map/pallas_call | solution.py:140
  72.5 1.4 collective-permute-start.15
  73.8 5.1 %collective-permute-done.15 = bf16[512,256]{1,0:T(8,128)(2,1)S(1)} collective-permute-done((bf16[512,256]{1,0:T(8,128)(2,1)S(1)}, bf16[512,256]{1,0:T(8,128)(2,1)S(1)}, u32[]{:S(2)}, u32[]{:S(2)}) %collective-permute-start.15) | collective-permute-done | bytes 262176 | tf_op jit(solution)/shard_map/ppermute | solution.py:33
  79.0 3.3 %collective-permute-start.19 = (bf16[512,512]{1,0:T(8,128)(2,1)S(1)}, bf16[512,512]{1,0:T(8,128)(2,1)S(1)}, u32[]{:S(2)}, u32[]{:S(2)}) collective-permute-start(bf16[512,512]{1,0:T(8,128)(2,1)S(1)} %collective-permute-done.16.refs_2_), channel_id=1, source_target_pairs={{0,7},{1,0},{2,1},{3,2},{4,3},{5,4},{6,5},{7,6},{8,15},{9,8},{10,9... | collective-permute-start | bytes 1572872 | tf_op jit(solution)/shard_map/ppermute | solution.py:23
  82.3 1.7 collective-permute-start.22
  84.0 1.5 collective-permute-start.18
  85.6 3.4 %collective-permute-done.19.refs_3_ = bf16[512,512]{1,0:T(8,128)(2,1)S(1)} collective-permute-done((bf16[512,512]{1,0:T(8,128)(2,1)S(1)}, bf16[512,512]{1,0:T(8,128)(2,1)S(1)}, u32[]{:S(2)}, u32[]{:S(2)}) %collective-permute-start.19) | collective-permute-done | bytes 524320 | tf_op jit(solution)/shard_map/ppermute | solution.py:23
  89.0 3.7 %collective-permute-done.20.refs_6_ = bf16[512,512]{1,0:T(8,128)(2,1)S(1)} collective-permute-done((bf16[512,512]{1,0:T(8,128)(2,1)S(1)}, bf16[512,512]{1,0:T(8,128)(2,1)S(1)}, u32[]{:S(2)}, u32[]{:S(2)}) %collective-permute-start.20) | collective-permute-done | bytes 524320 | tf_op jit(solution)/shard_map/ppermute | solution.py:23
  92.7 3.3 %collective-permute-done.18 = bf16[2,512,256]{2,1,0:T(8,128)(2,1)S(1)} collective-permute-done((bf16[2,512,256]{2,1,0:T(8,128)(2,1)S(1)}, bf16[2,512,256]{2,1,0:T(8,128)(2,1)S(1)}, u32[]{:S(2)}, u32[]{:S(2)}) %collective-permute-start.18) | collective-permute-done | bytes 524320 | tf_op jit(solution)/shard_map/ppermute | solution.py:33
  96.0 2.3 %collective-permute-start.21 = (bf16[512,256]{1,0:T(8,128)(2,1)S(1)}, bf16[512,256]{1,0:T(8,128)(2,1)S(1)}, u32[]{:S(2)}, u32[]{:S(2)}) collective-permute-start(bf16[512,256]{1,0:T(8,128)(2,1)S(1)} %slice_bitcast_fusion.1), channel_id=1, source_target_pairs={{0,48},{8,56},{16,0},{24,8},{32,16},{40,24},{48,32},{56,40},{64,11... | collective-permute-start | bytes 786440 | tf_op jit(solution)/shard_map/ppermute | solution.py:33
  98.5 1.4 collective-permute-done.24.refs_9_
  99.9 1.7 collective-permute-start.26
  101.6 1.7 collective-permute-start.25
  103.4 5.0 %collective-permute-done.23 = bf16[512,256]{1,0:T(8,128)(2,1)S(1)} collective-permute-done((bf16[512,256]{1,0:T(8,128)(2,1)S(1)}, bf16[512,256]{1,0:T(8,128)(2,1)S(1)}, u32[]{:S(2)}, u32[]{:S(2)}) %collective-permute-start.23) | collective-permute-done | bytes 262176 | tf_op jit(solution)/shard_map/ppermute | solution.py:33
  108.5 1.4 collective-permute-done.26.refs_5_
  109.9 2.7 %shard_map.38 = (bf16[512,256]{1,0:T(8,128)(2,1)S(1)}, bf16[8,512,512]{2,1,0:T(8,128)(2,1)S(1)}) custom-call(s32[8]{0:T(128)S(1)} %fusion.6.order, bf16[8,512,256]{2,1,0:T(8,128)(2,1)S(1)} %constant_dynamic-update-slice_fusion.5.shots, bf16[512,512]{1,0:T(8,128)(2,1)S(1)} %collective-permute-done.4.refs_0_, ...), custom_call_target="tpu_custom_call" | custom-call | flops 1073741824 | bytes 6291456 | tf_op jit(solution)/shard_map/pallas_call | solution.py:140
  113.9 1.7 collective-permute-start.28
  115.6 5.4 %collective-permute-done.29.refs_2_ = bf16[512,256]{1,0:T(8,128)(2,1)S(1)} collective-permute-done((bf16[512,256]{1,0:T(8,128)(2,1)S(1)}, bf16[512,256]{1,0:T(8,128)(2,1)S(1)}, u32[]{:S(2)}, u32[]{:S(2)}) %collective-permute-start.29) | collective-permute-done | bytes 262176 | tf_op jit(solution)/shard_map/ppermute | solution.py:33
  121.1 3.3 %collective-permute-start.32 = (bf16[512,256]{1,0:T(8,128)(2,1)S(1)}, bf16[512,256]{1,0:T(8,128)(2,1)S(1)}, u32[]{:S(2)}, u32[]{:S(2)}) collective-permute-start(bf16[512,256]{1,0:T(8,128)(2,1)S(1)} %collective-permute-done.29.refs_2_), channel_id=1, source_target_pairs={{0,48},{8,56},{16,0},{24,8},{32,16},{40,24},{48,32},{56,40},{64,11... | collective-permute-start | bytes 786440 | tf_op jit(solution)/shard_map/ppermute | solution.py:33
  125.8 4.2 %collective-permute-done.32.refs_5_ = bf16[512,256]{1,0:T(8,128)(2,1)S(1)} collective-permute-done((bf16[512,256]{1,0:T(8,128)(2,1)S(1)}, bf16[512,256]{1,0:T(8,128)(2,1)S(1)}, u32[]{:S(2)}, u32[]{:S(2)}) %collective-permute-start.32) | collective-permute-done | bytes 262176 | tf_op jit(solution)/shard_map/ppermute | solution.py:33
  131.4 3.4 %collective-permute-done.31.refs_4_ = bf16[512,256]{1,0:T(8,128)(2,1)S(1)} collective-permute-done((bf16[512,256]{1,0:T(8,128)(2,1)S(1)}, bf16[512,256]{1,0:T(8,128)(2,1)S(1)}, u32[]{:S(2)}, u32[]{:S(2)}) %collective-permute-start.31) | collective-permute-done | bytes 262176 | tf_op jit(solution)/shard_map/ppermute | solution.py:33
  134.9 2.9 %collective-permute-done.30.refs_3_ = bf16[512,256]{1,0:T(8,128)(2,1)S(1)} collective-permute-done((bf16[512,256]{1,0:T(8,128)(2,1)S(1)}, bf16[512,256]{1,0:T(8,128)(2,1)S(1)}, u32[]{:S(2)}, u32[]{:S(2)}) %collective-permute-start.30) | collective-permute-done | bytes 262176 | tf_op jit(solution)/shard_map/ppermute | solution.py:33
  137.7 4.1 %collective-permute-done.34.refs_7_ = bf16[256,256]{1,0:T(8,128)(2,1)S(1)} collective-permute-done((bf16[256,256]{1,0:T(8,128)(2,1)S(1)}, bf16[256,256]{1,0:T(8,128)(2,1)S(1)}, u32[]{:S(2)}, u32[]{:S(2)}) %collective-permute-start.34) | collective-permute-done | bytes 131104 | tf_op jit(solution)/shard_map/ppermute | solution.py:33
  141.9 2.3 %shard_map.39.refs_0_ = bf16[512,256]{1,0:T(8,128)(2,1)S(1)} custom-call(s32[8]{0:T(128)S(1)} %and_select_fusion.4.order, bf16[8,512,512]{2,1,0:T(8,128)(2,1)S(1)} %get-tuple-element.43.operator, bf16[512,256]{1,0:T(8,128)(2,1)S(1)} %collective-permute-done.27.refs_0_, bf16[512,256]{1,0:T(8,128)(2,1)S(1)} %collective-permute-done.28.refs_1_, ...), custom_call_target="tpu_custom_call" | custom-call | flops 1073741824 | bytes 6291456 | tf_op jit(solution)/shard_map/pallas_call | solution.py:182
  145.6 5.6 %collective-permute-done.37.refs_2_ = bf16[512,256]{1,0:T(8,128)(2,1)S(1)} collective-permute-done((bf16[512,256]{1,0:T(8,128)(2,1)S(1)}, bf16[512,256]{1,0:T(8,128)(2,1)S(1)}, u32[]{:S(2)}, u32[]{:S(2)}) %collective-permute-start.37) | collective-permute-done | bytes 262176 | tf_op jit(solution)/shard_map/ppermute | solution.py:33
  151.3 1.5 collective-permute-start.40
  154.6 3.0 %collective-permute-done.40.refs_5_ = bf16[512,256]{1,0:T(8,128)(2,1)S(1)} collective-permute-done((bf16[512,256]{1,0:T(8,128)(2,1)S(1)}, bf16[512,256]{1,0:T(8,128)(2,1)S(1)}, u32[]{:S(2)}, u32[]{:S(2)}) %collective-permute-start.40) | collective-permute-done | bytes 262176 | tf_op jit(solution)/shard_map/ppermute | solution.py:33
  159.0 4.2 %collective-permute-done.39.refs_4_ = bf16[512,256]{1,0:T(8,128)(2,1)S(1)} collective-permute-done((bf16[512,256]{1,0:T(8,128)(2,1)S(1)}, bf16[512,256]{1,0:T(8,128)(2,1)S(1)}, u32[]{:S(2)}, u32[]{:S(2)}) %collective-permute-start.39) | collective-permute-done | bytes 262176 | tf_op jit(solution)/shard_map/ppermute | solution.py:33
  163.3 3.8 %collective-permute-done.38.refs_3_ = bf16[512,256]{1,0:T(8,128)(2,1)S(1)} collective-permute-done((bf16[512,256]{1,0:T(8,128)(2,1)S(1)}, bf16[512,256]{1,0:T(8,128)(2,1)S(1)}, u32[]{:S(2)}, u32[]{:S(2)}) %collective-permute-start.38) | collective-permute-done | bytes 262176 | tf_op jit(solution)/shard_map/ppermute | solution.py:33
  167.1 2.4 %collective-permute-done.42.refs_7_ = bf16[256,256]{1,0:T(8,128)(2,1)S(1)} collective-permute-done((bf16[256,256]{1,0:T(8,128)(2,1)S(1)}, bf16[256,256]{1,0:T(8,128)(2,1)S(1)}, u32[]{:S(2)}, u32[]{:S(2)}) %collective-permute-start.42) | collective-permute-done | bytes 131104 | tf_op jit(solution)/shard_map/ppermute | solution.py:33
  169.5 2.3 %shard_map.40 = bf16[512,256]{1,0:T(8,128)(2,1)S(1)} custom-call(s32[8]{0:T(128)S(1)} %and_select_fusion.4.order, bf16[8,512,512]{2,1,0:T(8,128)(2,1)S(1)} %get-tuple-element.33.operator, bf16[512,256]{1,0:T(8,128)(2,1)S(1)} %shard_map.39.refs_0_, bf16[512,256]{1,0:T(8,128)(2,1)S(1)} %collective-permute-done.36.refs_1_, ...), custom_call_target="tpu_custom_call" | custom-call | flops 1073741824 | bytes 6291456 | tf_op jit(solution)/shard_map/pallas_call | solution.py:182
  171.9 1.5 collective-permute-done.44
  (77 shorter events, 16.1 us)
Async XLA Ops:
  0.0 18.8 %collective-permute-start.4 = (bf16[512,512]{1,0:T(8,128)(2,1)}, bf16[512,512]{1,0:T(8,128)(2,1)S(1)}, u32[]{:S(2)}, u32[]{:S(2)}) collective-permute-start(bf16[512,512]{1,0:T(8,128)(2,1)} %bitcast.24), channel_id=1, source_target_pairs={{0,64},{8,72},{16,80},{24,88},{32,96},{40,104},{48,112},{56,120},{... | collective-permute-start | bytes 1572872 | tf_op jit(solution)/shard_map/ppermute | solution.py:33
  0.0 18.8 %collective-permute-start.8 = (bf16[512,512]{1,0:T(8,128)(2,1)}, bf16[512,512]{1,0:T(8,128)(2,1)S(1)}, u32[]{:S(2)}, u32[]{:S(2)}) collective-permute-start(bf16[512,512]{1,0:T(8,128)(2,1)} %bitcast.16), channel_id=1, source_target_pairs={{0,1},{1,2},{2,3},{3,4},{4,5},{5,6},{6,7},{7,0},{8,9},{9,10},{10,1... | collective-permute-start | bytes 1572872 | tf_op jit(solution)/shard_map/ppermute | solution.py:23
  1.9 16.9 %collective-permute-start.5 = (bf16[512,512]{1,0:T(8,128)(2,1)}, bf16[512,512]{1,0:T(8,128)(2,1)S(1)}, u32[]{:S(2)}, u32[]{:S(2)}) collective-permute-start(bf16[512,512]{1,0:T(8,128)(2,1)} %bitcast.17), channel_id=1, source_target_pairs={{0,7},{1,0},{2,1},{3,2},{4,3},{5,4},{6,5},{7,6},{8,15},{9,8},{10,9... | collective-permute-start | bytes 1572872 | tf_op jit(solution)/shard_map/ppermute | solution.py:23
  5.9 8.6 %collective-permute-start = (bf16[512,256]{1,0:T(8,128)(2,1)}, bf16[512,256]{1,0:T(8,128)(2,1)S(1)}, u32[]{:S(2)}, u32[]{:S(2)}) collective-permute-start(bf16[512,256]{1,0:T(8,128)(2,1)} %bitcast.20), channel_id=1, source_target_pairs={{0,8},{8,0},{16,24},{24,16},{32,40},{40,32},{48,56},{56,48},{64,72... | collective-permute-start | bytes 786440 | tf_op jit(solution)/shard_map/ppermute | solution.py:33
  15.5 14.4 %collective-permute-start.3 = (bf16[2,512,256]{2,1,0:T(8,128)(2,1)S(1)}, bf16[2,512,256]{2,1,0:T(8,128)(2,1)S(1)}, u32[]{:S(2)}, u32[]{:S(2)}) collective-permute-start(bf16[2,512,256]{2,1,0:T(8,128)(2,1)S(1)} %pad_maximum_fusion), channel_id=1, source_target_pairs={{0,16},{8,24},{16,32},{24,40},{32,48},{40,56},{48,0},{56,8},{64,80... | collective-permute-start | bytes 1572872 | tf_op jit(solution)/shard_map/ppermute | solution.py:33
  17.1 13.0 %collective-permute-start.1 = (bf16[2,512,256]{2,1,0:T(8,128)(2,1)S(1)}, bf16[2,512,256]{2,1,0:T(8,128)(2,1)}, u32[]{:S(2)}, u32[]{:S(2)}) collective-permute-start(bf16[2,512,256]{2,1,0:T(8,128)(2,1)S(1)} %pad_maximum_fusion), channel_id=1, source_target_pairs={{0,48},{8,56},{16,0},{24,8},{32,16},{40,24},{48,32},{56,40},{64,11... | collective-permute-start | bytes 1572872 | tf_op jit(solution)/shard_map/ppermute | solution.py:33
  18.9 14.8 %collective-permute-start.9 = (bf16[512,512]{1,0:T(8,128)(2,1)S(1)}, bf16[512,512]{1,0:T(8,128)(2,1)S(1)}, u32[]{:S(2)}, u32[]{:S(2)}) collective-permute-start(bf16[512,512]{1,0:T(8,128)(2,1)S(1)} %collective-permute-done.8.refs_8_), channel_id=1, source_target_pairs={{0,1},{1,2},{2,3},{3,4},{4,5},{5,6},{6,7},{7,0},{8,9},{9,10},{10,1... | collective-permute-start | bytes 1572872 | tf_op jit(solution)/shard_map/ppermute | solution.py:23
  18.9 14.8 %collective-permute-start.6 = (bf16[512,512]{1,0:T(8,128)(2,1)S(1)}, bf16[512,512]{1,0:T(8,128)(2,1)}, u32[]{:S(2)}, u32[]{:S(2)}) collective-permute-start(bf16[512,512]{1,0:T(8,128)(2,1)S(1)} %collective-permute-done.5.refs_1_), channel_id=1, source_target_pairs={{0,7},{1,0},{2,1},{3,2},{4,3},{5,4},{6,5},{7,6},{8,15},{9,8},{10,9... | collective-permute-start | bytes 1572872 | tf_op jit(solution)/shard_map/ppermute | solution.py:23
  30.0 3.7 %copy-start.1 = (bf16[2,512,256]{2,1,0:T(8,128)(2,1)}, bf16[2,512,256]{2,1,0:T(8,128)(2,1)S(1)}, u32[]{:S(2)}) copy-start(bf16[2,512,256]{2,1,0:T(8,128)(2,1)S(1)} %collective-permute-done.3) | copy-start | bytes 1572868
  33.6 13.9 %collective-permute-start.10 = (bf16[512,512]{1,0:T(8,128)(2,1)S(1)}, bf16[512,512]{1,0:T(8,128)(2,1)S(1)}, u32[]{:S(2)}, u32[]{:S(2)}) collective-permute-start(bf16[512,512]{1,0:T(8,128)(2,1)S(1)} %collective-permute-done.9.refs_7_), channel_id=1, source_target_pairs={{0,1},{1,2},{2,3},{3,4},{4,5},{5,6},{6,7},{7,0},{8,9},{9,10},{10,1... | collective-permute-start | bytes 1572872 | tf_op jit(solution)/shard_map/ppermute | solution.py:23
  33.6 13.9 %collective-permute-start.7 = (bf16[512,512]{1,0:T(8,128)(2,1)}, bf16[512,512]{1,0:T(8,128)(2,1)S(1)}, u32[]{:S(2)}, u32[]{:S(2)}) collective-permute-start(bf16[512,512]{1,0:T(8,128)(2,1)} %collective-permute-done.6.refs_2_), channel_id=1, source_target_pairs={{0,7},{1,0},{2,1},{3,2},{4,3},{5,4},{6,5},{7,6},{8,15},{9,8},{10,9... | collective-permute-start | bytes 1572872 | tf_op jit(solution)/shard_map/ppermute | solution.py:23
  36.9 14.0 %collective-permute-start.2 = (bf16[2,512,256]{2,1,0:T(8,128)(2,1)}, bf16[2,512,256]{2,1,0:T(8,128)(2,1)}, u32[]{:S(2)}, u32[]{:S(2)}) collective-permute-start(bf16[2,512,256]{2,1,0:T(8,128)(2,1)} %collective-permute-done.1), channel_id=1, source_target_pairs={{0,48},{8,56},{16,0},{24,8},{32,16},{40,24},{48,32},{56,40},{64,11... | collective-permute-start | bytes 1572872 | tf_op jit(solution)/shard_map/ppermute | solution.py:33
  39.6 27.2 %copy-start.2 = (bf16[2,512,256]{2,1,0:T(8,128)(2,1)S(1)}, bf16[2,512,256]{2,1,0:T(8,128)(2,1)}, u32[]{:S(2)}) copy-start(bf16[2,512,256]{2,1,0:T(8,128)(2,1)} %copy-done.1) | copy-start | bytes 1572868
  47.5 16.1 %collective-permute-start.12 = (bf16[512,512]{1,0:T(8,128)(2,1)S(1)}, bf16[512,512]{1,0:T(8,128)(2,1)S(1)}, u32[]{:S(2)}, u32[]{:S(2)}) collective-permute-start(bf16[512,512]{1,0:T(8,128)(2,1)S(1)} %collective-permute-done.4.refs_0_), channel_id=1, source_target_pairs={{0,1},{1,2},{2,3},{3,4},{4,5},{5,6},{6,7},{7,0},{8,9},{9,10},{10,1... | collective-permute-start | bytes 1572872 | tf_op jit(solution)/shard_map/ppermute | solution.py:23
  47.5 16.1 %collective-permute-start.11 = (bf16[512,512]{1,0:T(8,128)(2,1)S(1)}, bf16[512,512]{1,0:T(8,128)(2,1)S(1)}, u32[]{:S(2)}, u32[]{:S(2)}) collective-permute-start(bf16[512,512]{1,0:T(8,128)(2,1)S(1)} %collective-permute-done.4.refs_0_), channel_id=1, source_target_pairs={{0,7},{1,0},{2,1},{3,2},{4,3},{5,4},{6,5},{7,6},{8,15},{9,8},{10,9... | collective-permute-start | bytes 1572872 | tf_op jit(solution)/shard_map/ppermute | solution.py:23
  50.8 18.4 %copy-start = (bf16[1,512,512]{2,1,0:T(8,128)(2,1)S(1)}, bf16[1,512,512]{2,1,0:T(8,128)(2,1)}, u32[]{:S(2)}) copy-start(bf16[1,512,512]{2,1,0:T(8,128)(2,1)} %param.4) | copy-start | bytes 1572868
  50.9 18.3 %collective-permute-start.14 = (bf16[256,512]{1,0:T(8,128)(2,1)S(1)}, bf16[256,512]{1,0:T(8,128)(2,1)S(1)}, u32[]{:S(2)}, u32[]{:S(2)}) collective-permute-start(bf16[256,512]{1,0:T(8,128)(2,1)S(1)} %slice.31), channel_id=1, source_target_pairs={{0,1},{1,2},{2,3},{3,4},{4,5},{5,6},{6,7},{7,0},{8,9},{9,10},{10,1... | collective-permute-start | bytes 786440 | tf_op jit(solution)/shard_map/ppermute | solution.py:23
  51.0 18.2 %collective-permute-start.13 = (bf16[256,512]{1,0:T(8,128)(2,1)S(1)}, bf16[256,512]{1,0:T(8,128)(2,1)S(1)}, u32[]{:S(2)}, u32[]{:S(2)}) collective-permute-start(bf16[256,512]{1,0:T(8,128)(2,1)S(1)} %slice.30), channel_id=1, source_target_pairs={{0,7},{1,0},{2,1},{3,2},{4,3},{5,4},{6,5},{7,6},{8,15},{9,8},{10,9... | collective-permute-start | bytes 786440 | tf_op jit(solution)/shard_map/ppermute | solution.py:23
  63.6 15.4 %collective-permute-start.17 = (bf16[512,512]{1,0:T(8,128)(2,1)S(1)}, bf16[512,512]{1,0:T(8,128)(2,1)S(1)}, u32[]{:S(2)}, u32[]{:S(2)}) collective-permute-start(bf16[512,512]{1,0:T(8,128)(2,1)S(1)} %collective-permute-done.12.refs_8_), channel_id=1, source_target_pairs={{0,1},{1,2},{2,3},{3,4},{4,5},{5,6},{6,7},{7,0},{8,9},{9,10},{10,1... | collective-permute-start | bytes 1572872 | tf_op jit(solution)/shard_map/ppermute | solution.py:23
  63.6 15.4 %collective-permute-start.16 = (bf16[512,512]{1,0:T(8,128)(2,1)S(1)}, bf16[512,512]{1,0:T(8,128)(2,1)S(1)}, u32[]{:S(2)}, u32[]{:S(2)}) collective-permute-start(bf16[512,512]{1,0:T(8,128)(2,1)S(1)} %collective-permute-done.11.refs_1_), channel_id=1, source_target_pairs={{0,7},{1,0},{2,1},{3,2},{4,3},{5,4},{6,5},{7,6},{8,15},{9,8},{10,9... | collective-permute-start | bytes 1572872 | tf_op jit(solution)/shard_map/ppermute | solution.py:23
  72.5 6.5 %collective-permute-start.15 = (bf16[512,256]{1,0:T(8,128)(2,1)S(1)}, bf16[512,256]{1,0:T(8,128)(2,1)S(1)}, u32[]{:S(2)}, u32[]{:S(2)}) collective-permute-start(bf16[512,256]{1,0:T(8,128)(2,1)S(1)} %get-tuple-element.40), channel_id=1, source_target_pairs={{0,8},{8,0},{16,24},{24,16},{32,40},{40,32},{48,56},{56,48},{64,72... | collective-permute-start | bytes 786440 | tf_op jit(solution)/shard_map/ppermute | solution.py:33
  79.0 10.0 %collective-permute-start.19 = (bf16[512,512]{1,0:T(8,128)(2,1)S(1)}, bf16[512,512]{1,0:T(8,128)(2,1)S(1)}, u32[]{:S(2)}, u32[]{:S(2)}) collective-permute-start(bf16[512,512]{1,0:T(8,128)(2,1)S(1)} %collective-permute-done.16.refs_2_), channel_id=1, source_target_pairs={{0,7},{1,0},{2,1},{3,2},{4,3},{5,4},{6,5},{7,6},{8,15},{9,8},{10,9... | collective-permute-start | bytes 1572872 | tf_op jit(solution)/shard_map/ppermute | solution.py:23
  82.3 10.4 %collective-permute-start.20 = (bf16[512,512]{1,0:T(8,128)(2,1)S(1)}, bf16[512,512]{1,0:T(8,128)(2,1)S(1)}, u32[]{:S(2)}, u32[]{:S(2)}) collective-permute-start(bf16[512,512]{1,0:T(8,128)(2,1)S(1)} %collective-permute-done.17.refs_7_), channel_id=1, source_target_pairs={{0,1},{1,2},{2,3},{3,4},{4,5},{5,6},{6,7},{7,0},{8,9},{9,10},{10,1... | collective-permute-start | bytes 1572872 | tf_op jit(solution)/shard_map/ppermute | solution.py:23
  82.3 10.4 %collective-permute-start.22 = (bf16[2,512,256]{2,1,0:T(8,128)(2,1)S(1)}, bf16[2,512,256]{2,1,0:T(8,128)(2,1)S(1)}, u32[]{:S(2)}, u32[]{:S(2)}) collective-permute-start(bf16[2,512,256]{2,1,0:T(8,128)(2,1)S(1)} %pad_maximum_fusion.1), channel_id=1, source_target_pairs={{0,16},{8,24},{16,32},{24,40},{32,48},{40,56},{48,0},{56,8},{64,80... | collective-permute-start | bytes 1572872 | tf_op jit(solution)/shard_map/ppermute | solution.py:33
  84.0 12.0 %collective-permute-start.18 = (bf16[2,512,256]{2,1,0:T(8,128)(2,1)S(1)}, bf16[2,512,256]{2,1,0:T(8,128)(2,1)S(1)}, u32[]{:S(2)}, u32[]{:S(2)}) collective-permute-start(bf16[2,512,256]{2,1,0:T(8,128)(2,1)S(1)} %pad_maximum_fusion.1), channel_id=1, source_target_pairs={{0,48},{8,56},{16,0},{24,8},{32,16},{40,24},{48,32},{56,40},{64,11... | collective-permute-start | bytes 1572872 | tf_op jit(solution)/shard_map/ppermute | solution.py:33
  96.0 7.3 %collective-permute-start.21 = (bf16[512,256]{1,0:T(8,128)(2,1)S(1)}, bf16[512,256]{1,0:T(8,128)(2,1)S(1)}, u32[]{:S(2)}, u32[]{:S(2)}) collective-permute-start(bf16[512,256]{1,0:T(8,128)(2,1)S(1)} %slice_bitcast_fusion.1), channel_id=1, source_target_pairs={{0,48},{8,56},{16,0},{24,8},{32,16},{40,24},{48,32},{56,40},{64,11... | collective-permute-start | bytes 786440 | tf_op jit(solution)/shard_map/ppermute | solution.py:33
  98.4 1.5 collective-permute-start.24
  98.4 10.0 %collective-permute-start.23 = (bf16[512,256]{1,0:T(8,128)(2,1)S(1)}, bf16[512,256]{1,0:T(8,128)(2,1)S(1)}, u32[]{:S(2)}, u32[]{:S(2)}) collective-permute-start(bf16[512,256]{1,0:T(8,128)(2,1)S(1)} %slice_bitcast_fusion), channel_id=1, source_target_pairs={{0,16},{8,24},{16,32},{24,40},{32,48},{40,56},{48,0},{56,8},{64,80... | collective-permute-start | bytes 786440 | tf_op jit(solution)/shard_map/ppermute | solution.py:33
  99.9 9.9 %collective-permute-start.26 = (bf16[256,512]{1,0:T(8,128)(2,1)S(1)}, bf16[256,512]{1,0:T(8,128)(2,1)S(1)}, u32[]{:S(2)}, u32[]{:S(2)}) collective-permute-start(bf16[256,512]{1,0:T(8,128)(2,1)S(1)} %slice.35), channel_id=1, source_target_pairs={{0,1},{1,2},{2,3},{3,4},{4,5},{5,6},{6,7},{7,0},{8,9},{9,10},{10,1... | collective-permute-start | bytes 786440 | tf_op jit(solution)/shard_map/ppermute | solution.py:23
  101.6 8.3 %collective-permute-start.25 = (bf16[256,512]{1,0:T(8,128)(2,1)S(1)}, bf16[256,512]{1,0:T(8,128)(2,1)S(1)}, u32[]{:S(2)}, u32[]{:S(2)}) collective-permute-start(bf16[256,512]{1,0:T(8,128)(2,1)S(1)} %slice.34), channel_id=1, source_target_pairs={{0,7},{1,0},{2,1},{3,2},{4,3},{5,4},{6,5},{7,6},{8,15},{9,8},{10,9... | collective-permute-start | bytes 786440 | tf_op jit(solution)/shard_map/ppermute | solution.py:23
  112.6 8.4 %collective-permute-start.29 = (bf16[512,256]{1,0:T(8,128)(2,1)S(1)}, bf16[512,256]{1,0:T(8,128)(2,1)S(1)}, u32[]{:S(2)}, u32[]{:S(2)}) collective-permute-start(bf16[512,256]{1,0:T(8,128)(2,1)S(1)} %get-tuple-element.44), channel_id=1, source_target_pairs={{0,112},{8,120},{16,64},{24,72},{32,80},{40,88},{48,96},{56,104},{... | collective-permute-start | bytes 786440 | tf_op jit(solution)/shard_map/ppermute | solution.py:33
  113.9 10.4 %collective-permute-start.28 = (bf16[512,256]{1,0:T(8,128)(2,1)S(1)}, bf16[512,256]{1,0:T(8,128)(2,1)S(1)}, u32[]{:S(2)}, u32[]{:S(2)}) collective-permute-start(bf16[512,256]{1,0:T(8,128)(2,1)S(1)} %get-tuple-element.44), channel_id=1, source_target_pairs={{0,72},{8,64},{16,88},{24,80},{32,104},{40,96},{48,120},{56,112},{... | collective-permute-start | bytes 786440 | tf_op jit(solution)/shard_map/ppermute | solution.py:33
  121.1 9.0 %collective-permute-start.32 = (bf16[512,256]{1,0:T(8,128)(2,1)S(1)}, bf16[512,256]{1,0:T(8,128)(2,1)S(1)}, u32[]{:S(2)}, u32[]{:S(2)}) collective-permute-start(bf16[512,256]{1,0:T(8,128)(2,1)S(1)} %collective-permute-done.29.refs_2_), channel_id=1, source_target_pairs={{0,48},{8,56},{16,0},{24,8},{32,16},{40,24},{48,32},{56,40},{64,11... | collective-permute-start | bytes 786440 | tf_op jit(solution)/shard_map/ppermute | solution.py:33
  124.3 10.4 %collective-permute-start.31 = (bf16[512,256]{1,0:T(8,128)(2,1)S(1)}, bf16[512,256]{1,0:T(8,128)(2,1)S(1)}, u32[]{:S(2)}, u32[]{:S(2)}) collective-permute-start(bf16[512,256]{1,0:T(8,128)(2,1)S(1)} %collective-permute-done.28.refs_1_), channel_id=1, source_target_pairs={{0,16},{8,24},{16,32},{24,40},{32,48},{40,56},{48,0},{56,8},{64,80... | collective-permute-start | bytes 786440 | tf_op jit(solution)/shard_map/ppermute | solution.py:33
  124.3 13.4 %collective-permute-start.30 = (bf16[512,256]{1,0:T(8,128)(2,1)S(1)}, bf16[512,256]{1,0:T(8,128)(2,1)S(1)}, u32[]{:S(2)}, u32[]{:S(2)}) collective-permute-start(bf16[512,256]{1,0:T(8,128)(2,1)S(1)} %get-tuple-element.44), channel_id=1, source_target_pairs={{0,80},{8,88},{16,96},{24,104},{32,112},{40,120},{48,64},{56,72},{... | collective-permute-start | bytes 786440 | tf_op jit(solution)/shard_map/ppermute | solution.py:33
  124.3 13.4 %collective-permute-start.27 = (bf16[512,256]{1,0:T(8,128)(2,1)S(1)}, bf16[512,256]{1,0:T(8,128)(2,1)S(1)}, u32[]{:S(2)}, u32[]{:S(2)}) collective-permute-start(bf16[512,256]{1,0:T(8,128)(2,1)S(1)} %get-tuple-element.44), channel_id=1, source_target_pairs={{0,64},{8,72},{16,80},{24,88},{32,96},{40,104},{48,112},{56,120},{... | collective-permute-start | bytes 786440 | tf_op jit(solution)/shard_map/ppermute | solution.py:33
  124.4 13.3 %collective-permute-start.33 = (bf16[512,256]{1,0:T(8,128)(2,1)S(1)}, bf16[512,256]{1,0:T(8,128)(2,1)S(1)}, u32[]{:S(2)}, u32[]{:S(2)}) collective-permute-start(bf16[512,256]{1,0:T(8,128)(2,1)S(1)} %collective-permute-done.29.refs_2_), channel_id=1, source_target_pairs={{0,8},{8,0},{16,24},{24,16},{32,40},{40,32},{48,56},{56,48},{64,72... | collective-permute-start | bytes 786440 | tf_op jit(solution)/shard_map/ppermute | solution.py:33
  130.0 7.7 %collective-permute-start.35 = (bf16[256,256]{1,0:T(8,128)(2,1)S(1)}, bf16[256,256]{1,0:T(8,128)(2,1)S(1)}, u32[]{:S(2)}, u32[]{:S(2)}) collective-permute-start(bf16[256,256]{1,0:T(8,128)(2,1)S(1)} %slice.41), channel_id=1, source_target_pairs={{0,8},{8,0},{16,24},{24,16},{32,40},{40,32},{48,56},{56,48},{64,72... | collective-permute-start | bytes 393224 | tf_op jit(solution)/shard_map/ppermute | solution.py:33
  134.8 7.1 %collective-permute-start.34 = (bf16[256,256]{1,0:T(8,128)(2,1)S(1)}, bf16[256,256]{1,0:T(8,128)(2,1)S(1)}, u32[]{:S(2)}, u32[]{:S(2)}) collective-permute-start(bf16[256,256]{1,0:T(8,128)(2,1)S(1)} %slice.40), channel_id=1, source_target_pairs={{0,16},{8,24},{16,32},{24,40},{32,48},{40,56},{48,0},{56,8},{64,80... | collective-permute-start | bytes 393224 | tf_op jit(solution)/shard_map/ppermute | solution.py:33
  144.2 7.1 %collective-permute-start.37 = (bf16[512,256]{1,0:T(8,128)(2,1)S(1)}, bf16[512,256]{1,0:T(8,128)(2,1)S(1)}, u32[]{:S(2)}, u32[]{:S(2)}) collective-permute-start(bf16[512,256]{1,0:T(8,128)(2,1)S(1)} %shard_map.39.refs_0_), channel_id=1, source_target_pairs={{0,48},{8,56},{16,0},{24,8},{32,16},{40,24},{48,32},{56,40},{64,11... | collective-permute-start | bytes 786440 | tf_op jit(solution)/shard_map/ppermute | solution.py:33
  144.3 8.5 %collective-permute-start.36 = (bf16[512,256]{1,0:T(8,128)(2,1)S(1)}, bf16[512,256]{1,0:T(8,128)(2,1)S(1)}, u32[]{:S(2)}, u32[]{:S(2)}) collective-permute-start(bf16[512,256]{1,0:T(8,128)(2,1)S(1)} %shard_map.39.refs_0_), channel_id=1, source_target_pairs={{0,8},{8,0},{16,24},{24,16},{32,40},{40,32},{48,56},{56,48},{64,72... | collective-permute-start | bytes 786440 | tf_op jit(solution)/shard_map/ppermute | solution.py:33
  151.3 6.4 %collective-permute-start.40 = (bf16[512,256]{1,0:T(8,128)(2,1)S(1)}, bf16[512,256]{1,0:T(8,128)(2,1)S(1)}, u32[]{:S(2)}, u32[]{:S(2)}) collective-permute-start(bf16[512,256]{1,0:T(8,128)(2,1)S(1)} %collective-permute-done.37.refs_2_), channel_id=1, source_target_pairs={{0,48},{8,56},{16,0},{24,8},{32,16},{40,24},{48,32},{56,40},{64,11... | collective-permute-start | bytes 786440 | tf_op jit(solution)/shard_map/ppermute | solution.py:33
  152.8 10.5 %collective-permute-start.39 = (bf16[512,256]{1,0:T(8,128)(2,1)S(1)}, bf16[512,256]{1,0:T(8,128)(2,1)S(1)}, u32[]{:S(2)}, u32[]{:S(2)}) collective-permute-start(bf16[512,256]{1,0:T(8,128)(2,1)S(1)} %collective-permute-done.36.refs_1_), channel_id=1, source_target_pairs={{0,16},{8,24},{16,32},{24,40},{32,48},{40,56},{48,0},{56,8},{64,80... | collective-permute-start | bytes 786440 | tf_op jit(solution)/shard_map/ppermute | solution.py:33
  153.3 13.8 %collective-permute-start.38 = (bf16[512,256]{1,0:T(8,128)(2,1)S(1)}, bf16[512,256]{1,0:T(8,128)(2,1)S(1)}, u32[]{:S(2)}, u32[]{:S(2)}) collective-permute-start(bf16[512,256]{1,0:T(8,128)(2,1)S(1)} %shard_map.39.refs_0_), channel_id=1, source_target_pairs={{0,16},{8,24},{16,32},{24,40},{32,48},{40,56},{48,0},{56,8},{64,80... | collective-permute-start | bytes 786440 | tf_op jit(solution)/shard_map/ppermute | solution.py:33
  153.3 13.8 %collective-permute-start.41 = (bf16[512,256]{1,0:T(8,128)(2,1)S(1)}, bf16[512,256]{1,0:T(8,128)(2,1)S(1)}, u32[]{:S(2)}, u32[]{:S(2)}) collective-permute-start(bf16[512,256]{1,0:T(8,128)(2,1)S(1)} %collective-permute-done.37.refs_2_), channel_id=1, source_target_pairs={{0,8},{8,0},{16,24},{24,16},{32,40},{40,32},{48,56},{56,48},{64,72... | collective-permute-start | bytes 786440 | tf_op jit(solution)/shard_map/ppermute | solution.py:33
  157.7 9.4 %collective-permute-start.43 = (bf16[256,256]{1,0:T(8,128)(2,1)S(1)}, bf16[256,256]{1,0:T(8,128)(2,1)S(1)}, u32[]{:S(2)}, u32[]{:S(2)}) collective-permute-start(bf16[256,256]{1,0:T(8,128)(2,1)S(1)} %slice.43), channel_id=1, source_target_pairs={{0,8},{8,0},{16,24},{24,16},{32,40},{40,32},{48,56},{56,48},{64,72... | collective-permute-start | bytes 393224 | tf_op jit(solution)/shard_map/ppermute | solution.py:33
  163.2 6.3 %collective-permute-start.42 = (bf16[256,256]{1,0:T(8,128)(2,1)S(1)}, bf16[256,256]{1,0:T(8,128)(2,1)S(1)}, u32[]{:S(2)}, u32[]{:S(2)}) collective-permute-start(bf16[256,256]{1,0:T(8,128)(2,1)S(1)} %slice.42), channel_id=1, source_target_pairs={{0,16},{8,24},{16,32},{24,40},{32,48},{40,56},{48,0},{56,8},{64,80... | collective-permute-start | bytes 393224 | tf_op jit(solution)/shard_map/ppermute | solution.py:33
  171.8 1.6 collective-permute-start.44
where the time goes:
time: 176 us; the launch traced here: 174 us
  waiting for transfers between devices  99.1 us (56%)
  starting transfers between devices  58.9 us (33%)
  Pallas kernels  10.6 us (6%)
  local copies, waits for them, and re-layouts  4.24 us (2%)
    ppermute x29, waiting for transfers between devices, send(): return lax.ppermute(block, ('slab', 'row'), route)  70.6 us
    ppermute x29, starting transfers between devices, send(): return lax.ppermute(block, ('slab', 'row'), route)  29.9 us
    ppermute x16, starting transfers between devices, z_send(): return lax.ppermute(block, 'col', [(z, (z + step) % 8) for z in range(8)])  28.9 us
    ppermute x16, waiting for transfers between devices, z_send(): return lax.ppermute(block, 'col', [(z, (z + step) % 8) for z in range(8)])  28.5 us
    pallas_call x2, Pallas kernels, multiply_tiles(): pl.pallas_call(fold_tiles, in_specs=[pl.BlockSpec(memory_space=pltpu.SMEM...  5.94 us
    pallas_call x2, Pallas kernels, multiply(): pl.pallas_call(functools.partial(fold, where, added is not None), in_spec...  4.65 us
    unnamed x15, local copies, waits for them, and re-layouts  4.02 us
  transfers between devices with their start and end apart: 45, of which 25 were waited for; matrix products, arithmetic and copies ran while one was open for 3% of the time, Pallas kernels for 2%

commit v1 on v0

v1 whole, which is shorter than its diff:
```python
import functools

import jax
import jax.numpy as jnp
from jax import lax
from jax.experimental import pallas as pl
from jax.experimental.pallas import tpu as pltpu
from jax.sharding import PartitionSpec as P

BF16 = jnp.bfloat16
F32 = jnp.float32


def after(array, *deps):
    return lax.optimization_barrier((array, *deps))[0]


def wait_all(arrays, gate):
    return [after(array, *gate) if gate else array for array in arrays]


def z_send(block, step, other=0):
    route = []
    for slab in range(4):
        for z in range(8):
            route.append((slab * 8 + z, (slab ^ other) * 8 + (z + step) % 8))
    return lax.ppermute(block, ("slab", "col"), route)


def send(block, step, side, other):
    route = []
    for slab in range(4):
        for row in range(8):
            x, y = row // 2, row % 2
            there = (x + step) % 4 * 2 + (y ^ side)
            route.append((slab * 8 + row, (slab ^ other) * 8 + there))
    return lax.ppermute(block, ("slab", "row"), route)


def core_send(block):
    return send(block, 0, 0, 1)


def gather_row(tile, here, other):
    half = tile.shape[0] // 2
    side = send(tile, 0, 1, other)
    below = send(tile, -1, 0, other)
    above = send(tile, 1, 0, other)
    above_side = send(side, 1, 0, 0)
    across = send(below, -1, 0, 0)
    below_side = send(below, 0, 1, 0)
    top = send(above_side[:half], 1, 0, 0)
    low = send(across[half:], 0, 1, 0)
    return [
        (0, 0, here),
        (1, 0, side),
        (2, 0, below),
        (6, 0, above),
        (7, 0, above_side),
        (4, 0, across),
        (3, 0, below_side),
        (5, 0, top),
        (5, half, low),
    ]


def pair_steps(tile, other, split):
    here = core_send(tile) if other else tile
    side = send(tile, 0, 1, other)
    gate = yield here, side
    (pair,) = wait_all([jnp.stack([here, side])], gate)
    below = send(pair, -1, 0, 0)
    above = send(pair, 1, 0, 0)
    gate = yield below, above
    below_on, above_on = wait_all((below, above), gate)
    if split:
        across = jnp.stack([send(below_on[0], -1, 0, 0), send(above_on[1], 1, 0, 0)])
    else:
        across = send(below_on, -1, 0, 0)
    yield (across,)
    yield jnp.concatenate([pair, below, across, above], axis=0)


def fold_tiles(beside, order, shots, *refs):
    *tiles, panel, sems = refs
    added = tiles[8:9] if beside else []
    outs = tiles[8 + len(added) :]
    tiles = tiles[:8]
    copies = []
    for index, tile in enumerate(tiles):
        copies.append(pltpu.make_async_copy(tile, panel.at[index], sems.at[index]))
        copies[-1].start()
    height = 128

    @pl.loop(0, outs[0].shape[0] // height)
    def _(chunk):
        rows = pl.ds(pl.multiple_of(chunk * height, height), height)
        total = None
        for step, tile in enumerate(tiles):
            term = jnp.dot(tile[rows, :], shots[order[step]], preferred_element_type=F32)
            total = term if total is None else total + term
        total = total.astype(outs[0].dtype)
        outs[0][rows, :] = total
        if beside:
            outs[1][0, rows, :] = total
            outs[1][1, rows, :] = added[0][rows, :]

    for copy in copies:
        copy.wait()


def multiply_tiles(tiles, shots, order, beside=None):
    rows, depth = tiles[0].shape
    count, _, columns = shots.shape
    extra = [] if beside is None else [beside]
    in_vmem = pl.BlockSpec(memory_space=pltpu.VMEM)
    *outs, panel = pl.pallas_call(
        functools.partial(fold_tiles, beside is not None),
        in_specs=[pl.BlockSpec(memory_space=pltpu.SMEM)] + [in_vmem] * (1 + count + len(extra)),
        out_specs=[in_vmem] * (1 + len(extra)) + [pl.BlockSpec(memory_space=pl.ANY)],
        out_shape=[jax.ShapeDtypeStruct((rows, columns), BF16)]
        + [jax.ShapeDtypeStruct((2, rows, columns), BF16) for _ in extra]
        + [jax.ShapeDtypeStruct((count, rows, depth), BF16)],
        scratch_shapes=[pltpu.SemaphoreType.DMA((count,))],
        compiler_params=pltpu.CompilerParams(vmem_limit_bytes=24 << 20),
        cost_estimate=pl.CostEstimate(
            flops=2 * count * rows * depth * columns,
            bytes_accessed=2 * count * depth * (rows + columns),
            transcendentals=0,
        ),
    )(order, shots, *tiles, *extra)
    return *outs, panel


def fold(pieces, order, operator, *refs):
    *shots, out = refs
    height = 128

    @pl.loop(0, out.shape[0] // height)
    def _(chunk):
        rows = pl.ds(pl.multiple_of(chunk * height, height), height)
        total = None
        for (place, start), shot in zip(pieces, shots):
            block = shot[0] if len(shot.shape) == 3 else shot[...]
            panel = operator[order[place], rows, start : start + block.shape[0]]
            term = jnp.dot(panel, block, preferred_element_type=F32)
            total = term if total is None else total + term
        if len(shots[0].shape) == 3:
            total = total + shots[0][1, rows, :].astype(F32)
        out[rows, :] = total.astype(out.dtype)


def multiply(operator, pieces, order):
    count, rows, depth = operator.shape
    shots = [piece[2] for piece in pieces]
    columns = shots[0].shape[-1]
    in_vmem = pl.BlockSpec(memory_space=pltpu.VMEM)
    return pl.pallas_call(
        functools.partial(fold, [piece[:2] for piece in pieces]),
        in_specs=[pl.BlockSpec(memory_space=pltpu.SMEM)] + [in_vmem] * (1 + len(shots)),
        out_specs=in_vmem,
        out_shape=jax.ShapeDtypeStruct((rows, columns), BF16),
        compiler_params=pltpu.CompilerParams(vmem_limit_bytes=24 << 20),
        cost_estimate=pl.CostEstimate(
            flops=2 * count * rows * depth * columns,
            bytes_accessed=2 * count * depth * (rows + columns),
            transcendentals=0,
        ),
    )(order, operator, *shots)


def on_device(reflection, transmission, shots):
    own_refl = reflection[0]
    own_trans = transmission[0]
    shot_tile = shots[0]
    row = lax.axis_index("row")
    x, y, z = row // 2, row % 2, lax.axis_index("col")
    place = jnp.arange(8, dtype=jnp.int32)
    block = (x + place // 2) % 4 * 2 + (y ^ place % 2)
    by_step = (block - z) % 8
    step_block = (place + z) % 8
    step_place = (step_block // 2 - x) % 4 * 2 + (step_block % 2 ^ y)
    t_down, t_up, r_down, r_up = {}, {}, {}, {}
    t_here = core_send(own_trans)
    t_down[1], t_up[1] = z_send(own_trans, -1, 1), z_send(own_trans, 1, 1)
    shot_ring = pair_steps(shot_tile, 1, False)
    gate = (*next(shot_ring), t_here)
    t_down[2] = z_send(after(t_down[1], *gate), -1)
    t_up[2] = z_send(after(t_up[1], *gate), 1)
    gate = next(shot_ring)
    t_down[3] = z_send(after(t_down[2], *gate), -1)
    t_up[3] = z_send(after(t_up[2], *gate), 1)
    gate = next(shot_ring)
    t_down[4] = z_send(after(t_down[3], *gate), -1)
    r_up[1] = z_send(after(own_refl, t_up[3], *gate), 1)
    incoming = after(next(shot_ring), r_up[1])
    tiles = [t_here, *(t_down[step] for step in (1, 2, 3, 4)), t_up[3], t_up[2], t_up[1]]
    first, trans = multiply_tiles(tiles, incoming, step_place)
    r_down[1] = z_send(after(own_refl, t_down[4]), -1)
    r_up[2] = z_send(r_up[1], 1)
    first_ring = pair_steps(first, 0, False)
    gate = next(first_ring)
    r_down[2] = z_send(after(r_down[1], *gate), -1)
    r_up[3] = z_send(after(r_up[2], *gate), 1)
    gate = first_ring.send((r_down[1], r_up[2]))
    r_down[3] = z_send(after(r_down[2], *gate), -1)
    r_up[4] = z_send(after(r_up[3], *gate), 1)
    first_ring.send((r_down[2], r_up[3]))
    passed = next(first_ring)
    tiles = [own_refl, *(r_down[step] for step in (1, 2, 3)), *(r_up[step] for step in (4, 3, 2, 1))]
    middle, pair, refl = multiply_tiles(tiles, passed, step_place, first)
    summed = multiply(refl, gather_row(middle, core_send(pair), 1), by_step)
    return multiply(trans, gather_row(summed, summed, 0), by_step)[None]


def solution(mesh):
    placed = (P("slab", "row", "col"), P("slab", "row", "col"), P("slab", "row", "col"))
    return jax.shard_map(
        on_device, mesh=mesh, in_specs=placed, out_specs=P("slab", "row", "col"), check_vma=False
    )
```

time: 176 us -> 168 us (0.955)
  starting transfers between devices: 58.9 us -> 51 us
  waiting for transfers between devices: 99.1 us -> 101 us
    ppermute x29 -> x27, waiting for transfers between devices: 70.6 us -> 80.6 us  [send(): return lax.ppermute(block, ('slab', 'row'), route)]
    ppermute x16 -> x14, waiting for transfers between devices: 28.5 us -> 20.6 us  [z_send(): return lax.ppermute(block, ('slab', 'col'), route)]
    ppermute x16 -> x14, starting transfers between devices: 28.9 us -> 23.7 us  [z_send(): return lax.ppermute(block, ('slab', 'col'), route)]
    ppermute x29 -> x27, starting transfers between devices: 29.9 us -> 27.3 us  [send(): return lax.ppermute(block, ('slab', 'row'), route)]
    unnamed x15 -> x12, local copies, waits for them, and re-layouts: 4.02 us -> 3.16 us
  transfers between devices with their start and end apart: 45 -> 41, of which waited for: 25 -> 28; matrix products, arithmetic and copies ran while one was open for 3% -> 2% of each run, Pallas kernels for 2% -> 2%
where the time goes in v1:
time: 168 us; the launch traced here: 167 us
  waiting for transfers between devices  101 us (60%)
  starting transfers between devices  51 us (30%)
  Pallas kernels  11.3 us (7%)
  local copies, waits for them, and re-layouts  3.23 us (2%)
    ppermute x27, waiting for transfers between devices, send(): return lax.ppermute(block, ('slab', 'row'), route)  80.6 us
    ppermute x27, starting transfers between devices, send(): return lax.ppermute(block, ('slab', 'row'), route)  27.3 us
    ppermute x14, starting transfers between devices, z_send(): return lax.ppermute(block, ('slab', 'col'), route)  23.7 us
    ppermute x14, waiting for transfers between devices, z_send(): return lax.ppermute(block, ('slab', 'col'), route)  20.6 us
    pallas_call x2, Pallas kernels, multiply_tiles(): pl.pallas_call(functools.partial(fold_tiles, beside is not None), in_spec...  5.92 us
    pallas_call x2, Pallas kernels, multiply(): pl.pallas_call(functools.partial(fold, [piece[:2] for piece in pieces]),...  5.35 us
  transfers between devices with their start and end apart: 41, of which 28 were waited for; matrix products, arithmetic and copies ran while one was open for 2% of the time, Pallas kernels for 2%

profile of v1, /device:TPU:16, one launch (start us, length us, event | category | flops | bytes accessed | tf_op | source)
XLA Modules:
  0.0 167.3 jit_solution(4869487940513783825)
XLA Ops:
  0.0 5.3 %collective-permute-start.10 = (bf16[512,512]{1,0:T(8,128)(2,1)}, bf16[512,512]{1,0:T(8,128)(2,1)S(1)}, u32[]{:S(2)}, u32[]{:S(2)}) collective-permute-start(bf16[512,512]{1,0:T(8,128)(2,1)} %bitcast.17), channel_id=1, source_target_pairs={{0,71},{1,64},{2,65},{3,66},{4,67},{5,68},{6,69},{7,70},{64,7},{65... | collective-permute-start | bytes 1572872 | tf_op jit(solution)/shard_map/ppermute | solution.py:27
  7.4 7.2 %collective-permute-done.1 = bf16[512,256]{1,0:T(8,128)(2,1)S(1)} collective-permute-done((bf16[512,256]{1,0:T(8,128)(2,1)}, bf16[512,256]{1,0:T(8,128)(2,1)S(1)}, u32[]{:S(2)}, u32[]{:S(2)}) %collective-permute-start.1) | collective-permute-done | bytes 262176 | tf_op jit(solution)/shard_map/ppermute | solution.py:37
  14.7 1.6 collective-permute-start.4
  16.2 1.7 %collective-permute-start.2 = (bf16[2,512,256]{2,1,0:T(8,128)(2,1)S(1)}, bf16[2,512,256]{2,1,0:T(8,128)(2,1)}, u32[]{:S(2)}, u32[]{:S(2)}) collective-permute-start(bf16[2,512,256]{2,1,0:T(8,128)(2,1)S(1)} %pad_maximum_fusion.1), channel_id=1, source_target_pairs={{0,48},{8,56},{16,0},{24,8},{32,16},{40,24},{48,32},{56,40},{64,11... | collective-permute-start | bytes 1572872 | tf_op jit(solution)/shard_map/ppermute | solution.py:37
  18.0 3.5 %collective-permute-start.11 = (bf16[512,512]{1,0:T(8,128)(2,1)S(1)}, bf16[512,512]{1,0:T(8,128)(2,1)S(1)}, u32[]{:S(2)}, u32[]{:S(2)}) collective-permute-start(bf16[512,512]{1,0:T(8,128)(2,1)S(1)} %collective-permute-done.10.refs_1_), channel_id=1, source_target_pairs={{0,7},{1,0},{2,1},{3,2},{4,3},{5,4},{6,5},{7,6},{64,71},{65,64},{6... | collective-permute-start | bytes 1572872 | tf_op jit(solution)/shard_map/ppermute | solution.py:27
  21.5 8.7 %collective-permute-done.2 = bf16[2,512,256]{2,1,0:T(8,128)(2,1)} collective-permute-done((bf16[2,512,256]{2,1,0:T(8,128)(2,1)S(1)}, bf16[2,512,256]{2,1,0:T(8,128)(2,1)}, u32[]{:S(2)}, u32[]{:S(2)}) %collective-permute-start.2) | collective-permute-done | bytes 524320 | tf_op jit(solution)/shard_map/ppermute | solution.py:37
  30.2 3.0 %collective-permute-start.3 = (bf16[2,512,256]{2,1,0:T(8,128)(2,1)}, bf16[2,512,256]{2,1,0:T(8,128)(2,1)}, u32[]{:S(2)}, u32[]{:S(2)}) collective-permute-start(bf16[2,512,256]{2,1,0:T(8,128)(2,1)} %collective-permute-done.2), channel_id=1, source_target_pairs={{0,48},{8,56},{16,0},{24,8},{32,16},{40,24},{48,32},{56,40},{64,11... | collective-permute-start | bytes 1572872 | tf_op jit(solution)/shard_map/ppermute | solution.py:37
  33.2 3.5 %collective-permute-start.12 = (bf16[512,512]{1,0:T(8,128)(2,1)S(1)}, bf16[512,512]{1,0:T(8,128)(2,1)S(1)}, u32[]{:S(2)}, u32[]{:S(2)}) collective-permute-start(bf16[512,512]{1,0:T(8,128)(2,1)S(1)} %collective-permute-done.11.refs_2_), channel_id=1, source_target_pairs={{0,7},{1,0},{2,1},{3,2},{4,3},{5,4},{6,5},{7,6},{64,71},{65,64},{6... | collective-permute-start | bytes 1572872 | tf_op jit(solution)/shard_map/ppermute | solution.py:27
  36.9 7.1 %collective-permute-done.3 = bf16[2,512,256]{2,1,0:T(8,128)(2,1)} collective-permute-done((bf16[2,512,256]{2,1,0:T(8,128)(2,1)}, bf16[2,512,256]{2,1,0:T(8,128)(2,1)}, u32[]{:S(2)}, u32[]{:S(2)}) %collective-permute-start.3) | collective-permute-done | bytes 524320 | tf_op jit(solution)/shard_map/ppermute | solution.py:37
  44.0 3.3 %collective-permute-done.12.refs_3_ = bf16[512,512]{1,0:T(8,128)(2,1)S(1)} collective-permute-done((bf16[512,512]{1,0:T(8,128)(2,1)S(1)}, bf16[512,512]{1,0:T(8,128)(2,1)S(1)}, u32[]{:S(2)}, u32[]{:S(2)}) %collective-permute-start.12) | collective-permute-done | bytes 524320 | tf_op jit(solution)/shard_map/ppermute | solution.py:27
  47.3 3.7 %collective-permute-start.13 = (bf16[512,512]{1,0:T(8,128)(2,1)S(1)}, bf16[512,512]{1,0:T(8,128)(2,1)S(1)}, u32[]{:S(2)}, u32[]{:S(2)}) collective-permute-start(bf16[512,512]{1,0:T(8,128)(2,1)S(1)} %collective-permute-done.12.refs_3_), channel_id=1, source_target_pairs={{0,7},{1,0},{2,1},{3,2},{4,3},{5,4},{6,5},{7,6},{64,71},{65,64},{6... | collective-permute-start | bytes 1572872 | tf_op jit(solution)/shard_map/ppermute | solution.py:27
  52.3 1.1 constant_dynamic-update-slice_fusion.2
  53.4 1.1 constant_dynamic-update-slice_fusion.1
  54.5 6.2 %collective-permute-done.13.refs_4_ = bf16[512,512]{1,0:T(8,128)(2,1)S(1)} collective-permute-done((bf16[512,512]{1,0:T(8,128)(2,1)S(1)}, bf16[512,512]{1,0:T(8,128)(2,1)S(1)}, u32[]{:S(2)}, u32[]{:S(2)}) %collective-permute-start.13) | collective-permute-done | bytes 524320 | tf_op jit(solution)/shard_map/ppermute | solution.py:27
  60.7 3.7 %collective-permute-start.15 = (bf16[512,512]{1,0:T(8,128)(2,1)S(1)}, bf16[512,512]{1,0:T(8,128)(2,1)S(1)}, u32[]{:S(2)}, u32[]{:S(2)}) collective-permute-start(bf16[512,512]{1,0:T(8,128)(2,1)S(1)} %bitcast.12), channel_id=1, source_target_pairs={{0,7},{1,0},{2,1},{3,2},{4,3},{5,4},{6,5},{7,6},{64,71},{65,64},{6... | collective-permute-start | bytes 1572872 | tf_op jit(solution)/shard_map/ppermute | solution.py:27
  65.1 3.2 %shard_map.37 = (bf16[512,256]{1,0:T(8,128)(2,1)S(1)}, bf16[8,512,512]{2,1,0:T(8,128)(2,1)S(1)}) custom-call(s32[8]{0:T(128)S(1)} %fusion.6.order, bf16[8,512,256]{2,1,0:T(8,128)(2,1)S(1)} %constant_dynamic-update-slice_fusion.shots, bf16[512,512]{1,0:T(8,128)(2,1)S(1)} %collective-permute-done.6.refs_0_, ...), custom_call_target="tpu_custom_call" | custom-call | flops 1073741824 | bytes 6291456 | tf_op jit(solution)/shard_map/pallas_call | solution.py:117
  68.4 1.4 collective-permute-start.14
  69.7 5.1 %collective-permute-done.14 = bf16[512,256]{1,0:T(8,128)(2,1)S(1)} collective-permute-done((bf16[512,256]{1,0:T(8,128)(2,1)S(1)}, bf16[512,256]{1,0:T(8,128)(2,1)S(1)}, u32[]{:S(2)}, u32[]{:S(2)}) %collective-permute-start.14) | collective-permute-done | bytes 262176 | tf_op jit(solution)/shard_map/ppermute | solution.py:37
  74.9 2.8 %collective-permute-done.16.refs_6_ = bf16[512,512]{1,0:T(8,128)(2,1)S(1)} collective-permute-done((bf16[512,512]{1,0:T(8,128)(2,1)S(1)}, bf16[512,512]{1,0:T(8,128)(2,1)S(1)}, u32[]{:S(2)}, u32[]{:S(2)}) %collective-permute-start.16) | collective-permute-done | bytes 524320 | tf_op jit(solution)/shard_map/ppermute | solution.py:27
  77.7 3.6 %collective-permute-start.17 = (bf16[2,512,256]{2,1,0:T(8,128)(2,1)S(1)}, bf16[2,512,256]{2,1,0:T(8,128)(2,1)S(1)}, u32[]{:S(2)}, u32[]{:S(2)}) collective-permute-start(bf16[2,512,256]{2,1,0:T(8,128)(2,1)S(1)} %pad_maximum_fusion.2), channel_id=1, source_target_pairs={{0,48},{8,56},{16,0},{24,8},{32,16},{40,24},{48,32},{56,40},{64,11... | collective-permute-start | bytes 1572872 | tf_op jit(solution)/shard_map/ppermute | solution.py:37
  81.6 1.8 %collective-permute-start.19 = (bf16[512,512]{1,0:T(8,128)(2,1)S(1)}, bf16[512,512]{1,0:T(8,128)(2,1)S(1)}, u32[]{:S(2)}, u32[]{:S(2)}) collective-permute-start(bf16[512,512]{1,0:T(8,128)(2,1)S(1)} %collective-permute-done.16.refs_6_), channel_id=1, source_target_pairs={{0,1},{1,2},{2,3},{3,4},{4,5},{5,6},{6,7},{7,0},{64,65},{65,66},{6... | collective-permute-start | bytes 1572872 | tf_op jit(solution)/shard_map/ppermute | solution.py:27
  83.3 6.4 %collective-permute-done.17 = bf16[2,512,256]{2,1,0:T(8,128)(2,1)S(1)} collective-permute-done((bf16[2,512,256]{2,1,0:T(8,128)(2,1)S(1)}, bf16[2,512,256]{2,1,0:T(8,128)(2,1)S(1)}, u32[]{:S(2)}, u32[]{:S(2)}) %collective-permute-start.17) | collective-permute-done | bytes 524320 | tf_op jit(solution)/shard_map/ppermute | solution.py:37
  89.7 2.1 %collective-permute-done.18.refs_2_ = bf16[512,512]{1,0:T(8,128)(2,1)S(1)} collective-permute-done((bf16[512,512]{1,0:T(8,128)(2,1)S(1)}, bf16[512,512]{1,0:T(8,128)(2,1)S(1)}, u32[]{:S(2)}, u32[]{:S(2)}) %collective-permute-start.18) | collective-permute-done | bytes 524320 | tf_op jit(solution)/shard_map/ppermute | solution.py:27
  91.8 1.2 collective-permute-done.19.refs_5_
  93.4 1.0 collective-permute-done.21
  94.4 1.5 collective-permute-start.22
  96.5 5.8 %collective-permute-done.20 = bf16[2,512,256]{2,1,0:T(8,128)(2,1)S(1)} collective-permute-done((bf16[2,512,256]{2,1,0:T(8,128)(2,1)S(1)}, bf16[2,512,256]{2,1,0:T(8,128)(2,1)S(1)}, u32[]{:S(2)}, u32[]{:S(2)}) %collective-permute-start.20) | collective-permute-done | bytes 524320 | tf_op jit(solution)/shard_map/ppermute | solution.py:37
  102.5 1.1 collective-permute-done.22.refs_3_
  103.6 2.7 %collective-permute-done.23.refs_4_ = bf16[512,512]{1,0:T(8,128)(2,1)S(1)} collective-permute-done((bf16[512,512]{1,0:T(8,128)(2,1)S(1)}, bf16[512,512]{1,0:T(8,128)(2,1)S(1)}, u32[]{:S(2)}, u32[]{:S(2)}) %collective-permute-start.23) | collective-permute-done | bytes 524320 | tf_op jit(solution)/shard_map/ppermute | solution.py:27
  106.3 2.7 %shard_map.38 = (bf16[512,256]{1,0:T(8,128)(2,1)S(1)}, bf16[2,512,256]{2,1,0:T(8,128)(2,1)S(1)}, bf16[8,512,512]{2,1,0:T(8,128)(2,1)S(1)}) custom-call(s32[8]{0:T(128)S(1)} %fusion.6.order, bf16[8,512,256]{2,1,0:T(8,128)(2,1)S(1)} %pad_maximum_fusion.shots, bf16[512,512]{1,0:T(8,128)(2,1)S(1)} %bitcast.13, ...), custom_call_target="tpu_custom_call" | custom-call | flops 1073741824 | bytes 6291456 | tf_op jit(solution)/shard_map/pallas_call | solution.py:117
  110.6 5.0 %collective-permute-done.26.refs_2_ = bf16[512,256]{1,0:T(8,128)(2,1)S(1)} collective-permute-done((bf16[512,256]{1,0:T(8,128)(2,1)S(1)}, bf16[512,256]{1,0:T(8,128)(2,1)S(1)}, u32[]{:S(2)}, u32[]{:S(2)}) %collective-permute-start.26) | collective-permute-done | bytes 262176 | tf_op jit(solution)/shard_map/ppermute | solution.py:37
  115.6 1.8 %collective-permute-start.29 = (bf16[512,256]{1,0:T(8,128)(2,1)S(1)}, bf16[512,256]{1,0:T(8,128)(2,1)S(1)}, u32[]{:S(2)}, u32[]{:S(2)}) collective-permute-start(bf16[512,256]{1,0:T(8,128)(2,1)S(1)} %collective-permute-done.26.refs_2_), channel_id=1, source_target_pairs={{0,48},{8,56},{16,0},{24,8},{32,16},{40,24},{48,32},{56,40},{64,11... | collective-permute-start | bytes 786440 | tf_op jit(solution)/shard_map/ppermute | solution.py:37
  119.5 4.5 %collective-permute-done.29.refs_5_ = bf16[512,256]{1,0:T(8,128)(2,1)S(1)} collective-permute-done((bf16[512,256]{1,0:T(8,128)(2,1)S(1)}, bf16[512,256]{1,0:T(8,128)(2,1)S(1)}, u32[]{:S(2)}, u32[]{:S(2)}) %collective-permute-start.29) | collective-permute-done | bytes 262176 | tf_op jit(solution)/shard_map/ppermute | solution.py:37
  124.0 1.6 collective-permute-start.32
  125.6 2.4 %collective-permute-done.28.refs_4_ = bf16[512,256]{1,0:T(8,128)(2,1)S(1)} collective-permute-done((bf16[512,256]{1,0:T(8,128)(2,1)S(1)}, bf16[512,256]{1,0:T(8,128)(2,1)S(1)}, u32[]{:S(2)}, u32[]{:S(2)}) %collective-permute-start.28) | collective-permute-done | bytes 262176 | tf_op jit(solution)/shard_map/ppermute | solution.py:37
  128.1 4.4 %collective-permute-done.27.refs_3_ = bf16[512,256]{1,0:T(8,128)(2,1)S(1)} collective-permute-done((bf16[512,256]{1,0:T(8,128)(2,1)S(1)}, bf16[512,256]{1,0:T(8,128)(2,1)S(1)}, u32[]{:S(2)}, u32[]{:S(2)}) %collective-permute-start.27) | collective-permute-done | bytes 262176 | tf_op jit(solution)/shard_map/ppermute | solution.py:37
  132.5 3.4 %collective-permute-done.31.refs_7_ = bf16[256,256]{1,0:T(8,128)(2,1)S(1)} collective-permute-done((bf16[256,256]{1,0:T(8,128)(2,1)S(1)}, bf16[256,256]{1,0:T(8,128)(2,1)S(1)}, u32[]{:S(2)}, u32[]{:S(2)}) %collective-permute-start.31) | collective-permute-done | bytes 131104 | tf_op jit(solution)/shard_map/ppermute | solution.py:37
  135.9 2.3 %shard_map.39.refs_0_ = bf16[512,256]{1,0:T(8,128)(2,1)S(1)} custom-call(s32[8]{0:T(128)S(1)} %and_select_fusion.4.order, bf16[8,512,512]{2,1,0:T(8,128)(2,1)S(1)} %get-tuple-element.40.operator, bf16[2,512,256]{2,1,0:T(8,128)(2,1)S(1)} %collective-permute-done.24.refs_0_, bf16[512,256]{1,0:T(8,128)(2,1)S(1)} %collective-permute-done.25.refs_1_, ...), custom_call_target="tpu_custom_call" | custom-call | flops 1073741824 | bytes 6291456 | tf_op jit(solution)/shard_map/pallas_call | solution.py:158
  138.3 1.4 collective-permute-start.33
  139.7 6.4 %collective-permute-done.34.refs_2_ = bf16[512,256]{1,0:T(8,128)(2,1)S(1)} collective-permute-done((bf16[512,256]{1,0:T(8,128)(2,1)S(1)}, bf16[512,256]{1,0:T(8,128)(2,1)S(1)}, u32[]{:S(2)}, u32[]{:S(2)}) %collective-permute-start.34) | collective-permute-done | bytes 262176 | tf_op jit(solution)/shard_map/ppermute | solution.py:37
  146.0 1.5 collective-permute-start.37
  148.2 1.4 collective-permute-start.38
  149.5 3.4 %collective-permute-done.37.refs_5_ = bf16[512,256]{1,0:T(8,128)(2,1)S(1)} collective-permute-done((bf16[512,256]{1,0:T(8,128)(2,1)S(1)}, bf16[512,256]{1,0:T(8,128)(2,1)S(1)}, u32[]{:S(2)}, u32[]{:S(2)}) %collective-permute-start.37) | collective-permute-done | bytes 262176 | tf_op jit(solution)/shard_map/ppermute | solution.py:37
  152.9 1.6 collective-permute-start.40
  154.5 3.5 %collective-permute-done.36.refs_4_ = bf16[512,256]{1,0:T(8,128)(2,1)S(1)} collective-permute-done((bf16[512,256]{1,0:T(8,128)(2,1)S(1)}, bf16[512,256]{1,0:T(8,128)(2,1)S(1)}, u32[]{:S(2)}, u32[]{:S(2)}) %collective-permute-start.36) | collective-permute-done | bytes 262176 | tf_op jit(solution)/shard_map/ppermute | solution.py:37
  158.1 4.6 %collective-permute-done.35.refs_3_ = bf16[512,256]{1,0:T(8,128)(2,1)S(1)} collective-permute-done((bf16[512,256]{1,0:T(8,128)(2,1)S(1)}, bf16[512,256]{1,0:T(8,128)(2,1)S(1)}, u32[]{:S(2)}, u32[]{:S(2)}) %collective-permute-start.35) | collective-permute-done | bytes 262176 | tf_op jit(solution)/shard_map/ppermute | solution.py:37
  162.7 1.6 collective-permute-done.39.refs_7_
  164.3 3.0 %shard_map.40 = bf16[512,256]{1,0:T(8,128)(2,1)} custom-call(s32[8]{0:T(128)S(1)} %and_select_fusion.4.order, bf16[8,512,512]{2,1,0:T(8,128)(2,1)S(1)} %get-tuple-element.31.operator, bf16[512,256]{1,0:T(8,128)(2,1)S(1)} %shard_map.39.refs_0_, bf16[512,256]{1,0:T(8,128)(2,1)S(1)} %collective-permute-done.33.refs_1_, ...), custom_call_target="tpu_custom_call" | custom-call | flops 1073741824 | bytes 6291456 | tf_op jit(solution)/shard_map/pallas_call | solution.py:158
  (60 shorter events, 10.5 us)
Async XLA Ops:
  0.0 18.0 %collective-permute-start.10 = (bf16[512,512]{1,0:T(8,128)(2,1)}, bf16[512,512]{1,0:T(8,128)(2,1)S(1)}, u32[]{:S(2)}, u32[]{:S(2)}) collective-permute-start(bf16[512,512]{1,0:T(8,128)(2,1)} %bitcast.17), channel_id=1, source_target_pairs={{0,71},{1,64},{2,65},{3,66},{4,67},{5,68},{6,69},{7,70},{64,7},{65... | collective-permute-start | bytes 1572872 | tf_op jit(solution)/shard_map/ppermute | solution.py:27
  5.3 12.7 %collective-permute-start.6 = (bf16[512,512]{1,0:T(8,128)(2,1)}, bf16[512,512]{1,0:T(8,128)(2,1)S(1)}, u32[]{:S(2)}, u32[]{:S(2)}) collective-permute-start(bf16[512,512]{1,0:T(8,128)(2,1)} %bitcast.18), channel_id=1, source_target_pairs={{0,64},{8,72},{16,80},{24,88},{32,96},{40,104},{48,112},{56,120},{... | collective-permute-start | bytes 1572872 | tf_op jit(solution)/shard_map/ppermute | solution.py:37
  6.0 15.5 %collective-permute-start.5 = (bf16[512,512]{1,0:T(8,128)(2,1)}, bf16[512,512]{1,0:T(8,128)(2,1)S(1)}, u32[]{:S(2)}, u32[]{:S(2)}) collective-permute-start(bf16[512,512]{1,0:T(8,128)(2,1)} %bitcast.19), channel_id=1, source_target_pairs={{0,65},{1,66},{2,67},{3,68},{4,69},{5,70},{6,71},{7,64},{64,1},{65... | collective-permute-start | bytes 1572872 | tf_op jit(solution)/shard_map/ppermute | solution.py:27
  6.0 8.6 %collective-permute-start.1 = (bf16[512,256]{1,0:T(8,128)(2,1)}, bf16[512,256]{1,0:T(8,128)(2,1)S(1)}, u32[]{:S(2)}, u32[]{:S(2)}) collective-permute-start(bf16[512,256]{1,0:T(8,128)(2,1)} %bitcast.20), channel_id=1, source_target_pairs={{0,72},{8,64},{16,88},{24,80},{32,104},{40,96},{48,120},{56,112},{... | collective-permute-start | bytes 786440 | tf_op jit(solution)/shard_map/ppermute | solution.py:37
  6.9 7.7 %collective-permute-start = (bf16[512,256]{1,0:T(8,128)(2,1)}, bf16[512,256]{1,0:T(8,128)(2,1)S(1)}, u32[]{:S(2)}, u32[]{:S(2)}) collective-permute-start(bf16[512,256]{1,0:T(8,128)(2,1)} %bitcast.21), channel_id=1, source_target_pairs={{0,64},{8,72},{16,80},{24,88},{32,96},{40,104},{48,112},{56,120},{... | collective-permute-start | bytes 786440 | tf_op jit(solution)/shard_map/ppermute | solution.py:37
  14.6 22.2 %copy-start.1 = (bf16[512,256]{1,0:T(8,128)(2,1)}, bf16[512,256]{1,0:T(8,128)(2,1)S(1)}, u32[]{:S(2)}) copy-start(bf16[512,256]{1,0:T(8,128)(2,1)S(1)} %collective-permute-done) | copy-start | bytes 786436
  14.7 18.5 %collective-permute-start.4 = (bf16[2,512,256]{2,1,0:T(8,128)(2,1)S(1)}, bf16[2,512,256]{2,1,0:T(8,128)(2,1)S(1)}, u32[]{:S(2)}, u32[]{:S(2)}) collective-permute-start(bf16[2,512,256]{2,1,0:T(8,128)(2,1)S(1)} %pad_maximum_fusion.1), channel_id=1, source_target_pairs={{0,16},{8,24},{16,32},{24,40},{32,48},{40,56},{48,0},{56,8},{64,80... | collective-permute-start | bytes 1572872 | tf_op jit(solution)/shard_map/ppermute | solution.py:37
  16.2 14.0 %collective-permute-start.2 = (bf16[2,512,256]{2,1,0:T(8,128)(2,1)S(1)}, bf16[2,512,256]{2,1,0:T(8,128)(2,1)}, u32[]{:S(2)}, u32[]{:S(2)}) collective-permute-start(bf16[2,512,256]{2,1,0:T(8,128)(2,1)S(1)} %pad_maximum_fusion.1), channel_id=1, source_target_pairs={{0,48},{8,56},{16,0},{24,8},{32,16},{40,24},{48,32},{56,40},{64,11... | collective-permute-start | bytes 1572872 | tf_op jit(solution)/shard_map/ppermute | solution.py:37
  18.0 15.2 %collective-permute-start.11 = (bf16[512,512]{1,0:T(8,128)(2,1)S(1)}, bf16[512,512]{1,0:T(8,128)(2,1)S(1)}, u32[]{:S(2)}, u32[]{:S(2)}) collective-permute-start(bf16[512,512]{1,0:T(8,128)(2,1)S(1)} %collective-permute-done.10.refs_1_), channel_id=1, source_target_pairs={{0,7},{1,0},{2,1},{3,2},{4,3},{5,4},{6,5},{7,6},{64,71},{65,64},{6... | collective-permute-start | bytes 1572872 | tf_op jit(solution)/shard_map/ppermute | solution.py:27
  21.5 15.3 %collective-permute-start.7 = (bf16[512,512]{1,0:T(8,128)(2,1)S(1)}, bf16[512,512]{1,0:T(8,128)(2,1)S(1)}, u32[]{:S(2)}, u32[]{:S(2)}) collective-permute-start(bf16[512,512]{1,0:T(8,128)(2,1)S(1)} %collective-permute-done.5.refs_7_), channel_id=1, source_target_pairs={{0,1},{1,2},{2,3},{3,4},{4,5},{5,6},{6,7},{7,0},{64,65},{65,66},{6... | collective-permute-start | bytes 1572872 | tf_op jit(solution)/shard_map/ppermute | solution.py:27
  30.2 13.8 %collective-permute-start.3 = (bf16[2,512,256]{2,1,0:T(8,128)(2,1)}, bf16[2,512,256]{2,1,0:T(8,128)(2,1)}, u32[]{:S(2)}, u32[]{:S(2)}) collective-permute-start(bf16[2,512,256]{2,1,0:T(8,128)(2,1)} %collective-permute-done.2), channel_id=1, source_target_pairs={{0,48},{8,56},{16,0},{24,8},{32,16},{40,24},{48,32},{56,40},{64,11... | collective-permute-start | bytes 1572872 | tf_op jit(solution)/shard_map/ppermute | solution.py:37
  33.2 3.6 %copy-start.2 = (bf16[2,512,256]{2,1,0:T(8,128)(2,1)}, bf16[2,512,256]{2,1,0:T(8,128)(2,1)S(1)}, u32[]{:S(2)}) copy-start(bf16[2,512,256]{2,1,0:T(8,128)(2,1)S(1)} %collective-permute-done.4) | copy-start | bytes 1572868
  33.2 14.1 %collective-permute-start.12 = (bf16[512,512]{1,0:T(8,128)(2,1)S(1)}, bf16[512,512]{1,0:T(8,128)(2,1)S(1)}, u32[]{:S(2)}, u32[]{:S(2)}) collective-permute-start(bf16[512,512]{1,0:T(8,128)(2,1)S(1)} %collective-permute-done.11.refs_2_), channel_id=1, source_target_pairs={{0,7},{1,0},{2,1},{3,2},{4,3},{5,4},{6,5},{7,6},{64,71},{65,64},{6... | collective-permute-start | bytes 1572872 | tf_op jit(solution)/shard_map/ppermute | solution.py:27
  36.8 14.6 %collective-permute-start.8 = (bf16[512,512]{1,0:T(8,128)(2,1)S(1)}, bf16[512,512]{1,0:T(8,128)(2,1)}, u32[]{:S(2)}, u32[]{:S(2)}) collective-permute-start(bf16[512,512]{1,0:T(8,128)(2,1)S(1)} %collective-permute-done.7.refs_6_), channel_id=1, source_target_pairs={{0,1},{1,2},{2,3},{3,4},{4,5},{5,6},{6,7},{7,0},{64,65},{65,66},{6... | collective-permute-start | bytes 1572872 | tf_op jit(solution)/shard_map/ppermute | solution.py:27
  36.8 23.9 %copy-start = (bf16[1,512,512]{2,1,0:T(8,128)(2,1)S(1)}, bf16[1,512,512]{2,1,0:T(8,128)(2,1)}, u32[]{:S(2)}) copy-start(bf16[1,512,512]{2,1,0:T(8,128)(2,1)} %param.3) | copy-start | bytes 1572868
  36.8 28.3 %copy-start.3 = (bf16[2,512,256]{2,1,0:T(8,128)(2,1)S(1)}, bf16[2,512,256]{2,1,0:T(8,128)(2,1)}, u32[]{:S(2)}) copy-start(bf16[2,512,256]{2,1,0:T(8,128)(2,1)} %copy-done.2) | copy-start | bytes 1572868
  47.3 13.4 %collective-permute-start.13 = (bf16[512,512]{1,0:T(8,128)(2,1)S(1)}, bf16[512,512]{1,0:T(8,128)(2,1)S(1)}, u32[]{:S(2)}, u32[]{:S(2)}) collective-permute-start(bf16[512,512]{1,0:T(8,128)(2,1)S(1)} %collective-permute-done.12.refs_3_), channel_id=1, source_target_pairs={{0,7},{1,0},{2,1},{3,2},{4,3},{5,4},{6,5},{7,6},{64,71},{65,64},{6... | collective-permute-start | bytes 1572872 | tf_op jit(solution)/shard_map/ppermute | solution.py:27
  51.3 13.7 %collective-permute-start.9 = (bf16[512,512]{1,0:T(8,128)(2,1)}, bf16[512,512]{1,0:T(8,128)(2,1)S(1)}, u32[]{:S(2)}, u32[]{:S(2)}) collective-permute-start(bf16[512,512]{1,0:T(8,128)(2,1)} %bitcast.11), channel_id=1, source_target_pairs={{0,1},{1,2},{2,3},{3,4},{4,5},{5,6},{6,7},{7,0},{64,65},{65,66},{6... | collective-permute-start | bytes 1572872 | tf_op jit(solution)/shard_map/ppermute | solution.py:27
  60.7 17.0 %collective-permute-start.15 = (bf16[512,512]{1,0:T(8,128)(2,1)S(1)}, bf16[512,512]{1,0:T(8,128)(2,1)S(1)}, u32[]{:S(2)}, u32[]{:S(2)}) collective-permute-start(bf16[512,512]{1,0:T(8,128)(2,1)S(1)} %bitcast.12), channel_id=1, source_target_pairs={{0,7},{1,0},{2,1},{3,2},{4,3},{5,4},{6,5},{7,6},{64,71},{65,64},{6... | collective-permute-start | bytes 1572872 | tf_op jit(solution)/shard_map/ppermute | solution.py:27
  65.1 12.6 %collective-permute-start.16 = (bf16[512,512]{1,0:T(8,128)(2,1)S(1)}, bf16[512,512]{1,0:T(8,128)(2,1)S(1)}, u32[]{:S(2)}, u32[]{:S(2)}) collective-permute-start(bf16[512,512]{1,0:T(8,128)(2,1)S(1)} %collective-permute-done.9.refs_7_), channel_id=1, source_target_pairs={{0,1},{1,2},{2,3},{3,4},{4,5},{5,6},{6,7},{7,0},{64,65},{65,66},{6... | collective-permute-start | bytes 1572872 | tf_op jit(solution)/shard_map/ppermute | solution.py:27
  68.4 6.5 %collective-permute-start.14 = (bf16[512,256]{1,0:T(8,128)(2,1)S(1)}, bf16[512,256]{1,0:T(8,128)(2,1)S(1)}, u32[]{:S(2)}, u32[]{:S(2)}) collective-permute-start(bf16[512,256]{1,0:T(8,128)(2,1)S(1)} %get-tuple-element.32.refs_8_), channel_id=1, source_target_pairs={{0,8},{8,0},{16,24},{24,16},{32,40},{40,32},{48,56},{56,48},{64,72... | collective-permute-start | bytes 786440 | tf_op jit(solution)/shard_map/ppermute | solution.py:37
  77.7 12.0 %collective-permute-start.17 = (bf16[2,512,256]{2,1,0:T(8,128)(2,1)S(1)}, bf16[2,512,256]{2,1,0:T(8,128)(2,1)S(1)}, u32[]{:S(2)}, u32[]{:S(2)}) collective-permute-start(bf16[2,512,256]{2,1,0:T(8,128)(2,1)S(1)} %pad_maximum_fusion.2), channel_id=1, source_target_pairs={{0,48},{8,56},{16,0},{24,8},{32,16},{40,24},{48,32},{56,40},{64,11... | collective-permute-start | bytes 1572872 | tf_op jit(solution)/shard_map/ppermute | solution.py:37
  81.3 10.5 %collective-permute-start.18 = (bf16[512,512]{1,0:T(8,128)(2,1)S(1)}, bf16[512,512]{1,0:T(8,128)(2,1)S(1)}, u32[]{:S(2)}, u32[]{:S(2)}) collective-permute-start(bf16[512,512]{1,0:T(8,128)(2,1)S(1)} %collective-permute-done.15.refs_1_), channel_id=1, source_target_pairs={{0,7},{1,0},{2,1},{3,2},{4,3},{5,4},{6,5},{7,6},{64,71},{65,64},{6... | collective-permute-start | bytes 1572872 | tf_op jit(solution)/shard_map/ppermute | solution.py:27
  81.6 11.4 %collective-permute-start.19 = (bf16[512,512]{1,0:T(8,128)(2,1)S(1)}, bf16[512,512]{1,0:T(8,128)(2,1)S(1)}, u32[]{:S(2)}, u32[]{:S(2)}) collective-permute-start(bf16[512,512]{1,0:T(8,128)(2,1)S(1)} %collective-permute-done.16.refs_6_), channel_id=1, source_target_pairs={{0,1},{1,2},{2,3},{3,4},{4,5},{5,6},{6,7},{7,0},{64,65},{65,66},{6... | collective-permute-start | bytes 1572872 | tf_op jit(solution)/shard_map/ppermute | solution.py:27
  83.3 11.1 %collective-permute-start.21 = (bf16[2,512,256]{2,1,0:T(8,128)(2,1)S(1)}, bf16[2,512,256]{2,1,0:T(8,128)(2,1)S(1)}, u32[]{:S(2)}, u32[]{:S(2)}) collective-permute-start(bf16[2,512,256]{2,1,0:T(8,128)(2,1)S(1)} %pad_maximum_fusion.2), channel_id=1, source_target_pairs={{0,16},{8,24},{16,32},{24,40},{32,48},{40,56},{48,0},{56,8},{64,80... | collective-permute-start | bytes 1572872 | tf_op jit(solution)/shard_map/ppermute | solution.py:37
  93.0 9.3 %collective-permute-start.20 = (bf16[2,512,256]{2,1,0:T(8,128)(2,1)S(1)}, bf16[2,512,256]{2,1,0:T(8,128)(2,1)S(1)}, u32[]{:S(2)}, u32[]{:S(2)}) collective-permute-start(bf16[2,512,256]{2,1,0:T(8,128)(2,1)S(1)} %collective-permute-done.17), channel_id=1, source_target_pairs={{0,48},{8,56},{16,0},{24,8},{32,16},{40,24},{48,32},{56,40},{64,11... | collective-permute-start | bytes 1572872 | tf_op jit(solution)/shard_map/ppermute | solution.py:37
  94.4 9.2 %collective-permute-start.22 = (bf16[512,512]{1,0:T(8,128)(2,1)S(1)}, bf16[512,512]{1,0:T(8,128)(2,1)S(1)}, u32[]{:S(2)}, u32[]{:S(2)}) collective-permute-start(bf16[512,512]{1,0:T(8,128)(2,1)S(1)} %collective-permute-done.18.refs_2_), channel_id=1, source_target_pairs={{0,7},{1,0},{2,1},{3,2},{4,3},{5,4},{6,5},{7,6},{64,71},{65,64},{6... | collective-permute-start | bytes 1572872 | tf_op jit(solution)/shard_map/ppermute | solution.py:27
  95.9 10.4 %collective-permute-start.23 = (bf16[512,512]{1,0:T(8,128)(2,1)S(1)}, bf16[512,512]{1,0:T(8,128)(2,1)S(1)}, u32[]{:S(2)}, u32[]{:S(2)}) collective-permute-start(bf16[512,512]{1,0:T(8,128)(2,1)S(1)} %collective-permute-done.19.refs_5_), channel_id=1, source_target_pairs={{0,1},{1,2},{2,3},{3,4},{4,5},{5,6},{6,7},{7,0},{64,65},{65,66},{6... | collective-permute-start | bytes 1572872 | tf_op jit(solution)/shard_map/ppermute | solution.py:27
  109.0 6.6 %collective-permute-start.26 = (bf16[512,256]{1,0:T(8,128)(2,1)S(1)}, bf16[512,256]{1,0:T(8,128)(2,1)S(1)}, u32[]{:S(2)}, u32[]{:S(2)}) collective-permute-start(bf16[512,256]{1,0:T(8,128)(2,1)S(1)} %get-tuple-element.42), channel_id=1, source_target_pairs={{0,112},{8,120},{16,64},{24,72},{32,80},{40,88},{48,96},{56,104},{... | collective-permute-start | bytes 786440 | tf_op jit(solution)/shard_map/ppermute | solution.py:37
  109.1 8.5 %collective-permute-start.25 = (bf16[512,256]{1,0:T(8,128)(2,1)S(1)}, bf16[512,256]{1,0:T(8,128)(2,1)S(1)}, u32[]{:S(2)}, u32[]{:S(2)}) collective-permute-start(bf16[512,256]{1,0:T(8,128)(2,1)S(1)} %get-tuple-element.42), channel_id=1, source_target_pairs={{0,72},{8,64},{16,88},{24,80},{32,104},{40,96},{48,120},{56,112},{... | collective-permute-start | bytes 786440 | tf_op jit(solution)/shard_map/ppermute | solution.py:37
  109.7 22.8 %collective-permute-start.24 = (bf16[2,512,256]{2,1,0:T(8,128)(2,1)S(1)}, bf16[2,512,256]{2,1,0:T(8,128)(2,1)S(1)}, u32[]{:S(2)}, u32[]{:S(2)}) collective-permute-start(bf16[2,512,256]{2,1,0:T(8,128)(2,1)S(1)} %get-tuple-element.41), channel_id=1, source_target_pairs={{0,64},{8,72},{16,80},{24,88},{32,96},{40,104},{48,112},{56,120},{... | collective-permute-start | bytes 1572872 | tf_op jit(solution)/shard_map/ppermute | solution.py:37
  115.6 8.4 %collective-permute-start.29 = (bf16[512,256]{1,0:T(8,128)(2,1)S(1)}, bf16[512,256]{1,0:T(8,128)(2,1)S(1)}, u32[]{:S(2)}, u32[]{:S(2)}) collective-permute-start(bf16[512,256]{1,0:T(8,128)(2,1)S(1)} %collective-permute-done.26.refs_2_), channel_id=1, source_target_pairs={{0,48},{8,56},{16,0},{24,8},{32,16},{40,24},{48,32},{56,40},{64,11... | collective-permute-start | bytes 786440 | tf_op jit(solution)/shard_map/ppermute | solution.py:37
  117.7 10.3 %collective-permute-start.28 = (bf16[512,256]{1,0:T(8,128)(2,1)S(1)}, bf16[512,256]{1,0:T(8,128)(2,1)S(1)}, u32[]{:S(2)}, u32[]{:S(2)}) collective-permute-start(bf16[512,256]{1,0:T(8,128)(2,1)S(1)} %collective-permute-done.25.refs_1_), channel_id=1, source_target_pairs={{0,16},{8,24},{16,32},{24,40},{32,48},{40,56},{48,0},{56,8},{64,80... | collective-permute-start | bytes 786440 | tf_op jit(solution)/shard_map/ppermute | solution.py:37
  118.0 14.5 %collective-permute-start.27 = (bf16[512,256]{1,0:T(8,128)(2,1)S(1)}, bf16[512,256]{1,0:T(8,128)(2,1)S(1)}, u32[]{:S(2)}, u32[]{:S(2)}) collective-permute-start(bf16[512,256]{1,0:T(8,128)(2,1)S(1)} %get-tuple-element.42), channel_id=1, source_target_pairs={{0,80},{8,88},{16,96},{24,104},{32,112},{40,120},{48,64},{56,72},{... | collective-permute-start | bytes 786440 | tf_op jit(solution)/shard_map/ppermute | solution.py:37
  118.8 13.7 %collective-permute-start.30 = (bf16[512,256]{1,0:T(8,128)(2,1)S(1)}, bf16[512,256]{1,0:T(8,128)(2,1)S(1)}, u32[]{:S(2)}, u32[]{:S(2)}) collective-permute-start(bf16[512,256]{1,0:T(8,128)(2,1)S(1)} %collective-permute-done.26.refs_2_), channel_id=1, source_target_pairs={{0,8},{8,0},{16,24},{24,16},{32,40},{40,32},{48,56},{56,48},{64,72... | collective-permute-start | bytes 786440 | tf_op jit(solution)/shard_map/ppermute | solution.py:37
  124.0 8.5 %collective-permute-start.32 = (bf16[256,256]{1,0:T(8,128)(2,1)S(1)}, bf16[256,256]{1,0:T(8,128)(2,1)S(1)}, u32[]{:S(2)}, u32[]{:S(2)}) collective-permute-start(bf16[256,256]{1,0:T(8,128)(2,1)S(1)} %slice.17), channel_id=1, source_target_pairs={{0,8},{8,0},{16,24},{24,16},{32,40},{40,32},{48,56},{56,48},{64,72... | collective-permute-start | bytes 393224 | tf_op jit(solution)/shard_map/ppermute | solution.py:37
  128.0 7.8 %collective-permute-start.31 = (bf16[256,256]{1,0:T(8,128)(2,1)S(1)}, bf16[256,256]{1,0:T(8,128)(2,1)S(1)}, u32[]{:S(2)}, u32[]{:S(2)}) collective-permute-start(bf16[256,256]{1,0:T(8,128)(2,1)S(1)} %slice.16), channel_id=1, source_target_pairs={{0,16},{8,24},{16,32},{24,40},{32,48},{40,56},{48,0},{56,8},{64,80... | collective-permute-start | bytes 393224 | tf_op jit(solution)/shard_map/ppermute | solution.py:37
  138.2 7.8 %collective-permute-start.34 = (bf16[512,256]{1,0:T(8,128)(2,1)S(1)}, bf16[512,256]{1,0:T(8,128)(2,1)S(1)}, u32[]{:S(2)}, u32[]{:S(2)}) collective-permute-start(bf16[512,256]{1,0:T(8,128)(2,1)S(1)} %shard_map.39.refs_0_), channel_id=1, source_target_pairs={{0,48},{8,56},{16,0},{24,8},{32,16},{40,24},{48,32},{56,40},{64,11... | collective-permute-start | bytes 786440 | tf_op jit(solution)/shard_map/ppermute | solution.py:37
  138.3 9.2 %collective-permute-start.33 = (bf16[512,256]{1,0:T(8,128)(2,1)S(1)}, bf16[512,256]{1,0:T(8,128)(2,1)S(1)}, u32[]{:S(2)}, u32[]{:S(2)}) collective-permute-start(bf16[512,256]{1,0:T(8,128)(2,1)S(1)} %shard_map.39.refs_0_), channel_id=1, source_target_pairs={{0,8},{8,0},{16,24},{24,16},{32,40},{40,32},{48,56},{56,48},{64,72... | collective-permute-start | bytes 786440 | tf_op jit(solution)/shard_map/ppermute | solution.py:37
  146.0 6.9 %collective-permute-start.37 = (bf16[512,256]{1,0:T(8,128)(2,1)S(1)}, bf16[512,256]{1,0:T(8,128)(2,1)S(1)}, u32[]{:S(2)}, u32[]{:S(2)}) collective-permute-start(bf16[512,256]{1,0:T(8,128)(2,1)S(1)} %collective-permute-done.34.refs_2_), channel_id=1, source_target_pairs={{0,48},{8,56},{16,0},{24,8},{32,16},{40,24},{48,32},{56,40},{64,11... | collective-permute-start | bytes 786440 | tf_op jit(solution)/shard_map/ppermute | solution.py:37
  147.5 10.5 %collective-permute-start.36 = (bf16[512,256]{1,0:T(8,128)(2,1)S(1)}, bf16[512,256]{1,0:T(8,128)(2,1)S(1)}, u32[]{:S(2)}, u32[]{:S(2)}) collective-permute-start(bf16[512,256]{1,0:T(8,128)(2,1)S(1)} %collective-permute-done.33.refs_1_), channel_id=1, source_target_pairs={{0,16},{8,24},{16,32},{24,40},{32,48},{40,56},{48,0},{56,8},{64,80... | collective-permute-start | bytes 786440 | tf_op jit(solution)/shard_map/ppermute | solution.py:37
  148.1 14.6 %collective-permute-start.35 = (bf16[512,256]{1,0:T(8,128)(2,1)S(1)}, bf16[512,256]{1,0:T(8,128)(2,1)S(1)}, u32[]{:S(2)}, u32[]{:S(2)}) collective-permute-start(bf16[512,256]{1,0:T(8,128)(2,1)S(1)} %shard_map.39.refs_0_), channel_id=1, source_target_pairs={{0,16},{8,24},{16,32},{24,40},{32,48},{40,56},{48,0},{56,8},{64,80... | collective-permute-start | bytes 786440 | tf_op jit(solution)/shard_map/ppermute | solution.py:37
  148.2 14.5 %collective-permute-start.38 = (bf16[512,256]{1,0:T(8,128)(2,1)S(1)}, bf16[512,256]{1,0:T(8,128)(2,1)S(1)}, u32[]{:S(2)}, u32[]{:S(2)}) collective-permute-start(bf16[512,256]{1,0:T(8,128)(2,1)S(1)} %collective-permute-done.34.refs_2_), channel_id=1, source_target_pairs={{0,8},{8,0},{16,24},{24,16},{32,40},{40,32},{48,56},{56,48},{64,72... | collective-permute-start | bytes 786440 | tf_op jit(solution)/shard_map/ppermute | solution.py:37
  152.9 9.8 %collective-permute-start.40 = (bf16[256,256]{1,0:T(8,128)(2,1)S(1)}, bf16[256,256]{1,0:T(8,128)(2,1)S(1)}, u32[]{:S(2)}, u32[]{:S(2)}) collective-permute-start(bf16[256,256]{1,0:T(8,128)(2,1)S(1)} %slice.19), channel_id=1, source_target_pairs={{0,8},{8,0},{16,24},{24,16},{32,40},{40,32},{48,56},{56,48},{64,72... | collective-permute-start | bytes 393224 | tf_op jit(solution)/shard_map/ppermute | solution.py:37
  158.0 6.3 %collective-permute-start.39 = (bf16[256,256]{1,0:T(8,128)(2,1)S(1)}, bf16[256,256]{1,0:T(8,128)(2,1)S(1)}, u32[]{:S(2)}, u32[]{:S(2)}) collective-permute-start(bf16[256,256]{1,0:T(8,128)(2,1)S(1)} %slice.18), channel_id=1, source_target_pairs={{0,16},{8,24},{16,32},{24,40},{32,48},{40,56},{48,0},{56,8},{64,80... | collective-permute-start | bytes 393224 | tf_op jit(solution)/shard_map/ppermute | solution.py:37

commit v2 on v1

--- a/solution.py
+++ b/solution.py
@@ -46,9 +46,10 @@
     side = send(tile, 0, 1, other)
     below = send(tile, -1, 0, other)
     above = send(tile, 1, 0, other)
-    above_side = send(side, 1, 0, 0)
-    across = send(below, -1, 0, 0)
-    below_side = send(below, 0, 1, 0)
+    side_on, below_on = wait_all((side, below), (above,))
+    above_side = send(side_on, 1, 0, 0)
+    across = send(below_on, -1, 0, 0)
+    below_side = send(below_on, 0, 1, 0)
     top = send(above_side[:half], 1, 0, 0)
     low = send(across[half:], 0, 1, 0)
     return [
@@ -90,7 +91,7 @@
     for index, tile in enumerate(tiles):
         copies.append(pltpu.make_async_copy(tile, panel.at[index], sems.at[index]))
         copies[-1].start()
-    height = 128
+    height = 256
 
     @pl.loop(0, outs[0].shape[0] // height)
     def _(chunk):
@@ -132,14 +133,14 @@
     return *outs, panel
 
 
-def fold(pieces, order, operator, *refs):
+def fold(pieces, added, order, operator, *refs):
     *shots, out = refs
-    height = 128
+    height = 256
 
     @pl.loop(0, out.shape[0] // height)
     def _(chunk):
         rows = pl.ds(pl.multiple_of(chunk * height, height), height)
-        total = None
+        total = shots[-1][rows, :] if added else None
         for (place, start), shot in zip(pieces, shots):
             block = shot[0] if len(shot.shape) == 3 else shot[...]
             panel = operator[order[place], rows, start : start + block.shape[0]]
@@ -150,23 +151,29 @@
         out[rows, :] = total.astype(out.dtype)
 
 
-def multiply(operator, pieces, order):
-    count, rows, depth = operator.shape
+def multiply_some(operator, pieces, order, dtype, added):
+    _, rows, _ = operator.shape
     shots = [piece[2] for piece in pieces]
     columns = shots[0].shape[-1]
+    depth = sum(shot.shape[-2] for shot in shots)
     in_vmem = pl.BlockSpec(memory_space=pltpu.VMEM)
     return pl.pallas_call(
-        functools.partial(fold, [piece[:2] for piece in pieces]),
-        in_specs=[pl.BlockSpec(memory_space=pltpu.SMEM)] + [in_vmem] * (1 + len(shots)),
+        functools.partial(fold, [piece[:2] for piece in pieces], len(added) > 0),
+        in_specs=[pl.BlockSpec(memory_space=pltpu.SMEM)] + [in_vmem] * (1 + len(shots) + len(added)),
         out_specs=in_vmem,
-        out_shape=jax.ShapeDtypeStruct((rows, columns), BF16),
+        out_shape=jax.ShapeDtypeStruct((rows, columns), dtype),
         compiler_params=pltpu.CompilerParams(vmem_limit_bytes=24 << 20),
         cost_estimate=pl.CostEstimate(
-            flops=2 * count * rows * depth * columns,
-            bytes_accessed=2 * count * depth * (rows + columns),
+            flops=2 * rows * depth * columns,
+            bytes_accessed=2 * depth * (rows + columns),
             transcendentals=0,
         ),
-    )(order, operator, *shots)
+    )(order, operator, *shots, *added)
+
+
+def multiply(operator, pieces, order):
+    early = multiply_some(operator, pieces[:7], order, F32, ())
+    return multiply_some(operator, pieces[7:], order, BF16, (early,))
 
 
 def on_device(reflection, transmission, shots):

time: 168 us -> 161 us (0.958)
  waiting for transfers between devices: 101 us -> 93.2 us
    ppermute x27, waiting for transfers between devices: 80.6 us -> 72.4 us  [send(): return lax.ppermute(block, ('slab', 'row'), route)]
    pallas_call x2 -> x4, Pallas kernels: 5.35 us -> 6.34 us  [multiply_some(): pl.pallas_call(functools.partial(fold, [piece[:2] for piece in pieces], l...]
  transfers between devices with their start and end apart: 41 -> 41, of which waited for: 28 -> 30; matrix products, arithmetic and copies ran while one was open for 2% -> 2% of each run, Pallas kernels for 2% -> 4%
where the time goes in v2:
time: 161 us; the launch traced here: 160 us
  waiting for transfers between devices  93.2 us (58%)
  starting transfers between devices  51.6 us (32%)
  Pallas kernels  11.5 us (7%)
  local copies, waits for them, and re-layouts  3.23 us (2%)
    ppermute x27, waiting for transfers between devices, send(): return lax.ppermute(block, ('slab', 'row'), route)  72.4 us
    ppermute x27, starting transfers between devices, send(): return lax.ppermute(block, ('slab', 'row'), route)  27.9 us
    ppermute x14, starting transfers between devices, z_send(): return lax.ppermute(block, ('slab', 'col'), route)  23.7 us
    ppermute x14, waiting for transfers between devices, z_send(): return lax.ppermute(block, ('slab', 'col'), route)  20.8 us
    pallas_call x4, Pallas kernels, multiply_some(): pl.pallas_call(functools.partial(fold, [piece[:2] for piece in pieces], l...  6.34 us
    pallas_call x2, Pallas kernels, multiply_tiles(): pl.pallas_call(functools.partial(fold_tiles, beside is not None), in_spec...  5.19 us
  transfers between devices with their start and end apart: 41, of which 30 were waited for; matrix products, arithmetic and copies ran while one was open for 2% of the time, Pallas kernels for 4%

profile of v2, /device:TPU:16, one launch (start us, length us, event | category | flops | bytes accessed | tf_op | source)
XLA Modules:
  0.0 160.3 jit_solution(6912323663723483405)
XLA Ops:
  0.0 5.3 %collective-permute-start.10 = (bf16[512,512]{1,0:T(8,128)(2,1)}, bf16[512,512]{1,0:T(8,128)(2,1)S(1)}, u32[]{:S(2)}, u32[]{:S(2)}) collective-permute-start(bf16[512,512]{1,0:T(8,128)(2,1)} %bitcast.17), channel_id=1, source_target_pairs={{0,71},{1,64},{2,65},{3,66},{4,67},{5,68},{6,69},{7,70},{64,7},{65... | collective-permute-start | bytes 1572872 | tf_op jit(solution)/shard_map/ppermute | solution.py:27
  7.4 7.2 %collective-permute-done.1 = bf16[512,256]{1,0:T(8,128)(2,1)S(1)} collective-permute-done((bf16[512,256]{1,0:T(8,128)(2,1)}, bf16[512,256]{1,0:T(8,128)(2,1)S(1)}, u32[]{:S(2)}, u32[]{:S(2)}) %collective-permute-start.1) | collective-permute-done | bytes 262176 | tf_op jit(solution)/shard_map/ppermute | solution.py:37
  14.7 1.6 collective-permute-start.4
  16.2 1.7 %collective-permute-start.2 = (bf16[2,512,256]{2,1,0:T(8,128)(2,1)S(1)}, bf16[2,512,256]{2,1,0:T(8,128)(2,1)}, u32[]{:S(2)}, u32[]{:S(2)}) collective-permute-start(bf16[2,512,256]{2,1,0:T(8,128)(2,1)S(1)} %pad_maximum_fusion.1), channel_id=1, source_target_pairs={{0,48},{8,56},{16,0},{24,8},{32,16},{40,24},{48,32},{56,40},{64,11... | collective-permute-start | bytes 1572872 | tf_op jit(solution)/shard_map/ppermute | solution.py:37
  18.0 3.5 %collective-permute-start.11 = (bf16[512,512]{1,0:T(8,128)(2,1)S(1)}, bf16[512,512]{1,0:T(8,128)(2,1)S(1)}, u32[]{:S(2)}, u32[]{:S(2)}) collective-permute-start(bf16[512,512]{1,0:T(8,128)(2,1)S(1)} %collective-permute-done.10.refs_1_), channel_id=1, source_target_pairs={{0,7},{1,0},{2,1},{3,2},{4,3},{5,4},{6,5},{7,6},{64,71},{65,64},{6... | collective-permute-start | bytes 1572872 | tf_op jit(solution)/shard_map/ppermute | solution.py:27
  21.5 8.7 %collective-permute-done.2 = bf16[2,512,256]{2,1,0:T(8,128)(2,1)} collective-permute-done((bf16[2,512,256]{2,1,0:T(8,128)(2,1)S(1)}, bf16[2,512,256]{2,1,0:T(8,128)(2,1)}, u32[]{:S(2)}, u32[]{:S(2)}) %collective-permute-start.2) | collective-permute-done | bytes 524320 | tf_op jit(solution)/shard_map/ppermute | solution.py:37
  30.2 3.0 %collective-permute-start.3 = (bf16[2,512,256]{2,1,0:T(8,128)(2,1)}, bf16[2,512,256]{2,1,0:T(8,128)(2,1)}, u32[]{:S(2)}, u32[]{:S(2)}) collective-permute-start(bf16[2,512,256]{2,1,0:T(8,128)(2,1)} %collective-permute-done.2), channel_id=1, source_target_pairs={{0,48},{8,56},{16,0},{24,8},{32,16},{40,24},{48,32},{56,40},{64,11... | collective-permute-start | bytes 1572872 | tf_op jit(solution)/shard_map/ppermute | solution.py:37
  33.2 3.5 %collective-permute-start.12 = (bf16[512,512]{1,0:T(8,128)(2,1)S(1)}, bf16[512,512]{1,0:T(8,128)(2,1)S(1)}, u32[]{:S(2)}, u32[]{:S(2)}) collective-permute-start(bf16[512,512]{1,0:T(8,128)(2,1)S(1)} %collective-permute-done.11.refs_2_), channel_id=1, source_target_pairs={{0,7},{1,0},{2,1},{3,2},{4,3},{5,4},{6,5},{7,6},{64,71},{65,64},{6... | collective-permute-start | bytes 1572872 | tf_op jit(solution)/shard_map/ppermute | solution.py:27
  36.9 7.1 %collective-permute-done.3 = bf16[2,512,256]{2,1,0:T(8,128)(2,1)} collective-permute-done((bf16[2,512,256]{2,1,0:T(8,128)(2,1)}, bf16[2,512,256]{2,1,0:T(8,128)(2,1)}, u32[]{:S(2)}, u32[]{:S(2)}) %collective-permute-start.3) | collective-permute-done | bytes 524320 | tf_op jit(solution)/shard_map/ppermute | solution.py:37
  44.0 3.3 %collective-permute-done.12.refs_3_ = bf16[512,512]{1,0:T(8,128)(2,1)S(1)} collective-permute-done((bf16[512,512]{1,0:T(8,128)(2,1)S(1)}, bf16[512,512]{1,0:T(8,128)(2,1)S(1)}, u32[]{:S(2)}, u32[]{:S(2)}) %collective-permute-start.12) | collective-permute-done | bytes 524320 | tf_op jit(solution)/shard_map/ppermute | solution.py:27
  47.3 3.7 %collective-permute-start.13 = (bf16[512,512]{1,0:T(8,128)(2,1)S(1)}, bf16[512,512]{1,0:T(8,128)(2,1)S(1)}, u32[]{:S(2)}, u32[]{:S(2)}) collective-permute-start(bf16[512,512]{1,0:T(8,128)(2,1)S(1)} %collective-permute-done.12.refs_3_), channel_id=1, source_target_pairs={{0,7},{1,0},{2,1},{3,2},{4,3},{5,4},{6,5},{7,6},{64,71},{65,64},{6... | collective-permute-start | bytes 1572872 | tf_op jit(solution)/shard_map/ppermute | solution.py:27
  53.4 1.1 constant_dynamic-update-slice_fusion.1
  54.5 6.2 %collective-permute-done.13.refs_4_ = bf16[512,512]{1,0:T(8,128)(2,1)S(1)} collective-permute-done((bf16[512,512]{1,0:T(8,128)(2,1)S(1)}, bf16[512,512]{1,0:T(8,128)(2,1)S(1)}, u32[]{:S(2)}, u32[]{:S(2)}) %collective-permute-start.13) | collective-permute-done | bytes 524320 | tf_op jit(solution)/shard_map/ppermute | solution.py:27
  60.7 3.7 %collective-permute-start.15 = (bf16[512,512]{1,0:T(8,128)(2,1)S(1)}, bf16[512,512]{1,0:T(8,128)(2,1)S(1)}, u32[]{:S(2)}, u32[]{:S(2)}) collective-permute-start(bf16[512,512]{1,0:T(8,128)(2,1)S(1)} %bitcast.12), channel_id=1, source_target_pairs={{0,7},{1,0},{2,1},{3,2},{4,3},{5,4},{6,5},{7,6},{64,71},{65,64},{6... | collective-permute-start | bytes 1572872 | tf_op jit(solution)/shard_map/ppermute | solution.py:27
  65.1 2.9 %shard_map.37 = (bf16[512,256]{1,0:T(8,128)(2,1)S(1)}, bf16[8,512,512]{2,1,0:T(8,128)(2,1)S(1)}) custom-call(s32[8]{0:T(128)S(1)} %fusion.6.order, bf16[8,512,256]{2,1,0:T(8,128)(2,1)S(1)} %constant_dynamic-update-slice_fusion.shots, bf16[512,512]{1,0:T(8,128)(2,1)S(1)} %collective-permute-done.6.refs_0_, ...), custom_call_target="tpu_custom_call" | custom-call | flops 1073741824 | bytes 6291456 | tf_op jit(solution)/shard_map/pallas_call | solution.py:118
  68.0 1.4 collective-permute-start.14
  69.4 5.1 %collective-permute-done.14 = bf16[512,256]{1,0:T(8,128)(2,1)S(1)} collective-permute-done((bf16[512,256]{1,0:T(8,128)(2,1)S(1)}, bf16[512,256]{1,0:T(8,128)(2,1)S(1)}, u32[]{:S(2)}, u32[]{:S(2)}) %collective-permute-start.14) | collective-permute-done | bytes 262176 | tf_op jit(solution)/shard_map/ppermute | solution.py:37
  74.5 3.2 %collective-permute-done.16.refs_6_ = bf16[512,512]{1,0:T(8,128)(2,1)S(1)} collective-permute-done((bf16[512,512]{1,0:T(8,128)(2,1)S(1)}, bf16[512,512]{1,0:T(8,128)(2,1)S(1)}, u32[]{:S(2)}, u32[]{:S(2)}) %collective-permute-start.16) | collective-permute-done | bytes 524320 | tf_op jit(solution)/shard_map/ppermute | solution.py:27
  77.7 3.6 %collective-permute-start.17 = (bf16[2,512,256]{2,1,0:T(8,128)(2,1)S(1)}, bf16[2,512,256]{2,1,0:T(8,128)(2,1)S(1)}, u32[]{:S(2)}, u32[]{:S(2)}) collective-permute-start(bf16[2,512,256]{2,1,0:T(8,128)(2,1)S(1)} %pad_maximum_fusion.2), channel_id=1, source_target_pairs={{0,48},{8,56},{16,0},{24,8},{32,16},{40,24},{48,32},{56,40},{64,11... | collective-permute-start | bytes 1572872 | tf_op jit(solution)/shard_map/ppermute | solution.py:37
  81.3 2.0 %collective-permute-start.19 = (bf16[512,512]{1,0:T(8,128)(2,1)S(1)}, bf16[512,512]{1,0:T(8,128)(2,1)S(1)}, u32[]{:S(2)}, u32[]{:S(2)}) collective-permute-start(bf16[512,512]{1,0:T(8,128)(2,1)S(1)} %collective-permute-done.16.refs_6_), channel_id=1, source_target_pairs={{0,1},{1,2},{2,3},{3,4},{4,5},{5,6},{6,7},{7,0},{64,65},{65,66},{6... | collective-permute-start | bytes 1572872 | tf_op jit(solution)/shard_map/ppermute | solution.py:27
  83.3 6.2 %collective-permute-done.17 = bf16[2,512,256]{2,1,0:T(8,128)(2,1)S(1)} collective-permute-done((bf16[2,512,256]{2,1,0:T(8,128)(2,1)S(1)}, bf16[2,512,256]{2,1,0:T(8,128)(2,1)S(1)}, u32[]{:S(2)}, u32[]{:S(2)}) %collective-permute-start.17) | collective-permute-done | bytes 524320 | tf_op jit(solution)/shard_map/ppermute | solution.py:37
  89.6 2.2 %collective-permute-done.18.refs_2_ = bf16[512,512]{1,0:T(8,128)(2,1)S(1)} collective-permute-done((bf16[512,512]{1,0:T(8,128)(2,1)S(1)}, bf16[512,512]{1,0:T(8,128)(2,1)S(1)}, u32[]{:S(2)}, u32[]{:S(2)}) %collective-permute-start.18) | collective-permute-done | bytes 524320 | tf_op jit(solution)/shard_map/ppermute | solution.py:27
  91.8 1.2 collective-permute-done.19.refs_5_
  93.3 1.1 collective-permute-done.21
  94.4 1.5 collective-permute-start.22
  96.5 6.0 %collective-permute-done.20 = bf16[2,512,256]{2,1,0:T(8,128)(2,1)S(1)} collective-permute-done((bf16[2,512,256]{2,1,0:T(8,128)(2,1)S(1)}, bf16[2,512,256]{2,1,0:T(8,128)(2,1)S(1)}, u32[]{:S(2)}, u32[]{:S(2)}) %collective-permute-start.20) | collective-permute-done | bytes 524320 | tf_op jit(solution)/shard_map/ppermute | solution.py:37
  103.6 2.7 %collective-permute-done.23.refs_4_ = bf16[512,512]{1,0:T(8,128)(2,1)S(1)} collective-permute-done((bf16[512,512]{1,0:T(8,128)(2,1)S(1)}, bf16[512,512]{1,0:T(8,128)(2,1)S(1)}, u32[]{:S(2)}, u32[]{:S(2)}) %collective-permute-start.23) | collective-permute-done | bytes 524320 | tf_op jit(solution)/shard_map/ppermute | solution.py:27
  106.3 2.3 %shard_map.38 = (bf16[512,256]{1,0:T(8,128)(2,1)S(1)}, bf16[2,512,256]{2,1,0:T(8,128)(2,1)S(1)}, bf16[8,512,512]{2,1,0:T(8,128)(2,1)S(1)}) custom-call(s32[8]{0:T(128)S(1)} %fusion.6.order, bf16[8,512,256]{2,1,0:T(8,128)(2,1)S(1)} %pad_maximum_fusion.shots, bf16[512,512]{1,0:T(8,128)(2,1)S(1)} %bitcast.13, ...), custom_call_target="tpu_custom_call" | custom-call | flops 1073741824 | bytes 6291456 | tf_op jit(solution)/shard_map/pallas_call | solution.py:118
  108.8 1.7 %collective-permute-start.25 = (bf16[512,256]{1,0:T(8,128)(2,1)S(1)}, bf16[512,256]{1,0:T(8,128)(2,1)S(1)}, u32[]{:S(2)}, u32[]{:S(2)}) collective-permute-start(bf16[512,256]{1,0:T(8,128)(2,1)S(1)} %get-tuple-element.45), channel_id=1, source_target_pairs={{0,80},{8,88},{16,96},{24,104},{32,112},{40,120},{48,64},{56,72},{... | collective-permute-start | bytes 786440 | tf_op jit(solution)/shard_map/ppermute | solution.py:37
  110.5 1.4 collective-permute-start.31
  111.9 3.4 %collective-permute-done.28.refs_2_ = bf16[512,256]{1,0:T(8,128)(2,1)S(1)} collective-permute-done((bf16[512,256]{1,0:T(8,128)(2,1)S(1)}, bf16[512,256]{1,0:T(8,128)(2,1)S(1)}, u32[]{:S(2)}, u32[]{:S(2)}) %collective-permute-start.28) | collective-permute-done | bytes 262176 | tf_op jit(solution)/shard_map/ppermute | solution.py:37
  115.3 3.1 %collective-permute-done.25.refs_3_ = bf16[512,256]{1,0:T(8,128)(2,1)S(1)} collective-permute-done((bf16[512,256]{1,0:T(8,128)(2,1)S(1)}, bf16[512,256]{1,0:T(8,128)(2,1)S(1)}, u32[]{:S(2)}, u32[]{:S(2)}) %collective-permute-start.25) | collective-permute-done | bytes 262176 | tf_op jit(solution)/shard_map/ppermute | solution.py:37
  118.9 1.5 collective-permute-start.26
  120.4 1.3 collective-permute-start.32
  121.7 4.8 %collective-permute-done.29.refs_5_ = bf16[512,256]{1,0:T(8,128)(2,1)S(1)} collective-permute-done((bf16[512,256]{1,0:T(8,128)(2,1)S(1)}, bf16[512,256]{1,0:T(8,128)(2,1)S(1)}, u32[]{:S(2)}, u32[]{:S(2)}) %collective-permute-start.29) | collective-permute-done | bytes 262176 | tf_op jit(solution)/shard_map/ppermute | solution.py:37
  126.5 1.6 collective-permute-start.30
  128.4 1.8 %shard_map.39.refs_2_ = f32[512,256]{1,0:T(8,128)S(1)} custom-call(s32[8]{0:T(128)S(1)} %and_select_fusion.4.order, bf16[8,512,512]{2,1,0:T(8,128)(2,1)S(1)} %get-tuple-element.44.operator, bf16[2,512,256]{2,1,0:T(8,128)(2,1)S(1)} %collective-permute-done.31.refs_0_, bf16[512,256]{1,0:T(8,128)(2,1)S(1)} %collective-permute-done.24.refs_1_, ...), custom_call_target="tpu_custom_call" | custom-call | flops 939524096 | bytes 5505024 | tf_op jit(solution)/shard_map/pallas_call | solution.py:160
  130.3 1.5 collective-permute-done.30.refs_1_
  131.8 2.8 %collective-permute-done.27.refs_0_ = bf16[256,256]{1,0:T(8,128)(2,1)S(1)} collective-permute-done((bf16[256,256]{1,0:T(8,128)(2,1)S(1)}, bf16[256,256]{1,0:T(8,128)(2,1)S(1)}, u32[]{:S(2)}, u32[]{:S(2)}) %collective-permute-start.27) | collective-permute-done | bytes 131104 | tf_op jit(solution)/shard_map/ppermute | solution.py:37
  135.7 2.0 %collective-permute-start.34 = (bf16[512,256]{1,0:T(8,128)(2,1)S(1)}, bf16[512,256]{1,0:T(8,128)(2,1)S(1)}, u32[]{:S(2)}, u32[]{:S(2)}) collective-permute-start(bf16[512,256]{1,0:T(8,128)(2,1)S(1)} %shard_map.40.refs_0_), channel_id=1, source_target_pairs={{0,16},{8,24},{16,32},{24,40},{32,48},{40,56},{48,0},{56,8},{64,80... | collective-permute-start | bytes 786440 | tf_op jit(solution)/shard_map/ppermute | solution.py:37
  138.4 3.7 %collective-permute-done.37.refs_2_ = bf16[512,256]{1,0:T(8,128)(2,1)S(1)} collective-permute-done((bf16[512,256]{1,0:T(8,128)(2,1)S(1)}, bf16[512,256]{1,0:T(8,128)(2,1)S(1)}, u32[]{:S(2)}, u32[]{:S(2)}) %collective-permute-start.37) | collective-permute-done | bytes 262176 | tf_op jit(solution)/shard_map/ppermute | solution.py:37
  142.0 1.3 collective-permute-done.34.refs_3_
  144.0 1.3 collective-permute-start.35
  146.1 3.6 %collective-permute-done.38.refs_5_ = bf16[512,256]{1,0:T(8,128)(2,1)S(1)} collective-permute-done((bf16[512,256]{1,0:T(8,128)(2,1)S(1)}, bf16[512,256]{1,0:T(8,128)(2,1)S(1)}, u32[]{:S(2)}, u32[]{:S(2)}) %collective-permute-start.38) | collective-permute-done | bytes 262176 | tf_op jit(solution)/shard_map/ppermute | solution.py:37
  150.5 1.8 %collective-permute-done.35.refs_4_ = bf16[512,256]{1,0:T(8,128)(2,1)S(1)} collective-permute-done((bf16[512,256]{1,0:T(8,128)(2,1)S(1)}, bf16[512,256]{1,0:T(8,128)(2,1)S(1)}, u32[]{:S(2)}, u32[]{:S(2)}) %collective-permute-start.35) | collective-permute-done | bytes 262176 | tf_op jit(solution)/shard_map/ppermute | solution.py:37
  153.2 1.8 %shard_map.41.refs_2_ = f32[512,256]{1,0:T(8,128)S(1)} custom-call(s32[8]{0:T(128)S(1)} %and_select_fusion.4.order, bf16[8,512,512]{2,1,0:T(8,128)(2,1)S(1)} %get-tuple-element.35.operator, bf16[512,256]{1,0:T(8,128)(2,1)S(1)} %shard_map.40.refs_0_, bf16[512,256]{1,0:T(8,128)(2,1)S(1)} %collective-permute-done.33.refs_1_, ...), custom_call_target="tpu_custom_call" | custom-call | flops 939524096 | bytes 5505024 | tf_op jit(solution)/shard_map/pallas_call | solution.py:160
  155.1 3.5 %collective-permute-done.36.refs_0_ = bf16[256,256]{1,0:T(8,128)(2,1)S(1)} collective-permute-done((bf16[256,256]{1,0:T(8,128)(2,1)S(1)}, bf16[256,256]{1,0:T(8,128)(2,1)S(1)}, u32[]{:S(2)}, u32[]{:S(2)}) %collective-permute-start.36) | collective-permute-done | bytes 131104 | tf_op jit(solution)/shard_map/ppermute | solution.py:37
  158.6 1.7 %shard_map.42 = bf16[512,256]{1,0:T(8,128)(2,1)} custom-call(s32[8]{0:T(128)S(1)} %and_select_fusion.4.order, bf16[8,512,512]{2,1,0:T(8,128)(2,1)S(1)} %get-tuple-element.35.operator, bf16[256,256]{1,0:T(8,128)(2,1)S(1)} %collective-permute-done.36.refs_0_, bf16[256,256]{1,0:T(8,128)(2,1)S(1)} %collective-permute-done.39.refs_1_, ...), custom_call_target="tpu_custom_call" | custom-call | flops 134217728 | bytes 786432 | tf_op jit(solution)/shard_map/pallas_call | solution.py:160
  (62 shorter events, 13.6 us)
Async XLA Ops:
  0.0 18.0 %collective-permute-start.10 = (bf16[512,512]{1,0:T(8,128)(2,1)}, bf16[512,512]{1,0:T(8,128)(2,1)S(1)}, u32[]{:S(2)}, u32[]{:S(2)}) collective-permute-start(bf16[512,512]{1,0:T(8,128)(2,1)} %bitcast.17), channel_id=1, source_target_pairs={{0,71},{1,64},{2,65},{3,66},{4,67},{5,68},{6,69},{7,70},{64,7},{65... | collective-permute-start | bytes 1572872 | tf_op jit(solution)/shard_map/ppermute | solution.py:27
  5.3 12.7 %collective-permute-start.6 = (bf16[512,512]{1,0:T(8,128)(2,1)}, bf16[512,512]{1,0:T(8,128)(2,1)S(1)}, u32[]{:S(2)}, u32[]{:S(2)}) collective-permute-start(bf16[512,512]{1,0:T(8,128)(2,1)} %bitcast.18), channel_id=1, source_target_pairs={{0,64},{8,72},{16,80},{24,88},{32,96},{40,104},{48,112},{56,120},{... | collective-permute-start | bytes 1572872 | tf_op jit(solution)/shard_map/ppermute | solution.py:37
  6.0 15.5 %collective-permute-start.5 = (bf16[512,512]{1,0:T(8,128)(2,1)}, bf16[512,512]{1,0:T(8,128)(2,1)S(1)}, u32[]{:S(2)}, u32[]{:S(2)}) collective-permute-start(bf16[512,512]{1,0:T(8,128)(2,1)} %bitcast.19), channel_id=1, source_target_pairs={{0,65},{1,66},{2,67},{3,68},{4,69},{5,70},{6,71},{7,64},{64,1},{65... | collective-permute-start | bytes 1572872 | tf_op jit(solution)/shard_map/ppermute | solution.py:27
  6.0 8.6 %collective-permute-start.1 = (bf16[512,256]{1,0:T(8,128)(2,1)}, bf16[512,256]{1,0:T(8,128)(2,1)S(1)}, u32[]{:S(2)}, u32[]{:S(2)}) collective-permute-start(bf16[512,256]{1,0:T(8,128)(2,1)} %bitcast.20), channel_id=1, source_target_pairs={{0,72},{8,64},{16,88},{24,80},{32,104},{40,96},{48,120},{56,112},{... | collective-permute-start | bytes 786440 | tf_op jit(solution)/shard_map/ppermute | solution.py:37
  6.9 7.7 %collective-permute-start = (bf16[512,256]{1,0:T(8,128)(2,1)}, bf16[512,256]{1,0:T(8,128)(2,1)S(1)}, u32[]{:S(2)}, u32[]{:S(2)}) collective-permute-start(bf16[512,256]{1,0:T(8,128)(2,1)} %bitcast.21), channel_id=1, source_target_pairs={{0,64},{8,72},{16,80},{24,88},{32,96},{40,104},{48,112},{56,120},{... | collective-permute-start | bytes 786440 | tf_op jit(solution)/shard_map/ppermute | solution.py:37
  14.6 22.2 %copy-start.1 = (bf16[512,256]{1,0:T(8,128)(2,1)}, bf16[512,256]{1,0:T(8,128)(2,1)S(1)}, u32[]{:S(2)}) copy-start(bf16[512,256]{1,0:T(8,128)(2,1)S(1)} %collective-permute-done) | copy-start | bytes 786436
  14.7 18.5 %collective-permute-start.4 = (bf16[2,512,256]{2,1,0:T(8,128)(2,1)S(1)}, bf16[2,512,256]{2,1,0:T(8,128)(2,1)S(1)}, u32[]{:S(2)}, u32[]{:S(2)}) collective-permute-start(bf16[2,512,256]{2,1,0:T(8,128)(2,1)S(1)} %pad_maximum_fusion.1), channel_id=1, source_target_pairs={{0,16},{8,24},{16,32},{24,40},{32,48},{40,56},{48,0},{56,8},{64,80... | collective-permute-start | bytes 1572872 | tf_op jit(solution)/shard_map/ppermute | solution.py:37
  16.2 14.0 %collective-permute-start.2 = (bf16[2,512,256]{2,1,0:T(8,128)(2,1)S(1)}, bf16[2,512,256]{2,1,0:T(8,128)(2,1)}, u32[]{:S(2)}, u32[]{:S(2)}) collective-permute-start(bf16[2,512,256]{2,1,0:T(8,128)(2,1)S(1)} %pad_maximum_fusion.1), channel_id=1, source_target_pairs={{0,48},{8,56},{16,0},{24,8},{32,16},{40,24},{48,32},{56,40},{64,11... | collective-permute-start | bytes 1572872 | tf_op jit(solution)/shard_map/ppermute | solution.py:37
  18.0 15.2 %collective-permute-start.11 = (bf16[512,512]{1,0:T(8,128)(2,1)S(1)}, bf16[512,512]{1,0:T(8,128)(2,1)S(1)}, u32[]{:S(2)}, u32[]{:S(2)}) collective-permute-start(bf16[512,512]{1,0:T(8,128)(2,1)S(1)} %collective-permute-done.10.refs_1_), channel_id=1, source_target_pairs={{0,7},{1,0},{2,1},{3,2},{4,3},{5,4},{6,5},{7,6},{64,71},{65,64},{6... | collective-permute-start | bytes 1572872 | tf_op jit(solution)/shard_map/ppermute | solution.py:27
  21.5 15.3 %collective-permute-start.7 = (bf16[512,512]{1,0:T(8,128)(2,1)S(1)}, bf16[512,512]{1,0:T(8,128)(2,1)S(1)}, u32[]{:S(2)}, u32[]{:S(2)}) collective-permute-start(bf16[512,512]{1,0:T(8,128)(2,1)S(1)} %collective-permute-done.5.refs_7_), channel_id=1, source_target_pairs={{0,1},{1,2},{2,3},{3,4},{4,5},{5,6},{6,7},{7,0},{64,65},{65,66},{6... | collective-permute-start | bytes 1572872 | tf_op jit(solution)/shard_map/ppermute | solution.py:27
  30.2 13.8 %collective-permute-start.3 = (bf16[2,512,256]{2,1,0:T(8,128)(2,1)}, bf16[2,512,256]{2,1,0:T(8,128)(2,1)}, u32[]{:S(2)}, u32[]{:S(2)}) collective-permute-start(bf16[2,512,256]{2,1,0:T(8,128)(2,1)} %collective-permute-done.2), channel_id=1, source_target_pairs={{0,48},{8,56},{16,0},{24,8},{32,16},{40,24},{48,32},{56,40},{64,11... | collective-permute-start | bytes 1572872 | tf_op jit(solution)/shard_map/ppermute | solution.py:37
  33.2 3.6 %copy-start.2 = (bf16[2,512,256]{2,1,0:T(8,128)(2,1)}, bf16[2,512,256]{2,1,0:T(8,128)(2,1)S(1)}, u32[]{:S(2)}) copy-start(bf16[2,512,256]{2,1,0:T(8,128)(2,1)S(1)} %collective-permute-done.4) | copy-start | bytes 1572868
  33.2 14.1 %collective-permute-start.12 = (bf16[512,512]{1,0:T(8,128)(2,1)S(1)}, bf16[512,512]{1,0:T(8,128)(2,1)S(1)}, u32[]{:S(2)}, u32[]{:S(2)}) collective-permute-start(bf16[512,512]{1,0:T(8,128)(2,1)S(1)} %collective-permute-done.11.refs_2_), channel_id=1, source_target_pairs={{0,7},{1,0},{2,1},{3,2},{4,3},{5,4},{6,5},{7,6},{64,71},{65,64},{6... | collective-permute-start | bytes 1572872 | tf_op jit(solution)/shard_map/ppermute | solution.py:27
  36.8 14.6 %collective-permute-start.8 = (bf16[512,512]{1,0:T(8,128)(2,1)S(1)}, bf16[512,512]{1,0:T(8,128)(2,1)}, u32[]{:S(2)}, u32[]{:S(2)}) collective-permute-start(bf16[512,512]{1,0:T(8,128)(2,1)S(1)} %collective-permute-done.7.refs_6_), channel_id=1, source_target_pairs={{0,1},{1,2},{2,3},{3,4},{4,5},{5,6},{6,7},{7,0},{64,65},{65,66},{6... | collective-permute-start | bytes 1572872 | tf_op jit(solution)/shard_map/ppermute | solution.py:27
  36.8 23.9 %copy-start = (bf16[1,512,512]{2,1,0:T(8,128)(2,1)S(1)}, bf16[1,512,512]{2,1,0:T(8,128)(2,1)}, u32[]{:S(2)}) copy-start(bf16[1,512,512]{2,1,0:T(8,128)(2,1)} %param.3) | copy-start | bytes 1572868
  36.8 28.3 %copy-start.3 = (bf16[2,512,256]{2,1,0:T(8,128)(2,1)S(1)}, bf16[2,512,256]{2,1,0:T(8,128)(2,1)}, u32[]{:S(2)}) copy-start(bf16[2,512,256]{2,1,0:T(8,128)(2,1)} %copy-done.2) | copy-start | bytes 1572868
  47.3 13.4 %collective-permute-start.13 = (bf16[512,512]{1,0:T(8,128)(2,1)S(1)}, bf16[512,512]{1,0:T(8,128)(2,1)S(1)}, u32[]{:S(2)}, u32[]{:S(2)}) collective-permute-start(bf16[512,512]{1,0:T(8,128)(2,1)S(1)} %collective-permute-done.12.refs_3_), channel_id=1, source_target_pairs={{0,7},{1,0},{2,1},{3,2},{4,3},{5,4},{6,5},{7,6},{64,71},{65,64},{6... | collective-permute-start | bytes 1572872 | tf_op jit(solution)/shard_map/ppermute | solution.py:27
  51.3 13.7 %collective-permute-start.9 = (bf16[512,512]{1,0:T(8,128)(2,1)}, bf16[512,512]{1,0:T(8,128)(2,1)S(1)}, u32[]{:S(2)}, u32[]{:S(2)}) collective-permute-start(bf16[512,512]{1,0:T(8,128)(2,1)} %bitcast.11), channel_id=1, source_target_pairs={{0,1},{1,2},{2,3},{3,4},{4,5},{5,6},{6,7},{7,0},{64,65},{65,66},{6... | collective-permute-start | bytes 1572872 | tf_op jit(solution)/shard_map/ppermute | solution.py:27
  60.7 17.0 %collective-permute-start.15 = (bf16[512,512]{1,0:T(8,128)(2,1)S(1)}, bf16[512,512]{1,0:T(8,128)(2,1)S(1)}, u32[]{:S(2)}, u32[]{:S(2)}) collective-permute-start(bf16[512,512]{1,0:T(8,128)(2,1)S(1)} %bitcast.12), channel_id=1, source_target_pairs={{0,7},{1,0},{2,1},{3,2},{4,3},{5,4},{6,5},{7,6},{64,71},{65,64},{6... | collective-permute-start | bytes 1572872 | tf_op jit(solution)/shard_map/ppermute | solution.py:27
  65.1 12.6 %collective-permute-start.16 = (bf16[512,512]{1,0:T(8,128)(2,1)S(1)}, bf16[512,512]{1,0:T(8,128)(2,1)S(1)}, u32[]{:S(2)}, u32[]{:S(2)}) collective-permute-start(bf16[512,512]{1,0:T(8,128)(2,1)S(1)} %collective-permute-done.9.refs_7_), channel_id=1, source_target_pairs={{0,1},{1,2},{2,3},{3,4},{4,5},{5,6},{6,7},{7,0},{64,65},{65,66},{6... | collective-permute-start | bytes 1572872 | tf_op jit(solution)/shard_map/ppermute | solution.py:27
  68.0 6.5 %collective-permute-start.14 = (bf16[512,256]{1,0:T(8,128)(2,1)S(1)}, bf16[512,256]{1,0:T(8,128)(2,1)S(1)}, u32[]{:S(2)}, u32[]{:S(2)}) collective-permute-start(bf16[512,256]{1,0:T(8,128)(2,1)S(1)} %get-tuple-element.36.refs_8_), channel_id=1, source_target_pairs={{0,8},{8,0},{16,24},{24,16},{32,40},{40,32},{48,56},{56,48},{64,72... | collective-permute-start | bytes 786440 | tf_op jit(solution)/shard_map/ppermute | solution.py:37
  77.7 11.9 %collective-permute-start.17 = (bf16[2,512,256]{2,1,0:T(8,128)(2,1)S(1)}, bf16[2,512,256]{2,1,0:T(8,128)(2,1)S(1)}, u32[]{:S(2)}, u32[]{:S(2)}) collective-permute-start(bf16[2,512,256]{2,1,0:T(8,128)(2,1)S(1)} %pad_maximum_fusion.2), channel_id=1, source_target_pairs={{0,48},{8,56},{16,0},{24,8},{32,16},{40,24},{48,32},{56,40},{64,11... | collective-permute-start | bytes 1572872 | tf_op jit(solution)/shard_map/ppermute | solution.py:37
  81.3 10.5 %collective-permute-start.18 = (bf16[512,512]{1,0:T(8,128)(2,1)S(1)}, bf16[512,512]{1,0:T(8,128)(2,1)S(1)}, u32[]{:S(2)}, u32[]{:S(2)}) collective-permute-start(bf16[512,512]{1,0:T(8,128)(2,1)S(1)} %collective-permute-done.15.refs_1_), channel_id=1, source_target_pairs={{0,7},{1,0},{2,1},{3,2},{4,3},{5,4},{6,5},{7,6},{64,71},{65,64},{6... | collective-permute-start | bytes 1572872 | tf_op jit(solution)/shard_map/ppermute | solution.py:27
  81.3 11.7 %collective-permute-start.19 = (bf16[512,512]{1,0:T(8,128)(2,1)S(1)}, bf16[512,512]{1,0:T(8,128)(2,1)S(1)}, u32[]{:S(2)}, u32[]{:S(2)}) collective-permute-start(bf16[512,512]{1,0:T(8,128)(2,1)S(1)} %collective-permute-done.16.refs_6_), channel_id=1, source_target_pairs={{0,1},{1,2},{2,3},{3,4},{4,5},{5,6},{6,7},{7,0},{64,65},{65,66},{6... | collective-permute-start | bytes 1572872 | tf_op jit(solution)/shard_map/ppermute | solution.py:27
  83.3 11.1 %collective-permute-start.21 = (bf16[2,512,256]{2,1,0:T(8,128)(2,1)S(1)}, bf16[2,512,256]{2,1,0:T(8,128)(2,1)S(1)}, u32[]{:S(2)}, u32[]{:S(2)}) collective-permute-start(bf16[2,512,256]{2,1,0:T(8,128)(2,1)S(1)} %pad_maximum_fusion.2), channel_id=1, source_target_pairs={{0,16},{8,24},{16,32},{24,40},{32,48},{40,56},{48,0},{56,8},{64,80... | collective-permute-start | bytes 1572872 | tf_op jit(solution)/shard_map/ppermute | solution.py:37
  93.0 9.5 %collective-permute-start.20 = (bf16[2,512,256]{2,1,0:T(8,128)(2,1)S(1)}, bf16[2,512,256]{2,1,0:T(8,128)(2,1)S(1)}, u32[]{:S(2)}, u32[]{:S(2)}) collective-permute-start(bf16[2,512,256]{2,1,0:T(8,128)(2,1)S(1)} %collective-permute-done.17), channel_id=1, source_target_pairs={{0,48},{8,56},{16,0},{24,8},{32,16},{40,24},{48,32},{56,40},{64,11... | collective-permute-start | bytes 1572872 | tf_op jit(solution)/shard_map/ppermute | solution.py:37
  94.4 9.2 %collective-permute-start.22 = (bf16[512,512]{1,0:T(8,128)(2,1)S(1)}, bf16[512,512]{1,0:T(8,128)(2,1)S(1)}, u32[]{:S(2)}, u32[]{:S(2)}) collective-permute-start(bf16[512,512]{1,0:T(8,128)(2,1)S(1)} %collective-permute-done.18.refs_2_), channel_id=1, source_target_pairs={{0,7},{1,0},{2,1},{3,2},{4,3},{5,4},{6,5},{7,6},{64,71},{65,64},{6... | collective-permute-start | bytes 1572872 | tf_op jit(solution)/shard_map/ppermute | solution.py:27
  95.9 10.4 %collective-permute-start.23 = (bf16[512,512]{1,0:T(8,128)(2,1)S(1)}, bf16[512,512]{1,0:T(8,128)(2,1)S(1)}, u32[]{:S(2)}, u32[]{:S(2)}) collective-permute-start(bf16[512,512]{1,0:T(8,128)(2,1)S(1)} %collective-permute-done.19.refs_5_), channel_id=1, source_target_pairs={{0,1},{1,2},{2,3},{3,4},{4,5},{5,6},{6,7},{7,0},{64,65},{65,66},{6... | collective-permute-start | bytes 1572872 | tf_op jit(solution)/shard_map/ppermute | solution.py:27
  108.7 6.7 %collective-permute-start.28 = (bf16[512,256]{1,0:T(8,128)(2,1)S(1)}, bf16[512,256]{1,0:T(8,128)(2,1)S(1)}, u32[]{:S(2)}, u32[]{:S(2)}) collective-permute-start(bf16[512,256]{1,0:T(8,128)(2,1)S(1)} %get-tuple-element.45), channel_id=1, source_target_pairs={{0,112},{8,120},{16,64},{24,72},{32,80},{40,88},{48,96},{56,104},{... | collective-permute-start | bytes 786440 | tf_op jit(solution)/shard_map/ppermute | solution.py:37
  108.8 9.6 %collective-permute-start.25 = (bf16[512,256]{1,0:T(8,128)(2,1)S(1)}, bf16[512,256]{1,0:T(8,128)(2,1)S(1)}, u32[]{:S(2)}, u32[]{:S(2)}) collective-permute-start(bf16[512,256]{1,0:T(8,128)(2,1)S(1)} %get-tuple-element.45), channel_id=1, source_target_pairs={{0,80},{8,88},{16,96},{24,104},{32,112},{40,120},{48,64},{56,72},{... | collective-permute-start | bytes 786440 | tf_op jit(solution)/shard_map/ppermute | solution.py:37
  110.5 8.4 %collective-permute-start.24 = (bf16[512,256]{1,0:T(8,128)(2,1)S(1)}, bf16[512,256]{1,0:T(8,128)(2,1)S(1)}, u32[]{:S(2)}, u32[]{:S(2)}) collective-permute-start(bf16[512,256]{1,0:T(8,128)(2,1)S(1)} %get-tuple-element.45), channel_id=1, source_target_pairs={{0,72},{8,64},{16,88},{24,80},{32,104},{40,96},{48,120},{56,112},{... | collective-permute-start | bytes 786440 | tf_op jit(solution)/shard_map/ppermute | solution.py:37
  110.5 17.9 %collective-permute-start.31 = (bf16[2,512,256]{2,1,0:T(8,128)(2,1)S(1)}, bf16[2,512,256]{2,1,0:T(8,128)(2,1)S(1)}, u32[]{:S(2)}, u32[]{:S(2)}) collective-permute-start(bf16[2,512,256]{2,1,0:T(8,128)(2,1)S(1)} %get-tuple-element.48), channel_id=1, source_target_pairs={{0,64},{8,72},{16,80},{24,88},{32,96},{40,104},{48,112},{56,120},{... | collective-permute-start | bytes 1572872 | tf_op jit(solution)/shard_map/ppermute | solution.py:37
  118.4 8.1 %collective-permute-start.29 = (bf16[512,256]{1,0:T(8,128)(2,1)S(1)}, bf16[512,256]{1,0:T(8,128)(2,1)S(1)}, u32[]{:S(2)}, u32[]{:S(2)}) collective-permute-start(bf16[512,256]{1,0:T(8,128)(2,1)S(1)} %collective-permute-done.28.refs_2_), channel_id=1, source_target_pairs={{0,48},{8,56},{16,0},{24,8},{32,16},{40,24},{48,32},{56,40},{64,11... | collective-permute-start | bytes 786440 | tf_op jit(solution)/shard_map/ppermute | solution.py:37
  118.9 9.4 %collective-permute-start.26 = (bf16[512,256]{1,0:T(8,128)(2,1)S(1)}, bf16[512,256]{1,0:T(8,128)(2,1)S(1)}, u32[]{:S(2)}, u32[]{:S(2)}) collective-permute-start(bf16[512,256]{1,0:T(8,128)(2,1)S(1)} %collective-permute-done.24.refs_1_), channel_id=1, source_target_pairs={{0,16},{8,24},{16,32},{24,40},{32,48},{40,56},{48,0},{56,8},{64,80... | collective-permute-start | bytes 786440 | tf_op jit(solution)/shard_map/ppermute | solution.py:37
  120.4 8.0 %collective-permute-start.32 = (bf16[512,256]{1,0:T(8,128)(2,1)S(1)}, bf16[512,256]{1,0:T(8,128)(2,1)S(1)}, u32[]{:S(2)}, u32[]{:S(2)}) collective-permute-start(bf16[512,256]{1,0:T(8,128)(2,1)S(1)} %collective-permute-done.28.refs_2_), channel_id=1, source_target_pairs={{0,8},{8,0},{16,24},{24,16},{32,40},{40,32},{48,56},{56,48},{64,72... | collective-permute-start | bytes 786440 | tf_op jit(solution)/shard_map/ppermute | solution.py:37
  126.5 5.3 %collective-permute-start.30 = (bf16[256,256]{1,0:T(8,128)(2,1)S(1)}, bf16[256,256]{1,0:T(8,128)(2,1)S(1)}, u32[]{:S(2)}, u32[]{:S(2)}) collective-permute-start(bf16[256,256]{1,0:T(8,128)(2,1)S(1)} %slice.17), channel_id=1, source_target_pairs={{0,8},{8,0},{16,24},{24,16},{32,40},{40,32},{48,56},{56,48},{64,72... | collective-permute-start | bytes 393224 | tf_op jit(solution)/shard_map/ppermute | solution.py:37
  128.3 6.3 %collective-permute-start.27 = (bf16[256,256]{1,0:T(8,128)(2,1)S(1)}, bf16[256,256]{1,0:T(8,128)(2,1)S(1)}, u32[]{:S(2)}, u32[]{:S(2)}) collective-permute-start(bf16[256,256]{1,0:T(8,128)(2,1)S(1)} %slice.16), channel_id=1, source_target_pairs={{0,16},{8,24},{16,32},{24,40},{32,48},{40,56},{48,0},{56,8},{64,80... | collective-permute-start | bytes 393224 | tf_op jit(solution)/shard_map/ppermute | solution.py:37
  135.6 6.4 %collective-permute-start.37 = (bf16[512,256]{1,0:T(8,128)(2,1)S(1)}, bf16[512,256]{1,0:T(8,128)(2,1)S(1)}, u32[]{:S(2)}, u32[]{:S(2)}) collective-permute-start(bf16[512,256]{1,0:T(8,128)(2,1)S(1)} %shard_map.40.refs_0_), channel_id=1, source_target_pairs={{0,48},{8,56},{16,0},{24,8},{32,16},{40,24},{48,32},{56,40},{64,11... | collective-permute-start | bytes 786440 | tf_op jit(solution)/shard_map/ppermute | solution.py:37
  135.7 7.6 %collective-permute-start.34 = (bf16[512,256]{1,0:T(8,128)(2,1)S(1)}, bf16[512,256]{1,0:T(8,128)(2,1)S(1)}, u32[]{:S(2)}, u32[]{:S(2)}) collective-permute-start(bf16[512,256]{1,0:T(8,128)(2,1)S(1)} %shard_map.40.refs_0_), channel_id=1, source_target_pairs={{0,16},{8,24},{16,32},{24,40},{32,48},{40,56},{48,0},{56,8},{64,80... | collective-permute-start | bytes 786440 | tf_op jit(solution)/shard_map/ppermute | solution.py:37
  137.7 6.4 %collective-permute-start.33 = (bf16[512,256]{1,0:T(8,128)(2,1)S(1)}, bf16[512,256]{1,0:T(8,128)(2,1)S(1)}, u32[]{:S(2)}, u32[]{:S(2)}) collective-permute-start(bf16[512,256]{1,0:T(8,128)(2,1)S(1)} %shard_map.40.refs_0_), channel_id=1, source_target_pairs={{0,8},{8,0},{16,24},{24,16},{32,40},{40,32},{48,56},{56,48},{64,72... | collective-permute-start | bytes 786440 | tf_op jit(solution)/shard_map/ppermute | solution.py:37
  143.3 6.4 %collective-permute-start.38 = (bf16[512,256]{1,0:T(8,128)(2,1)S(1)}, bf16[512,256]{1,0:T(8,128)(2,1)S(1)}, u32[]{:S(2)}, u32[]{:S(2)}) collective-permute-start(bf16[512,256]{1,0:T(8,128)(2,1)S(1)} %collective-permute-done.37.refs_2_), channel_id=1, source_target_pairs={{0,48},{8,56},{16,0},{24,8},{32,16},{40,24},{48,32},{56,40},{64,11... | collective-permute-start | bytes 786440 | tf_op jit(solution)/shard_map/ppermute | solution.py:37
  144.0 8.2 %collective-permute-start.35 = (bf16[512,256]{1,0:T(8,128)(2,1)S(1)}, bf16[512,256]{1,0:T(8,128)(2,1)S(1)}, u32[]{:S(2)}, u32[]{:S(2)}) collective-permute-start(bf16[512,256]{1,0:T(8,128)(2,1)S(1)} %collective-permute-done.33.refs_1_), channel_id=1, source_target_pairs={{0,16},{8,24},{16,32},{24,40},{32,48},{40,56},{48,0},{56,8},{64,80... | collective-permute-start | bytes 786440 | tf_op jit(solution)/shard_map/ppermute | solution.py:37
  145.4 7.9 %collective-permute-start.40 = (bf16[512,256]{1,0:T(8,128)(2,1)S(1)}, bf16[512,256]{1,0:T(8,128)(2,1)S(1)}, u32[]{:S(2)}, u32[]{:S(2)}) collective-permute-start(bf16[512,256]{1,0:T(8,128)(2,1)S(1)} %collective-permute-done.37.refs_2_), channel_id=1, source_target_pairs={{0,8},{8,0},{16,24},{24,16},{32,40},{40,32},{48,56},{56,48},{64,72... | collective-permute-start | bytes 786440 | tf_op jit(solution)/shard_map/ppermute | solution.py:37
  149.7 5.3 %collective-permute-start.39 = (bf16[256,256]{1,0:T(8,128)(2,1)S(1)}, bf16[256,256]{1,0:T(8,128)(2,1)S(1)}, u32[]{:S(2)}, u32[]{:S(2)}) collective-permute-start(bf16[256,256]{1,0:T(8,128)(2,1)S(1)} %slice.19), channel_id=1, source_target_pairs={{0,8},{8,0},{16,24},{24,16},{32,40},{40,32},{48,56},{56,48},{64,72... | collective-permute-start | bytes 393224 | tf_op jit(solution)/shard_map/ppermute | solution.py:37
  152.3 6.3 %collective-permute-start.36 = (bf16[256,256]{1,0:T(8,128)(2,1)S(1)}, bf16[256,256]{1,0:T(8,128)(2,1)S(1)}, u32[]{:S(2)}, u32[]{:S(2)}) collective-permute-start(bf16[256,256]{1,0:T(8,128)(2,1)S(1)} %slice.18), channel_id=1, source_target_pairs={{0,16},{8,24},{16,32},{24,40},{32,48},{40,56},{48,0},{56,8},{64,80... | collective-permute-start | bytes 393224 | tf_op jit(solution)/shard_map/ppermute | solution.py:37

commit v3 on v2

v3 whole, which is shorter than its diff:
```python
import functools

import jax
import jax.numpy as jnp
from jax import lax
from jax.experimental import pallas as pl
from jax.experimental.pallas import tpu as pltpu
from jax.sharding import PartitionSpec as P

BF16 = jnp.bfloat16
F32 = jnp.float32


def after(array, *deps):
    return lax.optimization_barrier((array, *deps))[0]


def wait_all(arrays, gate):
    return [after(array, *gate) if gate else array for array in arrays]


def z_send(block, step, other=0):
    route = []
    for slab in range(4):
        for z in range(8):
            route.append((slab * 8 + z, (slab ^ other) * 8 + (z + step) % 8))
    return lax.ppermute(block, ("slab", "col"), route)


def row_swap(block, flip, other=0):
    route = []
    for slab in range(4):
        for row in range(8):
            route.append((slab * 8 + row, (slab ^ other) * 8 + (row ^ flip)))
    return lax.ppermute(block, ("slab", "row"), route)


def core_swap(block):
    return row_swap(block, 0, 1)


def gather_row(tile, here, other):
    half = tile.shape[0] // 2
    near = row_swap(tile, 2, other)
    far = row_swap(tile, 6, other)
    side = row_swap(tile, 1, other)
    near_side = row_swap(side, 2)
    across = row_swap(near, 6)
    far_side = row_swap(far, 1)
    top = row_swap(far_side[:half], 2)
    low = row_swap(across[half:], 1)
    return [
        (0, 0, here),
        (1, 0, side),
        (2, 0, near),
        (6, 0, far),
        (3, 0, near_side),
        (4, 0, across),
        (7, 0, far_side),
        (5, 0, top),
        (5, half, low),
    ]


def pair_steps(tile, other, split):
    here = core_swap(tile) if other else tile
    side = row_swap(tile, 1, other)
    gate = yield here, side
    (pair,) = wait_all([jnp.stack([here, side])], gate)
    near = row_swap(pair, 2)
    far = row_swap(pair, 6)
    gate = yield near, far
    near_on, far_on = wait_all((near, far), gate)
    if split:
        across = jnp.stack([row_swap(far_on[0], 2), row_swap(near_on[1], 6)])
    else:
        across = row_swap(far_on, 2)
    yield (across,)
    yield jnp.concatenate([pair, near, across, far], axis=0)


def fold_tiles(steps, beside, order, shots, *refs):
    count = len(steps)
    tiles, refs = refs[:count], refs[count:]
    height = 256
    if beside:
        early, held, out, both = refs
    else:
        (out,) = refs

    @pl.loop(0, out.shape[0] // height)
    def _(chunk):
        rows = pl.ds(pl.multiple_of(chunk * height, height), height)
        total = early[rows, :] if beside else None
        for step, tile in zip(steps, tiles):
            term = jnp.dot(tile[rows, :], shots[order[step]], preferred_element_type=F32)
            total = term if total is None else total + term
        total = total.astype(out.dtype)
        out[rows, :] = total
        if beside:
            both[0, rows, :] = total
            both[1, rows, :] = held[rows, :]


def multiply_tiles(tiles, shots, order, dtype, beside=()):
    steps = tuple(tiles)
    rows, depth = tiles[steps[0]].shape
    columns = shots.shape[2]
    in_vmem = pl.BlockSpec(memory_space=pltpu.VMEM)
    out = jax.ShapeDtypeStruct((rows, columns), dtype)
    pair = jax.ShapeDtypeStruct((2, rows, columns), dtype)
    return pl.pallas_call(
        functools.partial(fold_tiles, steps, len(beside) > 0),
        in_specs=[pl.BlockSpec(memory_space=pltpu.SMEM)]
        + [in_vmem] * (1 + len(steps) + len(beside)),
        out_specs=[in_vmem] * 2 if beside else in_vmem,
        out_shape=[out, pair] if beside else out,
        compiler_params=pltpu.CompilerParams(vmem_limit_bytes=24 << 20),
        cost_estimate=pl.CostEstimate(
            flops=2 * len(steps) * rows * depth * columns,
            bytes_accessed=2 * len(steps) * depth * (rows + columns),
            transcendentals=0,
        ),
    )(order, shots, *tiles.values(), *beside)


def panel_of(tiles):
    count = len(tiles)
    rows, depth = tiles[0].shape

    def kernel(*refs):
        *parts, panel, sems = refs
        copies = []
        for step in range(count):
            copies.append(pltpu.make_async_copy(parts[step], panel.at[step], sems.at[step]))
            copies[-1].start()
        for copy in copies:
            copy.wait()

    return pl.pallas_call(
        kernel,
        in_specs=[pl.BlockSpec(memory_space=pl.ANY)] * count,
        out_specs=pl.BlockSpec(memory_space=pl.ANY),
        out_shape=jax.ShapeDtypeStruct((count, rows, depth), BF16),
        scratch_shapes=[pltpu.SemaphoreType.DMA((count,))],
        compiler_params=pltpu.CompilerParams(vmem_limit_bytes=1 << 20),
    )(*(tiles[step] for step in range(count)))


def fold(pieces, added, order, operator, *refs):
    *shots, out = refs
    height = 256

    @pl.loop(0, out.shape[0] // height)
    def _(chunk):
        rows = pl.ds(pl.multiple_of(chunk * height, height), height)
        total = shots[-1][rows, :] if added else None
        for (place, start), shot in zip(pieces, shots):
            block = shot[0] if len(shot.shape) == 3 else shot[...]
            panel = operator[order[place], rows, start : start + block.shape[0]]
            term = jnp.dot(panel, block, preferred_element_type=F32)
            total = term if total is None else total + term
        if len(shots[0].shape) == 3:
            total = total + shots[0][1, rows, :].astype(F32)
        out[rows, :] = total.astype(out.dtype)


def multiply_some(operator, pieces, order, dtype, added):
    _, rows, _ = operator.shape
    shots = [piece[2] for piece in pieces]
    columns = shots[0].shape[-1]
    depth = sum(shot.shape[-2] for shot in shots)
    in_vmem = pl.BlockSpec(memory_space=pltpu.VMEM)
    return pl.pallas_call(
        functools.partial(fold, [piece[:2] for piece in pieces], len(added) > 0),
        in_specs=[pl.BlockSpec(memory_space=pltpu.SMEM)] + [in_vmem] * (1 + len(shots) + len(added)),
        out_specs=in_vmem,
        out_shape=jax.ShapeDtypeStruct((rows, columns), dtype),
        compiler_params=pltpu.CompilerParams(vmem_limit_bytes=24 << 20),
        cost_estimate=pl.CostEstimate(
            flops=2 * rows * depth * columns,
            bytes_accessed=2 * depth * (rows + columns),
            transcendentals=0,
        ),
    )(order, operator, *shots, *added)


def multiply(operator, pieces, order):
    early = multiply_some(operator, pieces[:7], order, F32, ())
    return multiply_some(operator, pieces[7:], order, BF16, (early,))


def on_device(reflection, transmission, shots):
    own_refl = reflection[0]
    own_trans = transmission[0]
    shot_tile = shots[0]
    row, z = lax.axis_index("row"), lax.axis_index("col")
    place = jnp.arange(8, dtype=jnp.int32)
    by_step = ((row ^ place) - z + 8) % 8
    step_place = row ^ (z + place) % 8

    t_down, t_up, r_down, r_up = {}, {}, {}, {}
    t_here = core_swap(own_trans)
    t_down[1], t_up[1] = z_send(own_trans, -1, 1), z_send(own_trans, 1, 1)
    shot_ring = pair_steps(shot_tile, 1, False)
    gate = (*next(shot_ring), t_here)
    t_down[2] = z_send(after(t_down[1], *gate), -1)
    t_up[2] = z_send(after(t_up[1], *gate), 1)
    gate = next(shot_ring)
    t_down[3] = z_send(after(t_down[2], *gate), -1)
    t_up[3] = z_send(after(t_up[2], *gate), 1)
    gate = next(shot_ring)
    t_down[4] = z_send(after(t_down[3], *gate), -1)
    r_up[1] = z_send(after(own_refl, t_up[3], *gate), 1)
    incoming = after(next(shot_ring), r_up[1])
    tiles = {0: t_here, **t_down, 5: t_up[3], 6: t_up[2], 7: t_up[1]}
    first = multiply_tiles(tiles, incoming, step_place, BF16)
    trans = tiles
    r_down[1] = z_send(after(own_refl, t_down[4]), -1)
    r_up[2] = z_send(r_up[1], 1)
    first_ring = pair_steps(first, 0, True)
    gate = next(first_ring)
    r_down[2] = z_send(after(r_down[1], *gate), -1)
    r_up[3] = z_send(after(r_up[2], *gate), 1)
    first_ring.send((r_down[1], r_up[2]))
    r_down[3] = z_send(r_down[2], -1)
    r_up[4] = z_send(r_up[3], 1)
    first_ring.send((r_down[2], r_up[3]))
    passed = next(first_ring)
    tiles = {0: own_refl, 1: r_down[1], 2: r_down[2], 5: r_up[3], 6: r_up[2], 7: r_up[1]}
    early = multiply_tiles(tiles, passed, step_place, F32)
    late = {3: r_down[3], 4: r_up[4]}
    middle, pair = multiply_tiles(late, passed, step_place, BF16, (early, first))
    refl = panel_of({**tiles, **late})
    summed = multiply(refl, gather_row(middle, core_swap(pair), 1), by_step)
    return multiply(panel_of(trans), gather_row(summed, summed, 0), by_step)[None]


def solution(mesh):
    placed = (P("slab", "row", "col"), P("slab", "row", "col"), P("slab", "row", "col"))
    return jax.shard_map(
        on_device, mesh=mesh, in_specs=placed, out_specs=P("slab", "row", "col"), check_vma=False
    )
```

time: 161 us -> 158 us (0.981); the launches traced: 160 us -> 155 us
  waiting for transfers between devices: 93.2 us -> 78.9 us
  starting transfers between devices: 51.6 us -> 57.9 us
  Pallas kernels: 11.5 us -> 13.6 us
    ppermute x27 -> x28, waiting for transfers between devices: 72.4 us -> 58.3 us  [row_swap(): return lax.ppermute(block, ('slab', 'row'), route)]
    ppermute x27 -> x28, starting transfers between devices: 27.9 us -> 32.1 us  [row_swap(): return lax.ppermute(block, ('slab', 'row'), route)]
    pallas_call x2 -> x5, Pallas kernels: 5.19 us -> 7.24 us  [the longest x3 5.48 us: multiply_tiles(): pl.pallas_call(functools.partial(fold_tiles, steps, len(beside) > 0), in_...]
    ppermute x14, starting transfers between devices: 23.7 us -> 25.8 us  [z_send(): return lax.ppermute(block, ('slab', 'col'), route)]
  transfers between devices with their start and end apart: 41 -> 42, of which waited for: 30 -> 26; matrix products, arithmetic and copies ran while one was open for 2% -> 3% of each run, Pallas kernels for 4% -> 6%
where the time goes in v3:
time: 158 us; the launch traced here: 155 us
  waiting for transfers between devices  78.9 us (50%)
  starting transfers between devices  57.9 us (37%)
  Pallas kernels  13.6 us (9%)
  local copies, waits for them, and re-layouts  4.44 us (3%)
    ppermute x28, waiting for transfers between devices, row_swap(): return lax.ppermute(block, ('slab', 'row'), route)  58.3 us
    ppermute x28, starting transfers between devices, row_swap(): return lax.ppermute(block, ('slab', 'row'), route)  32.1 us
    ppermute x14, starting transfers between devices, z_send(): return lax.ppermute(block, ('slab', 'col'), route)  25.8 us
    ppermute x14, waiting for transfers between devices, z_send(): return lax.ppermute(block, ('slab', 'col'), route)  20.6 us
    pallas_call x4, Pallas kernels, multiply_some(): pl.pallas_call(functools.partial(fold, [piece[:2] for piece in pieces], l...  6.35 us
    pallas_call x3, Pallas kernels, multiply_tiles(): pl.pallas_call(functools.partial(fold_tiles, steps, len(beside) > 0), in_...  5.48 us
    unnamed x12, local copies, waits for them, and re-layouts  3.26 us
  transfers between devices with their start and end apart: 42, of which 26 were waited for; matrix products, arithmetic and copies ran while one was open for 3% of the time, Pallas kernels for 6%

profile of v3, /device:TPU:16, one launch (start us, length us, event | category | flops | bytes accessed | tf_op | source)
XLA Modules:
  0.0 155.1 jit_solution(15581493633295377366)
XLA Ops:
  0.0 2.0 %collective-permute-start.10 = (bf16[512,512]{1,0:T(8,128)(2,1)}, bf16[512,512]{1,0:T(8,128)(2,1)S(1)}, u32[]{:S(2)}, u32[]{:S(2)}) collective-permute-start(bf16[512,512]{1,0:T(8,128)(2,1)} %bitcast.27), channel_id=1, source_target_pairs={{0,65},{1,66},{2,67},{3,68},{4,69},{5,70},{6,71},{7,64},{64,1},{65... | collective-permute-start | bytes 1572872 | tf_op jit(solution)/shard_map/ppermute | solution.py:27
  2.0 4.0 %collective-permute-start.1 = (bf16[512,512]{1,0:T(8,128)(2,1)}, bf16[512,512]{1,0:T(8,128)(2,1)S(1)}, u32[]{:S(2)}, u32[]{:S(2)}) collective-permute-start(bf16[512,512]{1,0:T(8,128)(2,1)} %bitcast.28), channel_id=1, source_target_pairs={{0,71},{1,64},{2,65},{3,66},{4,67},{5,68},{6,69},{7,70},{64,7},{65... | collective-permute-start | bytes 1572872 | tf_op jit(solution)/shard_map/ppermute | solution.py:27
  6.1 1.3 collective-permute-start.3
  7.7 6.6 %collective-permute-done.3 = bf16[512,256]{1,0:T(8,128)(2,1)S(1)} collective-permute-done((bf16[512,256]{1,0:T(8,128)(2,1)}, bf16[512,256]{1,0:T(8,128)(2,1)S(1)}, u32[]{:S(2)}, u32[]{:S(2)}) %collective-permute-start.3) | collective-permute-done | bytes 262176 | tf_op jit(solution)/shard_map/ppermute | solution.py:35
  14.4 2.8 %collective-permute-start.6 = (bf16[2,512,256]{2,1,0:T(8,128)(2,1)S(1)}, bf16[2,512,256]{2,1,0:T(8,128)(2,1)}, u32[]{:S(2)}, u32[]{:S(2)}) collective-permute-start(bf16[2,512,256]{2,1,0:T(8,128)(2,1)S(1)} %pad_maximum_fusion), channel_id=1, source_target_pairs={{0,48},{8,56},{16,32},{24,40},{32,16},{40,24},{48,0},{56,8},{64,11... | collective-permute-start | bytes 1572872 | tf_op jit(solution)/shard_map/ppermute | solution.py:35
  18.5 3.2 %collective-permute-start.4 = (bf16[512,512]{1,0:T(8,128)(2,1)S(1)}, bf16[512,512]{1,0:T(8,128)(2,1)S(1)}, u32[]{:S(2)}, u32[]{:S(2)}) collective-permute-start(bf16[512,512]{1,0:T(8,128)(2,1)S(1)} %collective-permute-done.1.refs_1_), channel_id=1, source_target_pairs={{0,7},{1,0},{2,1},{3,2},{4,3},{5,4},{6,5},{7,6},{64,71},{65,64},{6... | collective-permute-start | bytes 1572872 | tf_op jit(solution)/shard_map/ppermute | solution.py:27
  21.7 8.6 %collective-permute-done.6 = bf16[2,512,256]{2,1,0:T(8,128)(2,1)} collective-permute-done((bf16[2,512,256]{2,1,0:T(8,128)(2,1)S(1)}, bf16[2,512,256]{2,1,0:T(8,128)(2,1)}, u32[]{:S(2)}, u32[]{:S(2)}) %collective-permute-start.6) | collective-permute-done | bytes 524320 | tf_op jit(solution)/shard_map/ppermute | solution.py:35
  31.6 2.1 %collective-permute-done.11.refs_6_ = bf16[512,512]{1,0:T(8,128)(2,1)S(1)} collective-permute-done((bf16[512,512]{1,0:T(8,128)(2,1)S(1)}, bf16[512,512]{1,0:T(8,128)(2,1)S(1)}, u32[]{:S(2)}, u32[]{:S(2)}) %collective-permute-start.11) | collective-permute-done | bytes 524320 | tf_op jit(solution)/shard_map/ppermute | solution.py:27
  33.6 3.2 %collective-permute-start.7 = (bf16[512,512]{1,0:T(8,128)(2,1)S(1)}, bf16[512,512]{1,0:T(8,128)(2,1)}, u32[]{:S(2)}, u32[]{:S(2)}) collective-permute-start(bf16[512,512]{1,0:T(8,128)(2,1)S(1)} %collective-permute-done.4.refs_2_), channel_id=1, source_target_pairs={{0,7},{1,0},{2,1},{3,2},{4,3},{5,4},{6,5},{7,6},{64,71},{65,64},{6... | collective-permute-start | bytes 1572872 | tf_op jit(solution)/shard_map/ppermute | solution.py:27
  36.9 7.4 %collective-permute-done.8 = bf16[2,512,256]{2,1,0:T(8,128)(2,1)} collective-permute-done((bf16[2,512,256]{2,1,0:T(8,128)(2,1)}, bf16[2,512,256]{2,1,0:T(8,128)(2,1)}, u32[]{:S(2)}, u32[]{:S(2)}) %collective-permute-start.8) | collective-permute-done | bytes 524320 | tf_op jit(solution)/shard_map/ppermute | solution.py:35
  44.3 3.8 %collective-permute-done.12.refs_5_ = bf16[512,512]{1,0:T(8,128)(2,1)} collective-permute-done((bf16[512,512]{1,0:T(8,128)(2,1)S(1)}, bf16[512,512]{1,0:T(8,128)(2,1)}, u32[]{:S(2)}, u32[]{:S(2)}) %collective-permute-start.12) | collective-permute-done | bytes 524320 | tf_op jit(solution)/shard_map/ppermute | solution.py:27
  48.1 3.2 %collective-permute-start.9 = (bf16[512,512]{1,0:T(8,128)(2,1)}, bf16[512,512]{1,0:T(8,128)(2,1)S(1)}, u32[]{:S(2)}, u32[]{:S(2)}) collective-permute-start(bf16[512,512]{1,0:T(8,128)(2,1)} %collective-permute-done.7.refs_3_), channel_id=1, source_target_pairs={{0,7},{1,0},{2,1},{3,2},{4,3},{5,4},{6,5},{7,6},{64,71},{65,64},{6... | collective-permute-start | bytes 1572872 | tf_op jit(solution)/shard_map/ppermute | solution.py:27
  54.5 6.6 %collective-permute-done.9.refs_4_ = bf16[512,512]{1,0:T(8,128)(2,1)S(1)} collective-permute-done((bf16[512,512]{1,0:T(8,128)(2,1)}, bf16[512,512]{1,0:T(8,128)(2,1)S(1)}, u32[]{:S(2)}, u32[]{:S(2)}) %collective-permute-start.9) | collective-permute-done | bytes 524320 | tf_op jit(solution)/shard_map/ppermute | solution.py:27
  61.0 3.6 %collective-permute-start.13 = (bf16[512,512]{1,0:T(8,128)(2,1)S(1)}, bf16[512,512]{1,0:T(8,128)(2,1)S(1)}, u32[]{:S(2)}, u32[]{:S(2)}) collective-permute-start(bf16[512,512]{1,0:T(8,128)(2,1)S(1)} %bitcast.20), channel_id=1, source_target_pairs={{0,7},{1,0},{2,1},{3,2},{4,3},{5,4},{6,5},{7,6},{64,71},{65,64},{6... | collective-permute-start | bytes 1572872 | tf_op jit(solution)/shard_map/ppermute | solution.py:27
  65.7 2.6 %shard_map.38.refs_3_ = bf16[512,256]{1,0:T(8,128)(2,1)S(1)} custom-call(s32[8]{0:T(128)S(1)} %fusion.order, bf16[8,512,256]{2,1,0:T(8,128)(2,1)S(1)} %constant_dynamic-update-slice_fusion.shots, bf16[512,512]{1,0:T(8,128)(2,1)S(1)} %collective-permute-done.refs_0_, bf16[512,512]{1,0:T(8,128)(2,1)S(1)} %collective-permute-done.1.refs_1_, ...), custom_call_target="tpu_custom_call" | custom-call | flops 1073741824 | bytes 6291456 | tf_op jit(solution)/shard_map/pallas_call | solution.py:112
  68.4 1.6 collective-permute-start.15
  69.9 5.1 %collective-permute-done.15 = bf16[512,256]{1,0:T(8,128)(2,1)S(1)} collective-permute-done((bf16[512,256]{1,0:T(8,128)(2,1)S(1)}, bf16[512,256]{1,0:T(8,128)(2,1)S(1)}, u32[]{:S(2)}, u32[]{:S(2)}) %collective-permute-start.15) | collective-permute-done | bytes 262176 | tf_op jit(solution)/shard_map/ppermute | solution.py:35
  75.1 1.5 collective-permute-done.18.refs_6_.refs_4_
  76.6 1.5 collective-permute-start.21
  78.1 3.2 %collective-permute-start.16 = (bf16[512,512]{1,0:T(8,128)(2,1)S(1)}, bf16[512,512]{1,0:T(8,128)(2,1)S(1)}, u32[]{:S(2)}, u32[]{:S(2)}) collective-permute-start(bf16[512,512]{1,0:T(8,128)(2,1)S(1)} %collective-permute-done.13.refs_1_), channel_id=1, source_target_pairs={{0,7},{1,0},{2,1},{3,2},{4,3},{5,4},{6,5},{7,6},{64,71},{65,64},{6... | collective-permute-start | bytes 1572872 | tf_op jit(solution)/shard_map/ppermute | solution.py:27
  81.3 2.1 %collective-permute-start.22 = (bf16[2,512,256]{2,1,0:T(8,128)(2,1)S(1)}, bf16[2,512,256]{2,1,0:T(8,128)(2,1)S(1)}, u32[]{:S(2)}, u32[]{:S(2)}) collective-permute-start(bf16[2,512,256]{2,1,0:T(8,128)(2,1)S(1)} %pad_maximum_fusion.1), channel_id=1, source_target_pairs={{0,48},{8,56},{16,32},{24,40},{32,16},{40,24},{48,0},{56,8},{64,11... | collective-permute-start | bytes 1572872 | tf_op jit(solution)/shard_map/ppermute | solution.py:35
  83.4 2.9 %collective-permute-done.21 = bf16[2,512,256]{2,1,0:T(8,128)(2,1)S(1)} collective-permute-done((bf16[2,512,256]{2,1,0:T(8,128)(2,1)S(1)}, bf16[2,512,256]{2,1,0:T(8,128)(2,1)S(1)}, u32[]{:S(2)}, u32[]{:S(2)}) %collective-permute-start.21) | collective-permute-done | bytes 524320 | tf_op jit(solution)/shard_map/ppermute | solution.py:35
  86.3 2.4 %collective-permute-done.19.refs_5_.refs_3_ = bf16[512,512]{1,0:T(8,128)(2,1)S(1)} collective-permute-done((bf16[512,512]{1,0:T(8,128)(2,1)S(1)}, bf16[512,512]{1,0:T(8,128)(2,1)S(1)}, u32[]{:S(2)}, u32[]{:S(2)}) %collective-permute-start.19) | collective-permute-done | bytes 524320 | tf_op jit(solution)/shard_map/ppermute | solution.py:27
  88.8 4.5 %collective-permute-done.22 = bf16[2,512,256]{2,1,0:T(8,128)(2,1)S(1)} collective-permute-done((bf16[2,512,256]{2,1,0:T(8,128)(2,1)S(1)}, bf16[2,512,256]{2,1,0:T(8,128)(2,1)S(1)}, u32[]{:S(2)}, u32[]{:S(2)}) %collective-permute-start.22) | collective-permute-done | bytes 524320 | tf_op jit(solution)/shard_map/ppermute | solution.py:35
  93.5 2.2 %collective-permute-start.24 = (bf16[512,256]{1,0:T(8,128)(2,1)S(1)}, bf16[512,256]{1,0:T(8,128)(2,1)S(1)}, u32[]{:S(2)}, u32[]{:S(2)}) collective-permute-start(bf16[512,256]{1,0:T(8,128)(2,1)S(1)} %slice_bitcast_fusion), channel_id=1, source_target_pairs={{0,48},{8,56},{16,32},{24,40},{32,16},{40,24},{48,0},{56,8},{64,11... | collective-permute-start | bytes 786440 | tf_op jit(solution)/shard_map/ppermute | solution.py:35
  95.6 3.2 %collective-permute-start.17 = (bf16[512,512]{1,0:T(8,128)(2,1)S(1)}, bf16[512,512]{1,0:T(8,128)(2,1)S(1)}, u32[]{:S(2)}, u32[]{:S(2)}) collective-permute-start(bf16[512,512]{1,0:T(8,128)(2,1)S(1)} %collective-permute-done.16.refs_2_), channel_id=1, source_target_pairs={{0,7},{1,0},{2,1},{3,2},{4,3},{5,4},{6,5},{7,6},{64,71},{65,64},{6... | collective-permute-start | bytes 1572872 | tf_op jit(solution)/shard_map/ppermute | solution.py:27
  99.8 1.3 collective-permute-done.24
  101.2 1.7 %shard_map.40.refs_2_ = f32[512,256]{1,0:T(8,128)S(1)} custom-call(s32[8]{0:T(128)S(1)} %fusion.order, bf16[8,512,256]{2,1,0:T(8,128)(2,1)S(1)} %constant_dynamic-update-slice_fusion.5.shots, bf16[512,512]{1,0:T(8,128)(2,1)S(1)} %bitcast.21, bf16[512,512]{1,0:T(8,128)(2,1)S(1)} %collective-permute-done.13.refs_1_, ...), custom_call_target="tpu_custom_call" | custom-call | flops 805306368 | bytes 4718592 | tf_op jit(solution)/shard_map/pallas_call | solution.py:112
  102.9 3.1 %collective-permute-done.20.refs_4_.refs_1_ = bf16[512,512]{1,0:T(8,128)(2,1)S(1)} collective-permute-done((bf16[512,512]{1,0:T(8,128)(2,1)S(1)}, bf16[512,512]{1,0:T(8,128)(2,1)S(1)}, u32[]{:S(2)}, u32[]{:S(2)}) %collective-permute-start.20) | collective-permute-done | bytes 524320 | tf_op jit(solution)/shard_map/ppermute | solution.py:27
  106.0 1.2 shard_map.41
  107.3 1.6 %collective-permute-start.28 = (bf16[512,256]{1,0:T(8,128)(2,1)S(1)}, bf16[512,256]{1,0:T(8,128)(2,1)S(1)}, u32[]{:S(2)}, u32[]{:S(2)}) collective-permute-start(bf16[512,256]{1,0:T(8,128)(2,1)S(1)} %get-tuple-element.33), channel_id=1, source_target_pairs={{0,80},{8,88},{16,64},{24,72},{32,112},{40,120},{48,96},{56,104},{... | collective-permute-start | bytes 786440 | tf_op jit(solution)/shard_map/ppermute | solution.py:35
  110.3 5.2 %collective-permute-done.25.refs_3_ = bf16[512,256]{1,0:T(8,128)(2,1)S(1)} collective-permute-done((bf16[512,256]{1,0:T(8,128)(2,1)S(1)}, bf16[512,256]{1,0:T(8,128)(2,1)S(1)}, u32[]{:S(2)}, u32[]{:S(2)}) %collective-permute-start.25) | collective-permute-done | bytes 262176 | tf_op jit(solution)/shard_map/ppermute | solution.py:35
  115.6 1.3 collective-permute-start.26
  116.9 2.1 %collective-permute-start.29 = (bf16[512,256]{1,0:T(8,128)(2,1)S(1)}, bf16[512,256]{1,0:T(8,128)(2,1)S(1)}, u32[]{:S(2)}, u32[]{:S(2)}) collective-permute-start(bf16[512,256]{1,0:T(8,128)(2,1)S(1)} %collective-permute-done.28.refs_2_), channel_id=1, source_target_pairs={{0,48},{8,56},{16,32},{24,40},{32,16},{40,24},{48,0},{56,8},{64,11... | collective-permute-start | bytes 786440 | tf_op jit(solution)/shard_map/ppermute | solution.py:35
  119.1 4.1 %collective-permute-done.26.refs_6_ = bf16[512,256]{1,0:T(8,128)(2,1)S(1)} collective-permute-done((bf16[512,256]{1,0:T(8,128)(2,1)S(1)}, bf16[512,256]{1,0:T(8,128)(2,1)S(1)}, u32[]{:S(2)}, u32[]{:S(2)}) %collective-permute-start.26) | collective-permute-done | bytes 262176 | tf_op jit(solution)/shard_map/ppermute | solution.py:35
  124.3 1.2 collective-permute-done.29.refs_5_
  125.5 1.4 collective-permute-start.30
  127.6 1.8 %shard_map.42.refs_2_ = f32[512,256]{1,0:T(8,128)S(1)} custom-call(s32[8]{0:T(128)S(1)} %and_select_fusion.1.order, bf16[8,512,512]{2,1,0:T(8,128)(2,1)S(1)} %shard_map.39.operator, bf16[2,512,256]{2,1,0:T(8,128)(2,1)S(1)} %collective-permute-done.31.refs_0_, bf16[512,256]{1,0:T(8,128)(2,1)S(1)} %collective-permute-done.32.refs_1_, ...), custom_call_target="tpu_custom_call" | custom-call | flops 939524096 | bytes 5505024 | tf_op jit(solution)/shard_map/pallas_call | solution.py:174
  131.6 2.5 %collective-permute-start.34 = (bf16[512,256]{1,0:T(8,128)(2,1)S(1)}, bf16[512,256]{1,0:T(8,128)(2,1)S(1)}, u32[]{:S(2)}, u32[]{:S(2)}) collective-permute-start(bf16[512,256]{1,0:T(8,128)(2,1)S(1)} %shard_map.43.refs_0_), channel_id=1, source_target_pairs={{0,48},{8,56},{16,32},{24,40},{32,16},{40,24},{48,0},{56,8},{64,11... | collective-permute-start | bytes 786440 | tf_op jit(solution)/shard_map/ppermute | solution.py:35
  135.1 4.4 %collective-permute-done.34.refs_3_ = bf16[512,256]{1,0:T(8,128)(2,1)S(1)} collective-permute-done((bf16[512,256]{1,0:T(8,128)(2,1)S(1)}, bf16[512,256]{1,0:T(8,128)(2,1)S(1)}, u32[]{:S(2)}, u32[]{:S(2)}) %collective-permute-start.34) | collective-permute-done | bytes 262176 | tf_op jit(solution)/shard_map/ppermute | solution.py:35
  139.5 1.3 collective-permute-start.35
  140.8 1.9 %collective-permute-start.38 = (bf16[512,256]{1,0:T(8,128)(2,1)S(1)}, bf16[512,256]{1,0:T(8,128)(2,1)S(1)}, u32[]{:S(2)}, u32[]{:S(2)}) collective-permute-start(bf16[512,256]{1,0:T(8,128)(2,1)S(1)} %collective-permute-done.37.refs_2_), channel_id=1, source_target_pairs={{0,48},{8,56},{16,32},{24,40},{32,16},{40,24},{48,0},{56,8},{64,11... | collective-permute-start | bytes 786440 | tf_op jit(solution)/shard_map/ppermute | solution.py:35
  142.7 1.9 %collective-permute-start.41 = (bf16[512,256]{1,0:T(8,128)(2,1)S(1)}, bf16[512,256]{1,0:T(8,128)(2,1)S(1)}, u32[]{:S(2)}, u32[]{:S(2)}) collective-permute-start(bf16[512,256]{1,0:T(8,128)(2,1)S(1)} %collective-permute-done.40.refs_1_), channel_id=1, source_target_pairs={{0,16},{8,24},{16,0},{24,8},{32,48},{40,56},{48,32},{56,40},{64,80... | collective-permute-start | bytes 786440 | tf_op jit(solution)/shard_map/ppermute | solution.py:35
  144.6 1.5 collective-permute-done.35.refs_6_
  146.1 1.4 collective-permute-start.36
  149.3 1.4 shard_map.37.operator
  150.7 1.8 %shard_map.44.refs_2_ = f32[512,256]{1,0:T(8,128)S(1)} custom-call(s32[8]{0:T(128)S(1)} %and_select_fusion.1.order, bf16[8,512,512]{2,1,0:T(8,128)(2,1)S(1)} %shard_map.37.operator, bf16[512,256]{1,0:T(8,128)(2,1)S(1)} %shard_map.43.refs_0_, bf16[512,256]{1,0:T(8,128)(2,1)S(1)} %collective-permute-done.40.refs_1_, ...), custom_call_target="tpu_custom_call" | custom-call | flops 939524096 | bytes 5505024 | tf_op jit(solution)/shard_map/pallas_call | solution.py:174
  153.4 1.7 %shard_map.45 = bf16[512,256]{1,0:T(8,128)(2,1)} custom-call(s32[8]{0:T(128)S(1)} %and_select_fusion.1.order, bf16[8,512,512]{2,1,0:T(8,128)(2,1)S(1)} %shard_map.37.operator, bf16[256,256]{1,0:T(8,128)(2,1)S(1)} %collective-permute-done.36.refs_0_, bf16[256,256]{1,0:T(8,128)(2,1)S(1)} %collective-permute-done.39.refs_1_, f32[512,256]{1,0:T(8,128)S(1)} %shard_map.44.refs_2_), custom_call_target="tpu_custom_call" | custom-call | flops 134217728 | bytes 786432 | tf_op jit(solution)/shard_map/pallas_call | solution.py:174
  (69 shorter events, 17.8 us)
Async XLA Ops:
  0.0 17.4 %collective-permute-start = (bf16[512,512]{1,0:T(8,128)(2,1)}, bf16[512,512]{1,0:T(8,128)(2,1)S(1)}, u32[]{:S(2)}, u32[]{:S(2)}) collective-permute-start(bf16[512,512]{1,0:T(8,128)(2,1)} %bitcast.26), channel_id=1, source_target_pairs={{0,64},{8,72},{16,80},{24,88},{32,96},{40,104},{48,112},{56,120},{... | collective-permute-start | bytes 1572872 | tf_op jit(solution)/shard_map/ppermute | solution.py:35
  0.0 18.5 %collective-permute-start.10 = (bf16[512,512]{1,0:T(8,128)(2,1)}, bf16[512,512]{1,0:T(8,128)(2,1)S(1)}, u32[]{:S(2)}, u32[]{:S(2)}) collective-permute-start(bf16[512,512]{1,0:T(8,128)(2,1)} %bitcast.27), channel_id=1, source_target_pairs={{0,65},{1,66},{2,67},{3,68},{4,69},{5,70},{6,71},{7,64},{64,1},{65... | collective-permute-start | bytes 1572872 | tf_op jit(solution)/shard_map/ppermute | solution.py:27
  2.0 16.4 %collective-permute-start.1 = (bf16[512,512]{1,0:T(8,128)(2,1)}, bf16[512,512]{1,0:T(8,128)(2,1)S(1)}, u32[]{:S(2)}, u32[]{:S(2)}) collective-permute-start(bf16[512,512]{1,0:T(8,128)(2,1)} %bitcast.28), channel_id=1, source_target_pairs={{0,71},{1,64},{2,65},{3,66},{4,67},{5,68},{6,69},{7,70},{64,7},{65... | collective-permute-start | bytes 1572872 | tf_op jit(solution)/shard_map/ppermute | solution.py:27
  6.0 1.7 %collective-permute-start.2 = (bf16[512,256]{1,0:T(8,128)(2,1)}, bf16[512,256]{1,0:T(8,128)(2,1)S(1)}, u32[]{:S(2)}, u32[]{:S(2)}) collective-permute-start(bf16[512,256]{1,0:T(8,128)(2,1)} %bitcast.29), channel_id=1, source_target_pairs={{0,64},{8,72},{16,80},{24,88},{32,96},{40,104},{48,112},{56,120},{... | collective-permute-start | bytes 786440 | tf_op jit(solution)/shard_map/ppermute | solution.py:35
  6.1 8.2 %collective-permute-start.3 = (bf16[512,256]{1,0:T(8,128)(2,1)}, bf16[512,256]{1,0:T(8,128)(2,1)S(1)}, u32[]{:S(2)}, u32[]{:S(2)}) collective-permute-start(bf16[512,256]{1,0:T(8,128)(2,1)} %bitcast.30), channel_id=1, source_target_pairs={{0,72},{8,64},{16,88},{24,80},{32,104},{40,96},{48,120},{56,112},{... | collective-permute-start | bytes 786440 | tf_op jit(solution)/shard_map/ppermute | solution.py:35
  14.3 3.1 %copy-start.1 = (bf16[512,256]{1,0:T(8,128)(2,1)}, bf16[512,256]{1,0:T(8,128)(2,1)S(1)}, u32[]{:S(2)}) copy-start(bf16[512,256]{1,0:T(8,128)(2,1)S(1)} %collective-permute-done.3) | copy-start | bytes 786436
  14.3 46.7 %copy-start = (bf16[1,512,512]{2,1,0:T(8,128)(2,1)S(1)}, bf16[1,512,512]{2,1,0:T(8,128)(2,1)}, u32[]{:S(2)}) copy-start(bf16[1,512,512]{2,1,0:T(8,128)(2,1)} %param.3) | copy-start | bytes 1572868
  14.4 15.9 %collective-permute-start.6 = (bf16[2,512,256]{2,1,0:T(8,128)(2,1)S(1)}, bf16[2,512,256]{2,1,0:T(8,128)(2,1)}, u32[]{:S(2)}, u32[]{:S(2)}) collective-permute-start(bf16[2,512,256]{2,1,0:T(8,128)(2,1)S(1)} %pad_maximum_fusion), channel_id=1, source_target_pairs={{0,48},{8,56},{16,32},{24,40},{32,16},{40,24},{48,0},{56,8},{64,11... | collective-permute-start | bytes 1572872 | tf_op jit(solution)/shard_map/ppermute | solution.py:35
  17.2 14.4 %collective-permute-start.5 = (bf16[2,512,256]{2,1,0:T(8,128)(2,1)S(1)}, bf16[2,512,256]{2,1,0:T(8,128)(2,1)}, u32[]{:S(2)}, u32[]{:S(2)}) collective-permute-start(bf16[2,512,256]{2,1,0:T(8,128)(2,1)S(1)} %pad_maximum_fusion), channel_id=1, source_target_pairs={{0,16},{8,24},{16,0},{24,8},{32,48},{40,56},{48,32},{56,40},{64,80... | collective-permute-start | bytes 1572872 | tf_op jit(solution)/shard_map/ppermute | solution.py:35
  18.5 15.2 %collective-permute-start.11 = (bf16[512,512]{1,0:T(8,128)(2,1)S(1)}, bf16[512,512]{1,0:T(8,128)(2,1)S(1)}, u32[]{:S(2)}, u32[]{:S(2)}) collective-permute-start(bf16[512,512]{1,0:T(8,128)(2,1)S(1)} %collective-permute-done.10.refs_7_), channel_id=1, source_target_pairs={{0,1},{1,2},{2,3},{3,4},{4,5},{5,6},{6,7},{7,0},{64,65},{65,66},{6... | collective-permute-start | bytes 1572872 | tf_op jit(solution)/shard_map/ppermute | solution.py:27
  18.5 15.2 %collective-permute-start.4 = (bf16[512,512]{1,0:T(8,128)(2,1)S(1)}, bf16[512,512]{1,0:T(8,128)(2,1)S(1)}, u32[]{:S(2)}, u32[]{:S(2)}) collective-permute-start(bf16[512,512]{1,0:T(8,128)(2,1)S(1)} %collective-permute-done.1.refs_1_), channel_id=1, source_target_pairs={{0,7},{1,0},{2,1},{3,2},{4,3},{5,4},{6,5},{7,6},{64,71},{65,64},{6... | collective-permute-start | bytes 1572872 | tf_op jit(solution)/shard_map/ppermute | solution.py:27
  30.3 14.0 %collective-permute-start.8 = (bf16[2,512,256]{2,1,0:T(8,128)(2,1)}, bf16[2,512,256]{2,1,0:T(8,128)(2,1)}, u32[]{:S(2)}, u32[]{:S(2)}) collective-permute-start(bf16[2,512,256]{2,1,0:T(8,128)(2,1)} %collective-permute-done.6), channel_id=1, source_target_pairs={{0,16},{8,24},{16,0},{24,8},{32,48},{40,56},{48,32},{56,40},{64,80... | collective-permute-start | bytes 1572872 | tf_op jit(solution)/shard_map/ppermute | solution.py:35
  33.6 14.4 %collective-permute-start.12 = (bf16[512,512]{1,0:T(8,128)(2,1)S(1)}, bf16[512,512]{1,0:T(8,128)(2,1)}, u32[]{:S(2)}, u32[]{:S(2)}) collective-permute-start(bf16[512,512]{1,0:T(8,128)(2,1)S(1)} %collective-permute-done.11.refs_6_), channel_id=1, source_target_pairs={{0,1},{1,2},{2,3},{3,4},{4,5},{5,6},{6,7},{7,0},{64,65},{65,66},{6... | collective-permute-start | bytes 1572872 | tf_op jit(solution)/shard_map/ppermute | solution.py:27
  33.6 14.4 %collective-permute-start.7 = (bf16[512,512]{1,0:T(8,128)(2,1)S(1)}, bf16[512,512]{1,0:T(8,128)(2,1)}, u32[]{:S(2)}, u32[]{:S(2)}) collective-permute-start(bf16[512,512]{1,0:T(8,128)(2,1)S(1)} %collective-permute-done.4.refs_2_), channel_id=1, source_target_pairs={{0,7},{1,0},{2,1},{3,2},{4,3},{5,4},{6,5},{7,6},{64,71},{65,64},{6... | collective-permute-start | bytes 1572872 | tf_op jit(solution)/shard_map/ppermute | solution.py:27
  48.1 16.6 %collective-permute-start.14 = (bf16[512,512]{1,0:T(8,128)(2,1)}, bf16[512,512]{1,0:T(8,128)(2,1)S(1)}, u32[]{:S(2)}, u32[]{:S(2)}) collective-permute-start(bf16[512,512]{1,0:T(8,128)(2,1)} %bitcast.19), channel_id=1, source_target_pairs={{0,1},{1,2},{2,3},{3,4},{4,5},{5,6},{6,7},{7,0},{64,65},{65,66},{6... | collective-permute-start | bytes 1572872 | tf_op jit(solution)/shard_map/ppermute | solution.py:27
  48.1 13.0 %collective-permute-start.9 = (bf16[512,512]{1,0:T(8,128)(2,1)}, bf16[512,512]{1,0:T(8,128)(2,1)S(1)}, u32[]{:S(2)}, u32[]{:S(2)}) collective-permute-start(bf16[512,512]{1,0:T(8,128)(2,1)} %collective-permute-done.7.refs_3_), channel_id=1, source_target_pairs={{0,7},{1,0},{2,1},{3,2},{4,3},{5,4},{6,5},{7,6},{64,71},{65,64},{6... | collective-permute-start | bytes 1572872 | tf_op jit(solution)/shard_map/ppermute | solution.py:27
  61.0 15.5 %collective-permute-start.13 = (bf16[512,512]{1,0:T(8,128)(2,1)S(1)}, bf16[512,512]{1,0:T(8,128)(2,1)S(1)}, u32[]{:S(2)}, u32[]{:S(2)}) collective-permute-start(bf16[512,512]{1,0:T(8,128)(2,1)S(1)} %bitcast.20), channel_id=1, source_target_pairs={{0,7},{1,0},{2,1},{3,2},{4,3},{5,4},{6,5},{7,6},{64,71},{65,64},{6... | collective-permute-start | bytes 1572872 | tf_op jit(solution)/shard_map/ppermute | solution.py:27
  64.6 11.9 %collective-permute-start.18 = (bf16[512,512]{1,0:T(8,128)(2,1)S(1)}, bf16[512,512]{1,0:T(8,128)(2,1)S(1)}, u32[]{:S(2)}, u32[]{:S(2)}) collective-permute-start(bf16[512,512]{1,0:T(8,128)(2,1)S(1)} %collective-permute-done.14.refs_7_.refs_5_), channel_id=1, source_target_pairs={{0,1},{1,2},{2,3},{3,4},{4,5},{5,6},{6,7},{7,0},{64,65},{65,66},{6... | collective-permute-start | bytes 1572872 | tf_op jit(solution)/shard_map/ppermute | solution.py:27
  68.4 6.6 %collective-permute-start.15 = (bf16[512,256]{1,0:T(8,128)(2,1)S(1)}, bf16[512,256]{1,0:T(8,128)(2,1)S(1)}, u32[]{:S(2)}, u32[]{:S(2)}) collective-permute-start(bf16[512,256]{1,0:T(8,128)(2,1)S(1)} %shard_map.38.refs_3_), channel_id=1, source_target_pairs={{0,8},{8,0},{16,24},{24,16},{32,40},{40,32},{48,56},{56,48},{64,72... | collective-permute-start | bytes 786440 | tf_op jit(solution)/shard_map/ppermute | solution.py:35
  76.6 9.8 %collective-permute-start.21 = (bf16[2,512,256]{2,1,0:T(8,128)(2,1)S(1)}, bf16[2,512,256]{2,1,0:T(8,128)(2,1)S(1)}, u32[]{:S(2)}, u32[]{:S(2)}) collective-permute-start(bf16[2,512,256]{2,1,0:T(8,128)(2,1)S(1)} %pad_maximum_fusion.1), channel_id=1, source_target_pairs={{0,16},{8,24},{16,0},{24,8},{32,48},{40,56},{48,32},{56,40},{64,80... | collective-permute-start | bytes 1572872 | tf_op jit(solution)/shard_map/ppermute | solution.py:35
  78.1 10.7 %collective-permute-start.19 = (bf16[512,512]{1,0:T(8,128)(2,1)S(1)}, bf16[512,512]{1,0:T(8,128)(2,1)S(1)}, u32[]{:S(2)}, u32[]{:S(2)}) collective-permute-start(bf16[512,512]{1,0:T(8,128)(2,1)S(1)} %collective-permute-done.18.refs_6_.refs_4_), channel_id=1, source_target_pairs={{0,1},{1,2},{2,3},{3,4},{4,5},{5,6},{6,7},{7,0},{64,65},{65,66},{6... | collective-permute-start | bytes 1572872 | tf_op jit(solution)/shard_map/ppermute | solution.py:27
  78.1 10.7 %collective-permute-start.16 = (bf16[512,512]{1,0:T(8,128)(2,1)S(1)}, bf16[512,512]{1,0:T(8,128)(2,1)S(1)}, u32[]{:S(2)}, u32[]{:S(2)}) collective-permute-start(bf16[512,512]{1,0:T(8,128)(2,1)S(1)} %collective-permute-done.13.refs_1_), channel_id=1, source_target_pairs={{0,7},{1,0},{2,1},{3,2},{4,3},{5,4},{6,5},{7,6},{64,71},{65,64},{6... | collective-permute-start | bytes 1572872 | tf_op jit(solution)/shard_map/ppermute | solution.py:27
  81.3 12.0 %collective-permute-start.22 = (bf16[2,512,256]{2,1,0:T(8,128)(2,1)S(1)}, bf16[2,512,256]{2,1,0:T(8,128)(2,1)S(1)}, u32[]{:S(2)}, u32[]{:S(2)}) collective-permute-start(bf16[2,512,256]{2,1,0:T(8,128)(2,1)S(1)} %pad_maximum_fusion.1), channel_id=1, source_target_pairs={{0,48},{8,56},{16,32},{24,40},{32,16},{40,24},{48,0},{56,8},{64,11... | collective-permute-start | bytes 1572872 | tf_op jit(solution)/shard_map/ppermute | solution.py:35
  93.3 6.5 %collective-permute-start.23 = (bf16[512,256]{1,0:T(8,128)(2,1)S(1)}, bf16[512,256]{1,0:T(8,128)(2,1)S(1)}, u32[]{:S(2)}, u32[]{:S(2)}) collective-permute-start(bf16[512,256]{1,0:T(8,128)(2,1)S(1)} %slice_bitcast_fusion.1), channel_id=1, source_target_pairs={{0,16},{8,24},{16,0},{24,8},{32,48},{40,56},{48,32},{56,40},{64,80... | collective-permute-start | bytes 786440 | tf_op jit(solution)/shard_map/ppermute | solution.py:35
  93.5 7.7 %collective-permute-start.24 = (bf16[512,256]{1,0:T(8,128)(2,1)S(1)}, bf16[512,256]{1,0:T(8,128)(2,1)S(1)}, u32[]{:S(2)}, u32[]{:S(2)}) collective-permute-start(bf16[512,256]{1,0:T(8,128)(2,1)S(1)} %slice_bitcast_fusion), channel_id=1, source_target_pairs={{0,48},{8,56},{16,32},{24,40},{32,16},{40,24},{48,0},{56,8},{64,11... | collective-permute-start | bytes 786440 | tf_op jit(solution)/shard_map/ppermute | solution.py:35
  95.6 10.4 %collective-permute-start.20 = (bf16[512,512]{1,0:T(8,128)(2,1)S(1)}, bf16[512,512]{1,0:T(8,128)(2,1)S(1)}, u32[]{:S(2)}, u32[]{:S(2)}) collective-permute-start(bf16[512,512]{1,0:T(8,128)(2,1)S(1)} %collective-permute-done.19.refs_5_.refs_3_), channel_id=1, source_target_pairs={{0,1},{1,2},{2,3},{3,4},{4,5},{5,6},{6,7},{7,0},{64,65},{65,66},{6... | collective-permute-start | bytes 1572872 | tf_op jit(solution)/shard_map/ppermute | solution.py:27
  95.6 10.4 %collective-permute-start.17 = (bf16[512,512]{1,0:T(8,128)(2,1)S(1)}, bf16[512,512]{1,0:T(8,128)(2,1)S(1)}, u32[]{:S(2)}, u32[]{:S(2)}) collective-permute-start(bf16[512,512]{1,0:T(8,128)(2,1)S(1)} %collective-permute-done.16.refs_2_), channel_id=1, source_target_pairs={{0,7},{1,0},{2,1},{3,2},{4,3},{5,4},{6,5},{7,6},{64,71},{65,64},{6... | collective-permute-start | bytes 1572872 | tf_op jit(solution)/shard_map/ppermute | solution.py:27
  107.2 8.4 %collective-permute-start.25 = (bf16[512,256]{1,0:T(8,128)(2,1)S(1)}, bf16[512,256]{1,0:T(8,128)(2,1)S(1)}, u32[]{:S(2)}, u32[]{:S(2)}) collective-permute-start(bf16[512,256]{1,0:T(8,128)(2,1)S(1)} %get-tuple-element.33), channel_id=1, source_target_pairs={{0,112},{8,120},{16,96},{24,104},{32,80},{40,88},{48,64},{56,72},{... | collective-permute-start | bytes 786440 | tf_op jit(solution)/shard_map/ppermute | solution.py:35
  107.3 9.6 %collective-permute-start.28 = (bf16[512,256]{1,0:T(8,128)(2,1)S(1)}, bf16[512,256]{1,0:T(8,128)(2,1)S(1)}, u32[]{:S(2)}, u32[]{:S(2)}) collective-permute-start(bf16[512,256]{1,0:T(8,128)(2,1)S(1)} %get-tuple-element.33), channel_id=1, source_target_pairs={{0,80},{8,88},{16,64},{24,72},{32,112},{40,120},{48,96},{56,104},{... | collective-permute-start | bytes 786440 | tf_op jit(solution)/shard_map/ppermute | solution.py:35
  108.9 10.0 %collective-permute-start.32 = (bf16[512,256]{1,0:T(8,128)(2,1)S(1)}, bf16[512,256]{1,0:T(8,128)(2,1)S(1)}, u32[]{:S(2)}, u32[]{:S(2)}) collective-permute-start(bf16[512,256]{1,0:T(8,128)(2,1)S(1)} %get-tuple-element.33), channel_id=1, source_target_pairs={{0,72},{8,64},{16,88},{24,80},{32,104},{40,96},{48,120},{56,112},{... | collective-permute-start | bytes 786440 | tf_op jit(solution)/shard_map/ppermute | solution.py:35
  109.8 17.5 %collective-permute-start.31 = (bf16[2,512,256]{2,1,0:T(8,128)(2,1)S(1)}, bf16[2,512,256]{2,1,0:T(8,128)(2,1)S(1)}, u32[]{:S(2)}, u32[]{:S(2)}) collective-permute-start(bf16[2,512,256]{2,1,0:T(8,128)(2,1)S(1)} %get-tuple-element.34), channel_id=1, source_target_pairs={{0,64},{8,72},{16,80},{24,88},{32,96},{40,104},{48,112},{56,120},{... | collective-permute-start | bytes 1572872 | tf_op jit(solution)/shard_map/ppermute | solution.py:35
  115.6 7.6 %collective-permute-start.26 = (bf16[512,256]{1,0:T(8,128)(2,1)S(1)}, bf16[512,256]{1,0:T(8,128)(2,1)S(1)}, u32[]{:S(2)}, u32[]{:S(2)}) collective-permute-start(bf16[512,256]{1,0:T(8,128)(2,1)S(1)} %collective-permute-done.25.refs_3_), channel_id=1, source_target_pairs={{0,8},{8,0},{16,24},{24,16},{32,40},{40,32},{48,56},{56,48},{64,72... | collective-permute-start | bytes 786440 | tf_op jit(solution)/shard_map/ppermute | solution.py:35
  116.9 8.7 %collective-permute-start.29 = (bf16[512,256]{1,0:T(8,128)(2,1)S(1)}, bf16[512,256]{1,0:T(8,128)(2,1)S(1)}, u32[]{:S(2)}, u32[]{:S(2)}) collective-permute-start(bf16[512,256]{1,0:T(8,128)(2,1)S(1)} %collective-permute-done.28.refs_2_), channel_id=1, source_target_pairs={{0,48},{8,56},{16,32},{24,40},{32,16},{40,24},{48,0},{56,8},{64,11... | collective-permute-start | bytes 786440 | tf_op jit(solution)/shard_map/ppermute | solution.py:35
  119.0 8.7 %collective-permute-start.33 = (bf16[512,256]{1,0:T(8,128)(2,1)S(1)}, bf16[512,256]{1,0:T(8,128)(2,1)S(1)}, u32[]{:S(2)}, u32[]{:S(2)}) collective-permute-start(bf16[512,256]{1,0:T(8,128)(2,1)S(1)} %collective-permute-done.32.refs_1_), channel_id=1, source_target_pairs={{0,16},{8,24},{16,0},{24,8},{32,48},{40,56},{48,32},{56,40},{64,80... | collective-permute-start | bytes 786440 | tf_op jit(solution)/shard_map/ppermute | solution.py:35
  123.2 6.3 %collective-permute-start.27 = (bf16[256,256]{1,0:T(8,128)(2,1)S(1)}, bf16[256,256]{1,0:T(8,128)(2,1)S(1)}, u32[]{:S(2)}, u32[]{:S(2)}) collective-permute-start(bf16[256,256]{1,0:T(8,128)(2,1)S(1)} %slice.24), channel_id=1, source_target_pairs={{0,16},{8,24},{16,0},{24,8},{32,48},{40,56},{48,32},{56,40},{64,80... | collective-permute-start | bytes 393224 | tf_op jit(solution)/shard_map/ppermute | solution.py:35
  125.5 5.1 %collective-permute-start.30 = (bf16[256,256]{1,0:T(8,128)(2,1)S(1)}, bf16[256,256]{1,0:T(8,128)(2,1)S(1)}, u32[]{:S(2)}, u32[]{:S(2)}) collective-permute-start(bf16[256,256]{1,0:T(8,128)(2,1)S(1)} %slice.25), channel_id=1, source_target_pairs={{0,8},{8,0},{16,24},{24,16},{32,40},{40,32},{48,56},{56,48},{64,72... | collective-permute-start | bytes 393224 | tf_op jit(solution)/shard_map/ppermute | solution.py:35
  131.6 7.9 %collective-permute-start.34 = (bf16[512,256]{1,0:T(8,128)(2,1)S(1)}, bf16[512,256]{1,0:T(8,128)(2,1)S(1)}, u32[]{:S(2)}, u32[]{:S(2)}) collective-permute-start(bf16[512,256]{1,0:T(8,128)(2,1)S(1)} %shard_map.43.refs_0_), channel_id=1, source_target_pairs={{0,48},{8,56},{16,32},{24,40},{32,16},{40,24},{48,0},{56,8},{64,11... | collective-permute-start | bytes 786440 | tf_op jit(solution)/shard_map/ppermute | solution.py:35
  134.1 6.7 %collective-permute-start.37 = (bf16[512,256]{1,0:T(8,128)(2,1)S(1)}, bf16[512,256]{1,0:T(8,128)(2,1)S(1)}, u32[]{:S(2)}, u32[]{:S(2)}) collective-permute-start(bf16[512,256]{1,0:T(8,128)(2,1)S(1)} %shard_map.43.refs_0_), channel_id=1, source_target_pairs={{0,16},{8,24},{16,0},{24,8},{32,48},{40,56},{48,32},{56,40},{64,80... | collective-permute-start | bytes 786440 | tf_op jit(solution)/shard_map/ppermute | solution.py:35
  134.1 8.6 %collective-permute-start.40 = (bf16[512,256]{1,0:T(8,128)(2,1)S(1)}, bf16[512,256]{1,0:T(8,128)(2,1)S(1)}, u32[]{:S(2)}, u32[]{:S(2)}) collective-permute-start(bf16[512,256]{1,0:T(8,128)(2,1)S(1)} %shard_map.43.refs_0_), channel_id=1, source_target_pairs={{0,8},{8,0},{16,24},{24,16},{32,40},{40,32},{48,56},{56,48},{64,72... | collective-permute-start | bytes 786440 | tf_op jit(solution)/shard_map/ppermute | solution.py:35
  139.5 6.6 %collective-permute-start.35 = (bf16[512,256]{1,0:T(8,128)(2,1)S(1)}, bf16[512,256]{1,0:T(8,128)(2,1)S(1)}, u32[]{:S(2)}, u32[]{:S(2)}) collective-permute-start(bf16[512,256]{1,0:T(8,128)(2,1)S(1)} %collective-permute-done.34.refs_3_), channel_id=1, source_target_pairs={{0,8},{8,0},{16,24},{24,16},{32,40},{40,32},{48,56},{56,48},{64,72... | collective-permute-start | bytes 786440 | tf_op jit(solution)/shard_map/ppermute | solution.py:35
  140.8 7.6 %collective-permute-start.38 = (bf16[512,256]{1,0:T(8,128)(2,1)S(1)}, bf16[512,256]{1,0:T(8,128)(2,1)S(1)}, u32[]{:S(2)}, u32[]{:S(2)}) collective-permute-start(bf16[512,256]{1,0:T(8,128)(2,1)S(1)} %collective-permute-done.37.refs_2_), channel_id=1, source_target_pairs={{0,48},{8,56},{16,32},{24,40},{32,16},{40,24},{48,0},{56,8},{64,11... | collective-permute-start | bytes 786440 | tf_op jit(solution)/shard_map/ppermute | solution.py:35
  142.7 8.0 %collective-permute-start.41 = (bf16[512,256]{1,0:T(8,128)(2,1)S(1)}, bf16[512,256]{1,0:T(8,128)(2,1)S(1)}, u32[]{:S(2)}, u32[]{:S(2)}) collective-permute-start(bf16[512,256]{1,0:T(8,128)(2,1)S(1)} %collective-permute-done.40.refs_1_), channel_id=1, source_target_pairs={{0,16},{8,24},{16,0},{24,8},{32,48},{40,56},{48,32},{56,40},{64,80... | collective-permute-start | bytes 786440 | tf_op jit(solution)/shard_map/ppermute | solution.py:35
  146.1 6.4 %collective-permute-start.36 = (bf16[256,256]{1,0:T(8,128)(2,1)S(1)}, bf16[256,256]{1,0:T(8,128)(2,1)S(1)}, u32[]{:S(2)}, u32[]{:S(2)}) collective-permute-start(bf16[256,256]{1,0:T(8,128)(2,1)S(1)} %slice.26), channel_id=1, source_target_pairs={{0,16},{8,24},{16,0},{24,8},{32,48},{40,56},{48,32},{56,40},{64,80... | collective-permute-start | bytes 393224 | tf_op jit(solution)/shard_map/ppermute | solution.py:35
  148.4 5.1 %collective-permute-start.39 = (bf16[256,256]{1,0:T(8,128)(2,1)S(1)}, bf16[256,256]{1,0:T(8,128)(2,1)S(1)}, u32[]{:S(2)}, u32[]{:S(2)}) collective-permute-start(bf16[256,256]{1,0:T(8,128)(2,1)S(1)} %slice.27), channel_id=1, source_target_pairs={{0,8},{8,0},{16,24},{24,16},{32,40},{40,32},{48,56},{56,48},{64,72... | collective-permute-start | bytes 393224 | tf_op jit(solution)/shard_map/ppermute | solution.py:35

commit v4 on v3

--- a/solution.py
+++ b/solution.py
@@ -225,7 +225,7 @@
     first_ring.send((r_down[1], r_up[2]))
     r_down[3] = z_send(r_down[2], -1)
     r_up[4] = z_send(r_up[3], 1)
-    first_ring.send((r_down[2], r_up[3]))
+    next(first_ring)
     passed = next(first_ring)
     tiles = {0: own_refl, 1: r_down[1], 2: r_down[2], 5: r_up[3], 6: r_up[2], 7: r_up[1]}
     early = multiply_tiles(tiles, passed, step_place, F32)

time: 158 us -> 156 us (0.987)
  starting transfers between devices: 57.9 us -> 56 us
    ppermute x14, waiting for transfers between devices: 20.6 us -> 16.4 us  [z_send(): return lax.ppermute(block, ('slab', 'col'), route)]
    ppermute x28, waiting for transfers between devices: 58.3 us -> 62.2 us  [row_swap(): return lax.ppermute(block, ('slab', 'row'), route)]
    ppermute x28, starting transfers between devices: 32.1 us -> 30.2 us  [row_swap(): return lax.ppermute(block, ('slab', 'row'), route)]
  transfers between devices with their start and end apart: 42 -> 42, of which waited for: 26 -> 24; matrix products, arithmetic and copies ran while one was open for 3% -> 3% of each run, Pallas kernels for 6% -> 6%
where the time goes in v4:
time: 156 us; the launch traced here: 153 us
  waiting for transfers between devices  78.6 us (50%)
  starting transfers between devices  56 us (36%)
  Pallas kernels  13.6 us (9%)
  local copies, waits for them, and re-layouts  4.45 us (3%)
    ppermute x28, waiting for transfers between devices, row_swap(): return lax.ppermute(block, ('slab', 'row'), route)  62.2 us
    ppermute x28, starting transfers between devices, row_swap(): return lax.ppermute(block, ('slab', 'row'), route)  30.2 us
    ppermute x14, starting transfers between devices, z_send(): return lax.ppermute(block, ('slab', 'col'), route)  25.8 us
    ppermute x14, waiting for transfers between devices, z_send(): return lax.ppermute(block, ('slab', 'col'), route)  16.4 us
    pallas_call x4, Pallas kernels, multiply_some(): pl.pallas_call(functools.partial(fold, [piece[:2] for piece in pieces], l...  6.36 us
    pallas_call x3, Pallas kernels, multiply_tiles(): pl.pallas_call(functools.partial(fold_tiles, steps, len(beside) > 0), in_...  5.48 us
    unnamed x12, local copies, waits for them, and re-layouts  3.26 us
  transfers between devices with their start and end apart: 42, of which 24 were waited for; matrix products, arithmetic and copies ran while one was open for 3% of the time, Pallas kernels for 6%

profile of v4, /device:TPU:16, one launch (start us, length us, event | category | flops | bytes accessed | tf_op | source)
XLA Modules:
  0.0 153.0 jit_solution(13789433772168584597)
XLA Ops:
  0.0 2.0 %collective-permute-start.10 = (bf16[512,512]{1,0:T(8,128)(2,1)}, bf16[512,512]{1,0:T(8,128)(2,1)S(1)}, u32[]{:S(2)}, u32[]{:S(2)}) collective-permute-start(bf16[512,512]{1,0:T(8,128)(2,1)} %bitcast.27), channel_id=1, source_target_pairs={{0,65},{1,66},{2,67},{3,68},{4,69},{5,70},{6,71},{7,64},{64,1},{65... | collective-permute-start | bytes 1572872 | tf_op jit(solution)/shard_map/ppermute | solution.py:27
  2.0 4.0 %collective-permute-start.1 = (bf16[512,512]{1,0:T(8,128)(2,1)}, bf16[512,512]{1,0:T(8,128)(2,1)S(1)}, u32[]{:S(2)}, u32[]{:S(2)}) collective-permute-start(bf16[512,512]{1,0:T(8,128)(2,1)} %bitcast.28), channel_id=1, source_target_pairs={{0,71},{1,64},{2,65},{3,66},{4,67},{5,68},{6,69},{7,70},{64,7},{65... | collective-permute-start | bytes 1572872 | tf_op jit(solution)/shard_map/ppermute | solution.py:27
  6.1 1.3 collective-permute-start.3
  7.7 6.6 %collective-permute-done.3 = bf16[512,256]{1,0:T(8,128)(2,1)S(1)} collective-permute-done((bf16[512,256]{1,0:T(8,128)(2,1)}, bf16[512,256]{1,0:T(8,128)(2,1)S(1)}, u32[]{:S(2)}, u32[]{:S(2)}) %collective-permute-start.3) | collective-permute-done | bytes 262176 | tf_op jit(solution)/shard_map/ppermute | solution.py:35
  14.4 2.8 %collective-permute-start.6 = (bf16[2,512,256]{2,1,0:T(8,128)(2,1)S(1)}, bf16[2,512,256]{2,1,0:T(8,128)(2,1)}, u32[]{:S(2)}, u32[]{:S(2)}) collective-permute-start(bf16[2,512,256]{2,1,0:T(8,128)(2,1)S(1)} %pad_maximum_fusion), channel_id=1, source_target_pairs={{0,48},{8,56},{16,32},{24,40},{32,16},{40,24},{48,0},{56,8},{64,11... | collective-permute-start | bytes 1572872 | tf_op jit(solution)/shard_map/ppermute | solution.py:35
  18.5 3.2 %collective-permute-start.4 = (bf16[512,512]{1,0:T(8,128)(2,1)S(1)}, bf16[512,512]{1,0:T(8,128)(2,1)S(1)}, u32[]{:S(2)}, u32[]{:S(2)}) collective-permute-start(bf16[512,512]{1,0:T(8,128)(2,1)S(1)} %collective-permute-done.1.refs_1_), channel_id=1, source_target_pairs={{0,7},{1,0},{2,1},{3,2},{4,3},{5,4},{6,5},{7,6},{64,71},{65,64},{6... | collective-permute-start | bytes 1572872 | tf_op jit(solution)/shard_map/ppermute | solution.py:27
  21.7 8.6 %collective-permute-done.6 = bf16[2,512,256]{2,1,0:T(8,128)(2,1)} collective-permute-done((bf16[2,512,256]{2,1,0:T(8,128)(2,1)S(1)}, bf16[2,512,256]{2,1,0:T(8,128)(2,1)}, u32[]{:S(2)}, u32[]{:S(2)}) %collective-permute-start.6) | collective-permute-done | bytes 524320 | tf_op jit(solution)/shard_map/ppermute | solution.py:35
  31.6 2.1 %collective-permute-done.11.refs_6_ = bf16[512,512]{1,0:T(8,128)(2,1)S(1)} collective-permute-done((bf16[512,512]{1,0:T(8,128)(2,1)S(1)}, bf16[512,512]{1,0:T(8,128)(2,1)S(1)}, u32[]{:S(2)}, u32[]{:S(2)}) %collective-permute-start.11) | collective-permute-done | bytes 524320 | tf_op jit(solution)/shard_map/ppermute | solution.py:27
  33.6 3.2 %collective-permute-start.7 = (bf16[512,512]{1,0:T(8,128)(2,1)S(1)}, bf16[512,512]{1,0:T(8,128)(2,1)}, u32[]{:S(2)}, u32[]{:S(2)}) collective-permute-start(bf16[512,512]{1,0:T(8,128)(2,1)S(1)} %collective-permute-done.4.refs_2_), channel_id=1, source_target_pairs={{0,7},{1,0},{2,1},{3,2},{4,3},{5,4},{6,5},{7,6},{64,71},{65,64},{6... | collective-permute-start | bytes 1572872 | tf_op jit(solution)/shard_map/ppermute | solution.py:27
  36.9 7.4 %collective-permute-done.8 = bf16[2,512,256]{2,1,0:T(8,128)(2,1)} collective-permute-done((bf16[2,512,256]{2,1,0:T(8,128)(2,1)}, bf16[2,512,256]{2,1,0:T(8,128)(2,1)}, u32[]{:S(2)}, u32[]{:S(2)}) %collective-permute-start.8) | collective-permute-done | bytes 524320 | tf_op jit(solution)/shard_map/ppermute | solution.py:35
  44.3 3.8 %collective-permute-done.12.refs_5_ = bf16[512,512]{1,0:T(8,128)(2,1)} collective-permute-done((bf16[512,512]{1,0:T(8,128)(2,1)S(1)}, bf16[512,512]{1,0:T(8,128)(2,1)}, u32[]{:S(2)}, u32[]{:S(2)}) %collective-permute-start.12) | collective-permute-done | bytes 524320 | tf_op jit(solution)/shard_map/ppermute | solution.py:27
  48.1 3.2 %collective-permute-start.9 = (bf16[512,512]{1,0:T(8,128)(2,1)}, bf16[512,512]{1,0:T(8,128)(2,1)S(1)}, u32[]{:S(2)}, u32[]{:S(2)}) collective-permute-start(bf16[512,512]{1,0:T(8,128)(2,1)} %collective-permute-done.7.refs_3_), channel_id=1, source_target_pairs={{0,7},{1,0},{2,1},{3,2},{4,3},{5,4},{6,5},{7,6},{64,71},{65,64},{6... | collective-permute-start | bytes 1572872 | tf_op jit(solution)/shard_map/ppermute | solution.py:27
  54.5 6.6 %collective-permute-done.9.refs_4_ = bf16[512,512]{1,0:T(8,128)(2,1)S(1)} collective-permute-done((bf16[512,512]{1,0:T(8,128)(2,1)}, bf16[512,512]{1,0:T(8,128)(2,1)S(1)}, u32[]{:S(2)}, u32[]{:S(2)}) %collective-permute-start.9) | collective-permute-done | bytes 524320 | tf_op jit(solution)/shard_map/ppermute | solution.py:27
  61.0 3.6 %collective-permute-start.13 = (bf16[512,512]{1,0:T(8,128)(2,1)S(1)}, bf16[512,512]{1,0:T(8,128)(2,1)S(1)}, u32[]{:S(2)}, u32[]{:S(2)}) collective-permute-start(bf16[512,512]{1,0:T(8,128)(2,1)S(1)} %bitcast.20), channel_id=1, source_target_pairs={{0,7},{1,0},{2,1},{3,2},{4,3},{5,4},{6,5},{7,6},{64,71},{65,64},{6... | collective-permute-start | bytes 1572872 | tf_op jit(solution)/shard_map/ppermute | solution.py:27
  65.7 2.6 %shard_map.38.refs_3_ = bf16[512,256]{1,0:T(8,128)(2,1)S(1)} custom-call(s32[8]{0:T(128)S(1)} %fusion.order, bf16[8,512,256]{2,1,0:T(8,128)(2,1)S(1)} %constant_dynamic-update-slice_fusion.shots, bf16[512,512]{1,0:T(8,128)(2,1)S(1)} %collective-permute-done.refs_0_, bf16[512,512]{1,0:T(8,128)(2,1)S(1)} %collective-permute-done.1.refs_1_, ...), custom_call_target="tpu_custom_call" | custom-call | flops 1073741824 | bytes 6291456 | tf_op jit(solution)/shard_map/pallas_call | solution.py:112
  68.4 1.6 %collective-permute-start.15 = (bf16[512,256]{1,0:T(8,128)(2,1)S(1)}, bf16[512,256]{1,0:T(8,128)(2,1)S(1)}, u32[]{:S(2)}, u32[]{:S(2)}) collective-permute-start(bf16[512,256]{1,0:T(8,128)(2,1)S(1)} %shard_map.38.refs_3_), channel_id=1, source_target_pairs={{0,8},{8,0},{16,24},{24,16},{32,40},{40,32},{48,56},{56,48},{64,72... | collective-permute-start | bytes 786440 | tf_op jit(solution)/shard_map/ppermute | solution.py:35
  69.9 5.1 %collective-permute-done.15 = bf16[512,256]{1,0:T(8,128)(2,1)S(1)} collective-permute-done((bf16[512,256]{1,0:T(8,128)(2,1)S(1)}, bf16[512,256]{1,0:T(8,128)(2,1)S(1)}, u32[]{:S(2)}, u32[]{:S(2)}) %collective-permute-start.15) | collective-permute-done | bytes 262176 | tf_op jit(solution)/shard_map/ppermute | solution.py:35
  75.1 1.5 collective-permute-done.18.refs_6_.refs_4_
  76.6 2.8 %collective-permute-start.22 = (bf16[2,512,256]{2,1,0:T(8,128)(2,1)S(1)}, bf16[2,512,256]{2,1,0:T(8,128)(2,1)S(1)}, u32[]{:S(2)}, u32[]{:S(2)}) collective-permute-start(bf16[2,512,256]{2,1,0:T(8,128)(2,1)S(1)} %pad_maximum_fusion.1), channel_id=1, source_target_pairs={{0,48},{8,56},{16,32},{24,40},{32,16},{40,24},{48,0},{56,8},{64,11... | collective-permute-start | bytes 1572872 | tf_op jit(solution)/shard_map/ppermute | solution.py:35
  79.5 3.2 %collective-permute-start.16 = (bf16[512,512]{1,0:T(8,128)(2,1)S(1)}, bf16[512,512]{1,0:T(8,128)(2,1)S(1)}, u32[]{:S(2)}, u32[]{:S(2)}) collective-permute-start(bf16[512,512]{1,0:T(8,128)(2,1)S(1)} %collective-permute-done.13.refs_1_), channel_id=1, source_target_pairs={{0,7},{1,0},{2,1},{3,2},{4,3},{5,4},{6,5},{7,6},{64,71},{65,64},{6... | collective-permute-start | bytes 1572872 | tf_op jit(solution)/shard_map/ppermute | solution.py:27
  82.8 4.7 %collective-permute-done.22 = bf16[2,512,256]{2,1,0:T(8,128)(2,1)S(1)} collective-permute-done((bf16[2,512,256]{2,1,0:T(8,128)(2,1)S(1)}, bf16[2,512,256]{2,1,0:T(8,128)(2,1)S(1)}, u32[]{:S(2)}, u32[]{:S(2)}) %collective-permute-start.22) | collective-permute-done | bytes 524320 | tf_op jit(solution)/shard_map/ppermute | solution.py:35
  88.1 3.5 %collective-permute-done.21 = bf16[2,512,256]{2,1,0:T(8,128)(2,1)S(1)} collective-permute-done((bf16[2,512,256]{2,1,0:T(8,128)(2,1)S(1)}, bf16[2,512,256]{2,1,0:T(8,128)(2,1)S(1)}, u32[]{:S(2)}, u32[]{:S(2)}) %collective-permute-start.21) | collective-permute-done | bytes 524320 | tf_op jit(solution)/shard_map/ppermute | solution.py:35
  92.3 2.8 %collective-permute-start.17 = (bf16[512,512]{1,0:T(8,128)(2,1)S(1)}, bf16[512,512]{1,0:T(8,128)(2,1)S(1)}, u32[]{:S(2)}, u32[]{:S(2)}) collective-permute-start(bf16[512,512]{1,0:T(8,128)(2,1)S(1)} %collective-permute-done.16.refs_2_), channel_id=1, source_target_pairs={{0,7},{1,0},{2,1},{3,2},{4,3},{5,4},{6,5},{7,6},{64,71},{65,64},{6... | collective-permute-start | bytes 1572872 | tf_op jit(solution)/shard_map/ppermute | solution.py:27
  95.2 4.2 %collective-permute-done.24 = bf16[512,256]{1,0:T(8,128)(2,1)S(1)} collective-permute-done((bf16[512,256]{1,0:T(8,128)(2,1)S(1)}, bf16[512,256]{1,0:T(8,128)(2,1)S(1)}, u32[]{:S(2)}, u32[]{:S(2)}) %collective-permute-start.24) | collective-permute-done | bytes 262176 | tf_op jit(solution)/shard_map/ppermute | solution.py:35
  99.4 1.7 %shard_map.40.refs_2_ = f32[512,256]{1,0:T(8,128)S(1)} custom-call(s32[8]{0:T(128)S(1)} %fusion.order, bf16[8,512,256]{2,1,0:T(8,128)(2,1)S(1)} %constant_dynamic-update-slice_fusion.5.shots, bf16[512,512]{1,0:T(8,128)(2,1)S(1)} %bitcast.21, bf16[512,512]{1,0:T(8,128)(2,1)S(1)} %collective-permute-done.13.refs_1_, ...), custom_call_target="tpu_custom_call" | custom-call | flops 805306368 | bytes 4718592 | tf_op jit(solution)/shard_map/pallas_call | solution.py:112
  101.1 1.2 collective-permute-done.20.refs_4_.refs_1_
  102.5 1.2 shard_map.41
  103.7 2.0 %collective-permute-start.28 = (bf16[512,256]{1,0:T(8,128)(2,1)S(1)}, bf16[512,256]{1,0:T(8,128)(2,1)S(1)}, u32[]{:S(2)}, u32[]{:S(2)}) collective-permute-start(bf16[512,256]{1,0:T(8,128)(2,1)S(1)} %get-tuple-element.29), channel_id=1, source_target_pairs={{0,80},{8,88},{16,64},{24,72},{32,112},{40,120},{48,96},{56,104},{... | collective-permute-start | bytes 786440 | tf_op jit(solution)/shard_map/ppermute | solution.py:35
  105.7 2.2 %collective-permute-start.32 = (bf16[512,256]{1,0:T(8,128)(2,1)S(1)}, bf16[512,256]{1,0:T(8,128)(2,1)S(1)}, u32[]{:S(2)}, u32[]{:S(2)}) collective-permute-start(bf16[512,256]{1,0:T(8,128)(2,1)S(1)} %get-tuple-element.29), channel_id=1, source_target_pairs={{0,72},{8,64},{16,88},{24,80},{32,104},{40,96},{48,120},{56,112},{... | collective-permute-start | bytes 786440 | tf_op jit(solution)/shard_map/ppermute | solution.py:35
  107.9 5.1 %collective-permute-done.25.refs_3_ = bf16[512,256]{1,0:T(8,128)(2,1)S(1)} collective-permute-done((bf16[512,256]{1,0:T(8,128)(2,1)S(1)}, bf16[512,256]{1,0:T(8,128)(2,1)S(1)}, u32[]{:S(2)}, u32[]{:S(2)}) %collective-permute-start.25) | collective-permute-done | bytes 262176 | tf_op jit(solution)/shard_map/ppermute | solution.py:35
  113.0 1.3 collective-permute-start.26
  114.3 1.1 collective-permute-start.29
  115.4 1.9 %collective-permute-start.33 = (bf16[512,256]{1,0:T(8,128)(2,1)S(1)}, bf16[512,256]{1,0:T(8,128)(2,1)S(1)}, u32[]{:S(2)}, u32[]{:S(2)}) collective-permute-start(bf16[512,256]{1,0:T(8,128)(2,1)S(1)} %collective-permute-done.32.refs_1_), channel_id=1, source_target_pairs={{0,16},{8,24},{16,0},{24,8},{32,48},{40,56},{48,32},{56,40},{64,80... | collective-permute-start | bytes 786440 | tf_op jit(solution)/shard_map/ppermute | solution.py:35
  117.3 4.3 %collective-permute-done.26.refs_6_ = bf16[512,256]{1,0:T(8,128)(2,1)S(1)} collective-permute-done((bf16[512,256]{1,0:T(8,128)(2,1)S(1)}, bf16[512,256]{1,0:T(8,128)(2,1)S(1)}, u32[]{:S(2)}, u32[]{:S(2)}) %collective-permute-start.26) | collective-permute-done | bytes 262176 | tf_op jit(solution)/shard_map/ppermute | solution.py:35
  122.7 1.1 collective-permute-done.29.refs_5_
  125.0 1.8 %shard_map.42.refs_2_ = f32[512,256]{1,0:T(8,128)S(1)} custom-call(s32[8]{0:T(128)S(1)} %and_select_fusion.1.order, bf16[8,512,512]{2,1,0:T(8,128)(2,1)S(1)} %shard_map.39.operator, bf16[2,512,256]{2,1,0:T(8,128)(2,1)S(1)} %collective-permute-done.31.refs_0_, bf16[512,256]{1,0:T(8,128)(2,1)S(1)} %collective-permute-done.32.refs_1_, ...), custom_call_target="tpu_custom_call" | custom-call | flops 939524096 | bytes 5505024 | tf_op jit(solution)/shard_map/pallas_call | solution.py:174
  126.9 2.0 %collective-permute-done.30.refs_1_ = bf16[256,256]{1,0:T(8,128)(2,1)S(1)} collective-permute-done((bf16[256,256]{1,0:T(8,128)(2,1)S(1)}, bf16[256,256]{1,0:T(8,128)(2,1)S(1)}, u32[]{:S(2)}, u32[]{:S(2)}) %collective-permute-start.30) | collective-permute-done | bytes 131104 | tf_op jit(solution)/shard_map/ppermute | solution.py:35
  129.8 1.7 %collective-permute-start.34 = (bf16[512,256]{1,0:T(8,128)(2,1)S(1)}, bf16[512,256]{1,0:T(8,128)(2,1)S(1)}, u32[]{:S(2)}, u32[]{:S(2)}) collective-permute-start(bf16[512,256]{1,0:T(8,128)(2,1)S(1)} %shard_map.43.refs_0_), channel_id=1, source_target_pairs={{0,48},{8,56},{16,32},{24,40},{32,16},{40,24},{48,0},{56,8},{64,11... | collective-permute-start | bytes 786440 | tf_op jit(solution)/shard_map/ppermute | solution.py:35
  131.6 1.3 collective-permute-start.40
  132.8 4.9 %collective-permute-done.34.refs_3_ = bf16[512,256]{1,0:T(8,128)(2,1)S(1)} collective-permute-done((bf16[512,256]{1,0:T(8,128)(2,1)S(1)}, bf16[512,256]{1,0:T(8,128)(2,1)S(1)}, u32[]{:S(2)}, u32[]{:S(2)}) %collective-permute-start.34) | collective-permute-done | bytes 262176 | tf_op jit(solution)/shard_map/ppermute | solution.py:35
  138.7 2.0 %collective-permute-start.38 = (bf16[512,256]{1,0:T(8,128)(2,1)S(1)}, bf16[512,256]{1,0:T(8,128)(2,1)S(1)}, u32[]{:S(2)}, u32[]{:S(2)}) collective-permute-start(bf16[512,256]{1,0:T(8,128)(2,1)S(1)} %collective-permute-done.37.refs_2_), channel_id=1, source_target_pairs={{0,48},{8,56},{16,32},{24,40},{32,16},{40,24},{48,0},{56,8},{64,11... | collective-permute-start | bytes 786440 | tf_op jit(solution)/shard_map/ppermute | solution.py:35
  140.6 1.2 collective-permute-start.41
  141.8 2.3 %collective-permute-done.35.refs_6_ = bf16[512,256]{1,0:T(8,128)(2,1)S(1)} collective-permute-done((bf16[512,256]{1,0:T(8,128)(2,1)S(1)}, bf16[512,256]{1,0:T(8,128)(2,1)S(1)}, u32[]{:S(2)}, u32[]{:S(2)}) %collective-permute-start.35) | collective-permute-done | bytes 262176 | tf_op jit(solution)/shard_map/ppermute | solution.py:35
  144.1 1.5 %collective-permute-start.36 = (bf16[256,256]{1,0:T(8,128)(2,1)S(1)}, bf16[256,256]{1,0:T(8,128)(2,1)S(1)}, u32[]{:S(2)}, u32[]{:S(2)}) collective-permute-start(bf16[256,256]{1,0:T(8,128)(2,1)S(1)} %slice.28), channel_id=1, source_target_pairs={{0,16},{8,24},{16,0},{24,8},{32,48},{40,56},{48,32},{56,40},{64,80... | collective-permute-start | bytes 393224 | tf_op jit(solution)/shard_map/ppermute | solution.py:35
  146.3 1.2 collective-permute-start.39
  147.4 1.4 shard_map.37.operator
  148.9 1.8 %shard_map.44.refs_2_ = f32[512,256]{1,0:T(8,128)S(1)} custom-call(s32[8]{0:T(128)S(1)} %and_select_fusion.1.order, bf16[8,512,512]{2,1,0:T(8,128)(2,1)S(1)} %shard_map.37.operator, bf16[512,256]{1,0:T(8,128)(2,1)S(1)} %shard_map.43.refs_0_, bf16[512,256]{1,0:T(8,128)(2,1)S(1)} %collective-permute-done.40.refs_1_, ...), custom_call_target="tpu_custom_call" | custom-call | flops 939524096 | bytes 5505024 | tf_op jit(solution)/shard_map/pallas_call | solution.py:174
  151.3 1.7 %shard_map.45 = bf16[512,256]{1,0:T(8,128)(2,1)} custom-call(s32[8]{0:T(128)S(1)} %and_select_fusion.1.order, bf16[8,512,512]{2,1,0:T(8,128)(2,1)S(1)} %shard_map.37.operator, bf16[256,256]{1,0:T(8,128)(2,1)S(1)} %collective-permute-done.36.refs_0_, bf16[256,256]{1,0:T(8,128)(2,1)S(1)} %collective-permute-done.39.refs_1_, f32[512,256]{1,0:T(8,128)S(1)} %shard_map.44.refs_2_), custom_call_target="tpu_custom_call" | custom-call | flops 134217728 | bytes 786432 | tf_op jit(solution)/shard_map/pallas_call | solution.py:174
  (69 shorter events, 14.7 us)
Async XLA Ops:
  0.0 17.4 %collective-permute-start = (bf16[512,512]{1,0:T(8,128)(2,1)}, bf16[512,512]{1,0:T(8,128)(2,1)S(1)}, u32[]{:S(2)}, u32[]{:S(2)}) collective-permute-start(bf16[512,512]{1,0:T(8,128)(2,1)} %bitcast.26), channel_id=1, source_target_pairs={{0,64},{8,72},{16,80},{24,88},{32,96},{40,104},{48,112},{56,120},{... | collective-permute-start | bytes 1572872 | tf_op jit(solution)/shard_map/ppermute | solution.py:35
  0.0 18.5 %collective-permute-start.10 = (bf16[512,512]{1,0:T(8,128)(2,1)}, bf16[512,512]{1,0:T(8,128)(2,1)S(1)}, u32[]{:S(2)}, u32[]{:S(2)}) collective-permute-start(bf16[512,512]{1,0:T(8,128)(2,1)} %bitcast.27), channel_id=1, source_target_pairs={{0,65},{1,66},{2,67},{3,68},{4,69},{5,70},{6,71},{7,64},{64,1},{65... | collective-permute-start | bytes 1572872 | tf_op jit(solution)/shard_map/ppermute | solution.py:27
  2.0 16.4 %collective-permute-start.1 = (bf16[512,512]{1,0:T(8,128)(2,1)}, bf16[512,512]{1,0:T(8,128)(2,1)S(1)}, u32[]{:S(2)}, u32[]{:S(2)}) collective-permute-start(bf16[512,512]{1,0:T(8,128)(2,1)} %bitcast.28), channel_id=1, source_target_pairs={{0,71},{1,64},{2,65},{3,66},{4,67},{5,68},{6,69},{7,70},{64,7},{65... | collective-permute-start | bytes 1572872 | tf_op jit(solution)/shard_map/ppermute | solution.py:27
  6.0 1.7 %collective-permute-start.2 = (bf16[512,256]{1,0:T(8,128)(2,1)}, bf16[512,256]{1,0:T(8,128)(2,1)S(1)}, u32[]{:S(2)}, u32[]{:S(2)}) collective-permute-start(bf16[512,256]{1,0:T(8,128)(2,1)} %bitcast.29), channel_id=1, source_target_pairs={{0,64},{8,72},{16,80},{24,88},{32,96},{40,104},{48,112},{56,120},{... | collective-permute-start | bytes 786440 | tf_op jit(solution)/shard_map/ppermute | solution.py:35
  6.1 8.2 %collective-permute-start.3 = (bf16[512,256]{1,0:T(8,128)(2,1)}, bf16[512,256]{1,0:T(8,128)(2,1)S(1)}, u32[]{:S(2)}, u32[]{:S(2)}) collective-permute-start(bf16[512,256]{1,0:T(8,128)(2,1)} %bitcast.30), channel_id=1, source_target_pairs={{0,72},{8,64},{16,88},{24,80},{32,104},{40,96},{48,120},{56,112},{... | collective-permute-start | bytes 786440 | tf_op jit(solution)/shard_map/ppermute | solution.py:35
  14.3 3.1 %copy-start.1 = (bf16[512,256]{1,0:T(8,128)(2,1)}, bf16[512,256]{1,0:T(8,128)(2,1)S(1)}, u32[]{:S(2)}) copy-start(bf16[512,256]{1,0:T(8,128)(2,1)S(1)} %collective-permute-done.3) | copy-start | bytes 786436
  14.3 46.7 %copy-start = (bf16[1,512,512]{2,1,0:T(8,128)(2,1)S(1)}, bf16[1,512,512]{2,1,0:T(8,128)(2,1)}, u32[]{:S(2)}) copy-start(bf16[1,512,512]{2,1,0:T(8,128)(2,1)} %param.3) | copy-start | bytes 1572868
  14.4 15.9 %collective-permute-start.6 = (bf16[2,512,256]{2,1,0:T(8,128)(2,1)S(1)}, bf16[2,512,256]{2,1,0:T(8,128)(2,1)}, u32[]{:S(2)}, u32[]{:S(2)}) collective-permute-start(bf16[2,512,256]{2,1,0:T(8,128)(2,1)S(1)} %pad_maximum_fusion), channel_id=1, source_target_pairs={{0,48},{8,56},{16,32},{24,40},{32,16},{40,24},{48,0},{56,8},{64,11... | collective-permute-start | bytes 1572872 | tf_op jit(solution)/shard_map/ppermute | solution.py:35
  17.2 14.4 %collective-permute-start.5 = (bf16[2,512,256]{2,1,0:T(8,128)(2,1)S(1)}, bf16[2,512,256]{2,1,0:T(8,128)(2,1)}, u32[]{:S(2)}, u32[]{:S(2)}) collective-permute-start(bf16[2,512,256]{2,1,0:T(8,128)(2,1)S(1)} %pad_maximum_fusion), channel_id=1, source_target_pairs={{0,16},{8,24},{16,0},{24,8},{32,48},{40,56},{48,32},{56,40},{64,80... | collective-permute-start | bytes 1572872 | tf_op jit(solution)/shard_map/ppermute | solution.py:35
  18.5 15.2 %collective-permute-start.11 = (bf16[512,512]{1,0:T(8,128)(2,1)S(1)}, bf16[512,512]{1,0:T(8,128)(2,1)S(1)}, u32[]{:S(2)}, u32[]{:S(2)}) collective-permute-start(bf16[512,512]{1,0:T(8,128)(2,1)S(1)} %collective-permute-done.10.refs_7_), channel_id=1, source_target_pairs={{0,1},{1,2},{2,3},{3,4},{4,5},{5,6},{6,7},{7,0},{64,65},{65,66},{6... | collective-permute-start | bytes 1572872 | tf_op jit(solution)/shard_map/ppermute | solution.py:27
  18.5 15.2 %collective-permute-start.4 = (bf16[512,512]{1,0:T(8,128)(2,1)S(1)}, bf16[512,512]{1,0:T(8,128)(2,1)S(1)}, u32[]{:S(2)}, u32[]{:S(2)}) collective-permute-start(bf16[512,512]{1,0:T(8,128)(2,1)S(1)} %collective-permute-done.1.refs_1_), channel_id=1, source_target_pairs={{0,7},{1,0},{2,1},{3,2},{4,3},{5,4},{6,5},{7,6},{64,71},{65,64},{6... | collective-permute-start | bytes 1572872 | tf_op jit(solution)/shard_map/ppermute | solution.py:27
  30.3 14.0 %collective-permute-start.8 = (bf16[2,512,256]{2,1,0:T(8,128)(2,1)}, bf16[2,512,256]{2,1,0:T(8,128)(2,1)}, u32[]{:S(2)}, u32[]{:S(2)}) collective-permute-start(bf16[2,512,256]{2,1,0:T(8,128)(2,1)} %collective-permute-done.6), channel_id=1, source_target_pairs={{0,16},{8,24},{16,0},{24,8},{32,48},{40,56},{48,32},{56,40},{64,80... | collective-permute-start | bytes 1572872 | tf_op jit(solution)/shard_map/ppermute | solution.py:35
  33.6 14.4 %collective-permute-start.12 = (bf16[512,512]{1,0:T(8,128)(2,1)S(1)}, bf16[512,512]{1,0:T(8,128)(2,1)}, u32[]{:S(2)}, u32[]{:S(2)}) collective-permute-start(bf16[512,512]{1,0:T(8,128)(2,1)S(1)} %collective-permute-done.11.refs_6_), channel_id=1, source_target_pairs={{0,1},{1,2},{2,3},{3,4},{4,5},{5,6},{6,7},{7,0},{64,65},{65,66},{6... | collective-permute-start | bytes 1572872 | tf_op jit(solution)/shard_map/ppermute | solution.py:27
  33.6 14.4 %collective-permute-start.7 = (bf16[512,512]{1,0:T(8,128)(2,1)S(1)}, bf16[512,512]{1,0:T(8,128)(2,1)}, u32[]{:S(2)}, u32[]{:S(2)}) collective-permute-start(bf16[512,512]{1,0:T(8,128)(2,1)S(1)} %collective-permute-done.4.refs_2_), channel_id=1, source_target_pairs={{0,7},{1,0},{2,1},{3,2},{4,3},{5,4},{6,5},{7,6},{64,71},{65,64},{6... | collective-permute-start | bytes 1572872 | tf_op jit(solution)/shard_map/ppermute | solution.py:27
  48.1 16.6 %collective-permute-start.14 = (bf16[512,512]{1,0:T(8,128)(2,1)}, bf16[512,512]{1,0:T(8,128)(2,1)S(1)}, u32[]{:S(2)}, u32[]{:S(2)}) collective-permute-start(bf16[512,512]{1,0:T(8,128)(2,1)} %bitcast.19), channel_id=1, source_target_pairs={{0,1},{1,2},{2,3},{3,4},{4,5},{5,6},{6,7},{7,0},{64,65},{65,66},{6... | collective-permute-start | bytes 1572872 | tf_op jit(solution)/shard_map/ppermute | solution.py:27
  48.1 13.0 %collective-permute-start.9 = (bf16[512,512]{1,0:T(8,128)(2,1)}, bf16[512,512]{1,0:T(8,128)(2,1)S(1)}, u32[]{:S(2)}, u32[]{:S(2)}) collective-permute-start(bf16[512,512]{1,0:T(8,128)(2,1)} %collective-permute-done.7.refs_3_), channel_id=1, source_target_pairs={{0,7},{1,0},{2,1},{3,2},{4,3},{5,4},{6,5},{7,6},{64,71},{65,64},{6... | collective-permute-start | bytes 1572872 | tf_op jit(solution)/shard_map/ppermute | solution.py:27
  61.0 15.5 %collective-permute-start.13 = (bf16[512,512]{1,0:T(8,128)(2,1)S(1)}, bf16[512,512]{1,0:T(8,128)(2,1)S(1)}, u32[]{:S(2)}, u32[]{:S(2)}) collective-permute-start(bf16[512,512]{1,0:T(8,128)(2,1)S(1)} %bitcast.20), channel_id=1, source_target_pairs={{0,7},{1,0},{2,1},{3,2},{4,3},{5,4},{6,5},{7,6},{64,71},{65,64},{6... | collective-permute-start | bytes 1572872 | tf_op jit(solution)/shard_map/ppermute | solution.py:27
  64.6 11.9 %collective-permute-start.18 = (bf16[512,512]{1,0:T(8,128)(2,1)S(1)}, bf16[512,512]{1,0:T(8,128)(2,1)S(1)}, u32[]{:S(2)}, u32[]{:S(2)}) collective-permute-start(bf16[512,512]{1,0:T(8,128)(2,1)S(1)} %collective-permute-done.14.refs_7_.refs_5_), channel_id=1, source_target_pairs={{0,1},{1,2},{2,3},{3,4},{4,5},{5,6},{6,7},{7,0},{64,65},{65,66},{6... | collective-permute-start | bytes 1572872 | tf_op jit(solution)/shard_map/ppermute | solution.py:27
  68.4 6.6 %collective-permute-start.15 = (bf16[512,256]{1,0:T(8,128)(2,1)S(1)}, bf16[512,256]{1,0:T(8,128)(2,1)S(1)}, u32[]{:S(2)}, u32[]{:S(2)}) collective-permute-start(bf16[512,256]{1,0:T(8,128)(2,1)S(1)} %shard_map.38.refs_3_), channel_id=1, source_target_pairs={{0,8},{8,0},{16,24},{24,16},{32,40},{40,32},{48,56},{56,48},{64,72... | collective-permute-start | bytes 786440 | tf_op jit(solution)/shard_map/ppermute | solution.py:35
  76.6 11.0 %collective-permute-start.22 = (bf16[2,512,256]{2,1,0:T(8,128)(2,1)S(1)}, bf16[2,512,256]{2,1,0:T(8,128)(2,1)S(1)}, u32[]{:S(2)}, u32[]{:S(2)}) collective-permute-start(bf16[2,512,256]{2,1,0:T(8,128)(2,1)S(1)} %pad_maximum_fusion.1), channel_id=1, source_target_pairs={{0,48},{8,56},{16,32},{24,40},{32,16},{40,24},{48,0},{56,8},{64,11... | collective-permute-start | bytes 1572872 | tf_op jit(solution)/shard_map/ppermute | solution.py:35
  79.3 12.3 %collective-permute-start.21 = (bf16[2,512,256]{2,1,0:T(8,128)(2,1)S(1)}, bf16[2,512,256]{2,1,0:T(8,128)(2,1)S(1)}, u32[]{:S(2)}, u32[]{:S(2)}) collective-permute-start(bf16[2,512,256]{2,1,0:T(8,128)(2,1)S(1)} %pad_maximum_fusion.1), channel_id=1, source_target_pairs={{0,16},{8,24},{16,0},{24,8},{32,48},{40,56},{48,32},{56,40},{64,80... | collective-permute-start | bytes 1572872 | tf_op jit(solution)/shard_map/ppermute | solution.py:35
  79.5 12.3 %collective-permute-start.19 = (bf16[512,512]{1,0:T(8,128)(2,1)S(1)}, bf16[512,512]{1,0:T(8,128)(2,1)S(1)}, u32[]{:S(2)}, u32[]{:S(2)}) collective-permute-start(bf16[512,512]{1,0:T(8,128)(2,1)S(1)} %collective-permute-done.18.refs_6_.refs_4_), channel_id=1, source_target_pairs={{0,1},{1,2},{2,3},{3,4},{4,5},{5,6},{6,7},{7,0},{64,65},{65,66},{6... | collective-permute-start | bytes 1572872 | tf_op jit(solution)/shard_map/ppermute | solution.py:27
  79.5 12.8 %collective-permute-start.16 = (bf16[512,512]{1,0:T(8,128)(2,1)S(1)}, bf16[512,512]{1,0:T(8,128)(2,1)S(1)}, u32[]{:S(2)}, u32[]{:S(2)}) collective-permute-start(bf16[512,512]{1,0:T(8,128)(2,1)S(1)} %collective-permute-done.13.refs_1_), channel_id=1, source_target_pairs={{0,7},{1,0},{2,1},{3,2},{4,3},{5,4},{6,5},{7,6},{64,71},{65,64},{6... | collective-permute-start | bytes 1572872 | tf_op jit(solution)/shard_map/ppermute | solution.py:27
  87.6 7.6 %collective-permute-start.23 = (bf16[512,256]{1,0:T(8,128)(2,1)S(1)}, bf16[512,256]{1,0:T(8,128)(2,1)S(1)}, u32[]{:S(2)}, u32[]{:S(2)}) collective-permute-start(bf16[512,256]{1,0:T(8,128)(2,1)S(1)} %slice_bitcast_fusion.1), channel_id=1, source_target_pairs={{0,16},{8,24},{16,0},{24,8},{32,48},{40,56},{48,32},{56,40},{64,80... | collective-permute-start | bytes 786440 | tf_op jit(solution)/shard_map/ppermute | solution.py:35
  91.7 7.7 %collective-permute-start.24 = (bf16[512,256]{1,0:T(8,128)(2,1)S(1)}, bf16[512,256]{1,0:T(8,128)(2,1)S(1)}, u32[]{:S(2)}, u32[]{:S(2)}) collective-permute-start(bf16[512,256]{1,0:T(8,128)(2,1)S(1)} %slice_bitcast_fusion), channel_id=1, source_target_pairs={{0,48},{8,56},{16,32},{24,40},{32,16},{40,24},{48,0},{56,8},{64,11... | collective-permute-start | bytes 786440 | tf_op jit(solution)/shard_map/ppermute | solution.py:35
  91.8 10.5 %collective-permute-start.20 = (bf16[512,512]{1,0:T(8,128)(2,1)S(1)}, bf16[512,512]{1,0:T(8,128)(2,1)S(1)}, u32[]{:S(2)}, u32[]{:S(2)}) collective-permute-start(bf16[512,512]{1,0:T(8,128)(2,1)S(1)} %collective-permute-done.19.refs_5_.refs_3_), channel_id=1, source_target_pairs={{0,1},{1,2},{2,3},{3,4},{4,5},{5,6},{6,7},{7,0},{64,65},{65,66},{6... | collective-permute-start | bytes 1572872 | tf_op jit(solution)/shard_map/ppermute | solution.py:27
  92.3 10.1 %collective-permute-start.17 = (bf16[512,512]{1,0:T(8,128)(2,1)S(1)}, bf16[512,512]{1,0:T(8,128)(2,1)S(1)}, u32[]{:S(2)}, u32[]{:S(2)}) collective-permute-start(bf16[512,512]{1,0:T(8,128)(2,1)S(1)} %collective-permute-done.16.refs_2_), channel_id=1, source_target_pairs={{0,7},{1,0},{2,1},{3,2},{4,3},{5,4},{6,5},{7,6},{64,71},{65,64},{6... | collective-permute-start | bytes 1572872 | tf_op jit(solution)/shard_map/ppermute | solution.py:27
  103.6 9.4 %collective-permute-start.25 = (bf16[512,256]{1,0:T(8,128)(2,1)S(1)}, bf16[512,256]{1,0:T(8,128)(2,1)S(1)}, u32[]{:S(2)}, u32[]{:S(2)}) collective-permute-start(bf16[512,256]{1,0:T(8,128)(2,1)S(1)} %get-tuple-element.29), channel_id=1, source_target_pairs={{0,112},{8,120},{16,96},{24,104},{32,80},{40,88},{48,64},{56,72},{... | collective-permute-start | bytes 786440 | tf_op jit(solution)/shard_map/ppermute | solution.py:35
  103.7 10.6 %collective-permute-start.28 = (bf16[512,256]{1,0:T(8,128)(2,1)S(1)}, bf16[512,256]{1,0:T(8,128)(2,1)S(1)}, u32[]{:S(2)}, u32[]{:S(2)}) collective-permute-start(bf16[512,256]{1,0:T(8,128)(2,1)S(1)} %get-tuple-element.29), channel_id=1, source_target_pairs={{0,80},{8,88},{16,64},{24,72},{32,112},{40,120},{48,96},{56,104},{... | collective-permute-start | bytes 786440 | tf_op jit(solution)/shard_map/ppermute | solution.py:35
  105.7 9.7 %collective-permute-start.32 = (bf16[512,256]{1,0:T(8,128)(2,1)S(1)}, bf16[512,256]{1,0:T(8,128)(2,1)S(1)}, u32[]{:S(2)}, u32[]{:S(2)}) collective-permute-start(bf16[512,256]{1,0:T(8,128)(2,1)S(1)} %get-tuple-element.29), channel_id=1, source_target_pairs={{0,72},{8,64},{16,88},{24,80},{32,104},{40,96},{48,120},{56,112},{... | collective-permute-start | bytes 786440 | tf_op jit(solution)/shard_map/ppermute | solution.py:35
  107.9 17.1 %collective-permute-start.31 = (bf16[2,512,256]{2,1,0:T(8,128)(2,1)S(1)}, bf16[2,512,256]{2,1,0:T(8,128)(2,1)S(1)}, u32[]{:S(2)}, u32[]{:S(2)}) collective-permute-start(bf16[2,512,256]{2,1,0:T(8,128)(2,1)S(1)} %get-tuple-element.30), channel_id=1, source_target_pairs={{0,64},{8,72},{16,80},{24,88},{32,96},{40,104},{48,112},{56,120},{... | collective-permute-start | bytes 1572872 | tf_op jit(solution)/shard_map/ppermute | solution.py:35
  113.0 8.5 %collective-permute-start.26 = (bf16[512,256]{1,0:T(8,128)(2,1)S(1)}, bf16[512,256]{1,0:T(8,128)(2,1)S(1)}, u32[]{:S(2)}, u32[]{:S(2)}) collective-permute-start(bf16[512,256]{1,0:T(8,128)(2,1)S(1)} %collective-permute-done.25.refs_3_), channel_id=1, source_target_pairs={{0,8},{8,0},{16,24},{24,16},{32,40},{40,32},{48,56},{56,48},{64,72... | collective-permute-start | bytes 786440 | tf_op jit(solution)/shard_map/ppermute | solution.py:35
  114.3 9.5 %collective-permute-start.29 = (bf16[512,256]{1,0:T(8,128)(2,1)S(1)}, bf16[512,256]{1,0:T(8,128)(2,1)S(1)}, u32[]{:S(2)}, u32[]{:S(2)}) collective-permute-start(bf16[512,256]{1,0:T(8,128)(2,1)S(1)} %collective-permute-done.28.refs_2_), channel_id=1, source_target_pairs={{0,48},{8,56},{16,32},{24,40},{32,16},{40,24},{48,0},{56,8},{64,11... | collective-permute-start | bytes 786440 | tf_op jit(solution)/shard_map/ppermute | solution.py:35
  115.4 9.6 %collective-permute-start.33 = (bf16[512,256]{1,0:T(8,128)(2,1)S(1)}, bf16[512,256]{1,0:T(8,128)(2,1)S(1)}, u32[]{:S(2)}, u32[]{:S(2)}) collective-permute-start(bf16[512,256]{1,0:T(8,128)(2,1)S(1)} %collective-permute-done.32.refs_1_), channel_id=1, source_target_pairs={{0,16},{8,24},{16,0},{24,8},{32,48},{40,56},{48,32},{56,40},{64,80... | collective-permute-start | bytes 786440 | tf_op jit(solution)/shard_map/ppermute | solution.py:35
  121.6 5.3 %collective-permute-start.27 = (bf16[256,256]{1,0:T(8,128)(2,1)S(1)}, bf16[256,256]{1,0:T(8,128)(2,1)S(1)}, u32[]{:S(2)}, u32[]{:S(2)}) collective-permute-start(bf16[256,256]{1,0:T(8,128)(2,1)S(1)} %slice.26), channel_id=1, source_target_pairs={{0,16},{8,24},{16,0},{24,8},{32,48},{40,56},{48,32},{56,40},{64,80... | collective-permute-start | bytes 393224 | tf_op jit(solution)/shard_map/ppermute | solution.py:35
  123.8 5.1 %collective-permute-start.30 = (bf16[256,256]{1,0:T(8,128)(2,1)S(1)}, bf16[256,256]{1,0:T(8,128)(2,1)S(1)}, u32[]{:S(2)}, u32[]{:S(2)}) collective-permute-start(bf16[256,256]{1,0:T(8,128)(2,1)S(1)} %slice.27), channel_id=1, source_target_pairs={{0,8},{8,0},{16,24},{24,16},{32,40},{40,32},{48,56},{56,48},{64,72... | collective-permute-start | bytes 393224 | tf_op jit(solution)/shard_map/ppermute | solution.py:35
  129.8 7.9 %collective-permute-start.34 = (bf16[512,256]{1,0:T(8,128)(2,1)S(1)}, bf16[512,256]{1,0:T(8,128)(2,1)S(1)}, u32[]{:S(2)}, u32[]{:S(2)}) collective-permute-start(bf16[512,256]{1,0:T(8,128)(2,1)S(1)} %shard_map.43.refs_0_), channel_id=1, source_target_pairs={{0,48},{8,56},{16,32},{24,40},{32,16},{40,24},{48,0},{56,8},{64,11... | collective-permute-start | bytes 786440 | tf_op jit(solution)/shard_map/ppermute | solution.py:35
  131.5 7.1 %collective-permute-start.37 = (bf16[512,256]{1,0:T(8,128)(2,1)S(1)}, bf16[512,256]{1,0:T(8,128)(2,1)S(1)}, u32[]{:S(2)}, u32[]{:S(2)}) collective-permute-start(bf16[512,256]{1,0:T(8,128)(2,1)S(1)} %shard_map.43.refs_0_), channel_id=1, source_target_pairs={{0,16},{8,24},{16,0},{24,8},{32,48},{40,56},{48,32},{56,40},{64,80... | collective-permute-start | bytes 786440 | tf_op jit(solution)/shard_map/ppermute | solution.py:35
  131.6 9.1 %collective-permute-start.40 = (bf16[512,256]{1,0:T(8,128)(2,1)S(1)}, bf16[512,256]{1,0:T(8,128)(2,1)S(1)}, u32[]{:S(2)}, u32[]{:S(2)}) collective-permute-start(bf16[512,256]{1,0:T(8,128)(2,1)S(1)} %shard_map.43.refs_0_), channel_id=1, source_target_pairs={{0,8},{8,0},{16,24},{24,16},{32,40},{40,32},{48,56},{56,48},{64,72... | collective-permute-start | bytes 786440 | tf_op jit(solution)/shard_map/ppermute | solution.py:35
  137.7 6.4 %collective-permute-start.35 = (bf16[512,256]{1,0:T(8,128)(2,1)S(1)}, bf16[512,256]{1,0:T(8,128)(2,1)S(1)}, u32[]{:S(2)}, u32[]{:S(2)}) collective-permute-start(bf16[512,256]{1,0:T(8,128)(2,1)S(1)} %collective-permute-done.34.refs_3_), channel_id=1, source_target_pairs={{0,8},{8,0},{16,24},{24,16},{32,40},{40,32},{48,56},{56,48},{64,72... | collective-permute-start | bytes 786440 | tf_op jit(solution)/shard_map/ppermute | solution.py:35
  138.7 7.6 %collective-permute-start.38 = (bf16[512,256]{1,0:T(8,128)(2,1)S(1)}, bf16[512,256]{1,0:T(8,128)(2,1)S(1)}, u32[]{:S(2)}, u32[]{:S(2)}) collective-permute-start(bf16[512,256]{1,0:T(8,128)(2,1)S(1)} %collective-permute-done.37.refs_2_), channel_id=1, source_target_pairs={{0,48},{8,56},{16,32},{24,40},{32,16},{40,24},{48,0},{56,8},{64,11... | collective-permute-start | bytes 786440 | tf_op jit(solution)/shard_map/ppermute | solution.py:35
  140.6 8.2 %collective-permute-start.41 = (bf16[512,256]{1,0:T(8,128)(2,1)S(1)}, bf16[512,256]{1,0:T(8,128)(2,1)S(1)}, u32[]{:S(2)}, u32[]{:S(2)}) collective-permute-start(bf16[512,256]{1,0:T(8,128)(2,1)S(1)} %collective-permute-done.40.refs_1_), channel_id=1, source_target_pairs={{0,16},{8,24},{16,0},{24,8},{32,48},{40,56},{48,32},{56,40},{64,80... | collective-permute-start | bytes 786440 | tf_op jit(solution)/shard_map/ppermute | solution.py:35
  144.1 6.6 %collective-permute-start.36 = (bf16[256,256]{1,0:T(8,128)(2,1)S(1)}, bf16[256,256]{1,0:T(8,128)(2,1)S(1)}, u32[]{:S(2)}, u32[]{:S(2)}) collective-permute-start(bf16[256,256]{1,0:T(8,128)(2,1)S(1)} %slice.28), channel_id=1, source_target_pairs={{0,16},{8,24},{16,0},{24,8},{32,48},{40,56},{48,32},{56,40},{64,80... | collective-permute-start | bytes 393224 | tf_op jit(solution)/shard_map/ppermute | solution.py:35
  146.3 5.1 %collective-permute-start.39 = (bf16[256,256]{1,0:T(8,128)(2,1)S(1)}, bf16[256,256]{1,0:T(8,128)(2,1)S(1)}, u32[]{:S(2)}, u32[]{:S(2)}) collective-permute-start(bf16[256,256]{1,0:T(8,128)(2,1)S(1)} %slice.29), channel_id=1, source_target_pairs={{0,8},{8,0},{16,24},{24,16},{32,40},{40,32},{48,56},{56,48},{64,72... | collective-permute-start | bytes 393224 | tf_op jit(solution)/shard_map/ppermute | solution.py:35

commit v5 on v4

--- a/solution.py
+++ b/solution.py
@@ -83,8 +83,10 @@
     count = len(steps)
     tiles, refs = refs[:count], refs[count:]
     height = 256
-    if beside:
+    if beside == 2:
         early, held, out, both = refs
+    elif beside == 1:
+        early, out = refs
     else:
         (out,) = refs
 
@@ -97,7 +99,7 @@
             total = term if total is None else total + term
         total = total.astype(out.dtype)
         out[rows, :] = total
-        if beside:
+        if beside == 2:
             both[0, rows, :] = total
             both[1, rows, :] = held[rows, :]
 
@@ -110,11 +112,11 @@
     out = jax.ShapeDtypeStruct((rows, columns), dtype)
     pair = jax.ShapeDtypeStruct((2, rows, columns), dtype)
     return pl.pallas_call(
-        functools.partial(fold_tiles, steps, len(beside) > 0),
+        functools.partial(fold_tiles, steps, len(beside)),
         in_specs=[pl.BlockSpec(memory_space=pltpu.SMEM)]
         + [in_vmem] * (1 + len(steps) + len(beside)),
-        out_specs=[in_vmem] * 2 if beside else in_vmem,
-        out_shape=[out, pair] if beside else out,
+        out_specs=[in_vmem] * 2 if len(beside) == 2 else in_vmem,
+        out_shape=[out, pair] if len(beside) == 2 else out,
         compiler_params=pltpu.CompilerParams(vmem_limit_bytes=24 << 20),
         cost_estimate=pl.CostEstimate(
             flops=2 * len(steps) * rows * depth * columns,
@@ -212,9 +214,12 @@
     gate = next(shot_ring)
     t_down[4] = z_send(after(t_down[3], *gate), -1)
     r_up[1] = z_send(after(own_refl, t_up[3], *gate), 1)
-    incoming = after(next(shot_ring), r_up[1])
+    incoming = next(shot_ring)
     tiles = {0: t_here, **t_down, 5: t_up[3], 6: t_up[2], 7: t_up[1]}
-    first = multiply_tiles(tiles, incoming, step_place, BF16)
+    soon = {step: tiles[step] for step in tiles if step != 4}
+    early = multiply_tiles(soon, incoming, step_place, F32)
+    late = {4: after(t_down[4], r_up[1])}
+    first = multiply_tiles(late, incoming, step_place, BF16, (early,))
     trans = tiles
     r_down[1] = z_send(after(own_refl, t_down[4]), -1)
     r_up[2] = z_send(r_up[1], 1)
@@ -222,10 +227,10 @@
     gate = next(first_ring)
     r_down[2] = z_send(after(r_down[1], *gate), -1)
     r_up[3] = z_send(after(r_up[2], *gate), 1)
-    first_ring.send((r_down[1], r_up[2]))
+    next(first_ring)
     r_down[3] = z_send(r_down[2], -1)
     r_up[4] = z_send(r_up[3], 1)
-    next(first_ring)
+    first_ring.send((r_down[1], r_up[2]))
     passed = next(first_ring)
     tiles = {0: own_refl, 1: r_down[1], 2: r_down[2], 5: r_up[3], 6: r_up[2], 7: r_up[1]}
     early = multiply_tiles(tiles, passed, step_place, F32)

time: 156 us -> 154 us (0.987)
  waiting for transfers between devices: 78.6 us -> 76.2 us
    ppermute x28, waiting for transfers between devices: 62.2 us -> 49.7 us  [row_swap(): return lax.ppermute(block, ('slab', 'row'), route)]
    ppermute x14, waiting for transfers between devices: 16.4 us -> 26.5 us  [z_send(): return lax.ppermute(block, ('slab', 'col'), route)]
    ppermute x28, starting transfers between devices: 30.2 us -> 31.8 us  [row_swap(): return lax.ppermute(block, ('slab', 'row'), route)]
    pallas_call x3 -> x4, Pallas kernels: 5.48 us -> 6.2 us  [multiply_tiles(): pl.pallas_call(functools.partial(fold_tiles, steps, len(beside)), in_spec...]
    unnamed x12 -> x13, local copies, waits for them, and re-layouts: 3.26 us -> 3.26 us
  transfers between devices with their start and end apart: 42 -> 42, of which waited for: 24 -> 20; matrix products, arithmetic and copies ran while one was open for 3% -> 3% of each run, Pallas kernels for 6% -> 6%
where the time goes in v5:
time: 154 us; the launch traced here: 152 us
  waiting for transfers between devices  76.2 us (49%)
  starting transfers between devices  56.9 us (37%)
  Pallas kernels  14.1 us (9%)
  local copies, waits for them, and re-layouts  4.45 us (3%)
    ppermute x28, waiting for transfers between devices, row_swap(): return lax.ppermute(block, ('slab', 'row'), route)  49.7 us
    ppermute x28, starting transfers between devices, row_swap(): return lax.ppermute(block, ('slab', 'row'), route)  31.8 us
    ppermute x14, waiting for transfers between devices, z_send(): return lax.ppermute(block, ('slab', 'col'), route)  26.5 us
    ppermute x14, starting transfers between devices, z_send(): return lax.ppermute(block, ('slab', 'col'), route)  25.1 us
    pallas_call x4, Pallas kernels, multiply_some(): pl.pallas_call(functools.partial(fold, [piece[:2] for piece in pieces], l...  6.35 us
    pallas_call x4, Pallas kernels, multiply_tiles(): pl.pallas_call(functools.partial(fold_tiles, steps, len(beside)), in_spec...  6.2 us
    unnamed x13, local copies, waits for them, and re-layouts  3.26 us
  transfers between devices with their start and end apart: 42, of which 20 were waited for; matrix products, arithmetic and copies ran while one was open for 3% of the time, Pallas kernels for 6%

profile of v5, /device:TPU:16, one launch (start us, length us, event | category | flops | bytes accessed | tf_op | source)
XLA Modules:
  0.0 152.1 jit_solution(7959415577920474325)
XLA Ops:
  0.0 2.0 %collective-permute-start.10 = (bf16[512,512]{1,0:T(8,128)(2,1)}, bf16[512,512]{1,0:T(8,128)(2,1)S(1)}, u32[]{:S(2)}, u32[]{:S(2)}) collective-permute-start(bf16[512,512]{1,0:T(8,128)(2,1)} %bitcast.29), channel_id=1, source_target_pairs={{0,65},{1,66},{2,67},{3,68},{4,69},{5,70},{6,71},{7,64},{64,1},{65... | collective-permute-start | bytes 1572872 | tf_op jit(solution)/shard_map/ppermute | solution.py:27
  2.0 4.0 %collective-permute-start.1 = (bf16[512,512]{1,0:T(8,128)(2,1)}, bf16[512,512]{1,0:T(8,128)(2,1)S(1)}, u32[]{:S(2)}, u32[]{:S(2)}) collective-permute-start(bf16[512,512]{1,0:T(8,128)(2,1)} %bitcast.30), channel_id=1, source_target_pairs={{0,71},{1,64},{2,65},{3,66},{4,67},{5,68},{6,69},{7,70},{64,7},{65... | collective-permute-start | bytes 1572872 | tf_op jit(solution)/shard_map/ppermute | solution.py:27
  6.1 1.3 collective-permute-start.3
  7.7 6.6 %collective-permute-done.3 = bf16[512,256]{1,0:T(8,128)(2,1)S(1)} collective-permute-done((bf16[512,256]{1,0:T(8,128)(2,1)}, bf16[512,256]{1,0:T(8,128)(2,1)S(1)}, u32[]{:S(2)}, u32[]{:S(2)}) %collective-permute-start.3) | collective-permute-done | bytes 262176 | tf_op jit(solution)/shard_map/ppermute | solution.py:35
  14.4 1.6 %collective-permute-start.5 = (bf16[2,512,256]{2,1,0:T(8,128)(2,1)S(1)}, bf16[2,512,256]{2,1,0:T(8,128)(2,1)}, u32[]{:S(2)}, u32[]{:S(2)}) collective-permute-start(bf16[2,512,256]{2,1,0:T(8,128)(2,1)S(1)} %pad_maximum_fusion), channel_id=1, source_target_pairs={{0,16},{8,24},{16,0},{24,8},{32,48},{40,56},{48,32},{56,40},{64,80... | collective-permute-start | bytes 1572872 | tf_op jit(solution)/shard_map/ppermute | solution.py:35
  15.9 2.1 %collective-permute-start.6 = (bf16[2,512,256]{2,1,0:T(8,128)(2,1)S(1)}, bf16[2,512,256]{2,1,0:T(8,128)(2,1)}, u32[]{:S(2)}, u32[]{:S(2)}) collective-permute-start(bf16[2,512,256]{2,1,0:T(8,128)(2,1)S(1)} %pad_maximum_fusion), channel_id=1, source_target_pairs={{0,48},{8,56},{16,32},{24,40},{32,16},{40,24},{48,0},{56,8},{64,11... | collective-permute-start | bytes 1572872 | tf_op jit(solution)/shard_map/ppermute | solution.py:35
  18.5 3.2 %collective-permute-start.4 = (bf16[512,512]{1,0:T(8,128)(2,1)S(1)}, bf16[512,512]{1,0:T(8,128)(2,1)S(1)}, u32[]{:S(2)}, u32[]{:S(2)}) collective-permute-start(bf16[512,512]{1,0:T(8,128)(2,1)S(1)} %collective-permute-done.1.refs_1_), channel_id=1, source_target_pairs={{0,7},{1,0},{2,1},{3,2},{4,3},{5,4},{6,5},{7,6},{64,71},{65,64},{6... | collective-permute-start | bytes 1572872 | tf_op jit(solution)/shard_map/ppermute | solution.py:27
  21.7 9.8 %collective-permute-done.6 = bf16[2,512,256]{2,1,0:T(8,128)(2,1)} collective-permute-done((bf16[2,512,256]{2,1,0:T(8,128)(2,1)S(1)}, bf16[2,512,256]{2,1,0:T(8,128)(2,1)}, u32[]{:S(2)}, u32[]{:S(2)}) %collective-permute-start.6) | collective-permute-done | bytes 524320 | tf_op jit(solution)/shard_map/ppermute | solution.py:35
  31.5 2.1 %collective-permute-done.11.refs_6_.refs_5_ = bf16[512,512]{1,0:T(8,128)(2,1)S(1)} collective-permute-done((bf16[512,512]{1,0:T(8,128)(2,1)S(1)}, bf16[512,512]{1,0:T(8,128)(2,1)S(1)}, u32[]{:S(2)}, u32[]{:S(2)}) %collective-permute-start.11) | collective-permute-done | bytes 524320 | tf_op jit(solution)/shard_map/ppermute | solution.py:27
  33.6 3.2 %collective-permute-start.7 = (bf16[512,512]{1,0:T(8,128)(2,1)S(1)}, bf16[512,512]{1,0:T(8,128)(2,1)}, u32[]{:S(2)}, u32[]{:S(2)}) collective-permute-start(bf16[512,512]{1,0:T(8,128)(2,1)S(1)} %collective-permute-done.4.refs_2_), channel_id=1, source_target_pairs={{0,7},{1,0},{2,1},{3,2},{4,3},{5,4},{6,5},{7,6},{64,71},{65,64},{6... | collective-permute-start | bytes 1572872 | tf_op jit(solution)/shard_map/ppermute | solution.py:27
  37.9 7.4 %collective-permute-done.8 = bf16[2,512,256]{2,1,0:T(8,128)(2,1)} collective-permute-done((bf16[2,512,256]{2,1,0:T(8,128)(2,1)}, bf16[2,512,256]{2,1,0:T(8,128)(2,1)}, u32[]{:S(2)}, u32[]{:S(2)}) %collective-permute-start.8) | collective-permute-done | bytes 524320 | tf_op jit(solution)/shard_map/ppermute | solution.py:35
  45.3 2.7 %collective-permute-done.12.refs_5_.refs_4_ = bf16[512,512]{1,0:T(8,128)(2,1)S(1)} collective-permute-done((bf16[512,512]{1,0:T(8,128)(2,1)S(1)}, bf16[512,512]{1,0:T(8,128)(2,1)S(1)}, u32[]{:S(2)}, u32[]{:S(2)}) %collective-permute-start.12) | collective-permute-done | bytes 524320 | tf_op jit(solution)/shard_map/ppermute | solution.py:27
  48.0 3.2 %collective-permute-start.9 = (bf16[512,512]{1,0:T(8,128)(2,1)}, bf16[512,512]{1,0:T(8,128)(2,1)S(1)}, u32[]{:S(2)}, u32[]{:S(2)}) collective-permute-start(bf16[512,512]{1,0:T(8,128)(2,1)} %collective-permute-done.7.refs_3_), channel_id=1, source_target_pairs={{0,7},{1,0},{2,1},{3,2},{4,3},{5,4},{6,5},{7,6},{64,71},{65,64},{6... | collective-permute-start | bytes 1572872 | tf_op jit(solution)/shard_map/ppermute | solution.py:27
  52.3 1.1 constant_dynamic-update-slice_fusion.1
  54.5 2.3 %shard_map.38.refs_1_ = f32[512,256]{1,0:T(8,128)S(1)} custom-call(s32[8]{0:T(128)S(1)} %fusion.order, bf16[8,512,256]{2,1,0:T(8,128)(2,1)S(1)} %constant_dynamic-update-slice_fusion.shots, bf16[512,512]{1,0:T(8,128)(2,1)S(1)} %collective-permute-done.refs_0_, bf16[512,512]{1,0:T(8,128)(2,1)S(1)} %collective-permute-done.1.refs_1_, ...), custom_call_target="tpu_custom_call" | custom-call | flops 939524096 | bytes 5505024 | tf_op jit(solution)/shard_map/pallas_call | solution.py:114
  56.8 4.7 %collective-permute-done.14.refs_7_.refs_5_ = bf16[512,512]{1,0:T(8,128)(2,1)S(1)} collective-permute-done((bf16[512,512]{1,0:T(8,128)(2,1)}, bf16[512,512]{1,0:T(8,128)(2,1)S(1)}, u32[]{:S(2)}, u32[]{:S(2)}) %collective-permute-start.14) | collective-permute-done | bytes 524320 | tf_op jit(solution)/shard_map/ppermute | solution.py:27
  62.6 1.4 collective-permute-start.15
  64.0 2.9 %collective-permute-start.13 = (bf16[512,512]{1,0:T(8,128)(2,1)S(1)}, bf16[512,512]{1,0:T(8,128)(2,1)S(1)}, u32[]{:S(2)}, u32[]{:S(2)}) collective-permute-start(bf16[512,512]{1,0:T(8,128)(2,1)S(1)} %bitcast.22), channel_id=1, source_target_pairs={{0,7},{1,0},{2,1},{3,2},{4,3},{5,4},{6,5},{7,6},{64,71},{65,64},{6... | collective-permute-start | bytes 1572872 | tf_op jit(solution)/shard_map/ppermute | solution.py:27
  66.9 2.1 %collective-permute-done.15 = bf16[512,256]{1,0:T(8,128)(2,1)S(1)} collective-permute-done((bf16[512,256]{1,0:T(8,128)(2,1)S(1)}, bf16[512,256]{1,0:T(8,128)(2,1)S(1)}, u32[]{:S(2)}, u32[]{:S(2)}) %collective-permute-start.15) | collective-permute-done | bytes 262176 | tf_op jit(solution)/shard_map/ppermute | solution.py:35
  69.1 1.6 %collective-permute-start.21 = (bf16[2,512,256]{2,1,0:T(8,128)(2,1)S(1)}, bf16[2,512,256]{2,1,0:T(8,128)(2,1)S(1)}, u32[]{:S(2)}, u32[]{:S(2)}) collective-permute-start(bf16[2,512,256]{2,1,0:T(8,128)(2,1)S(1)} %pad_maximum_fusion.1), channel_id=1, source_target_pairs={{0,16},{8,24},{16,0},{24,8},{32,48},{40,56},{48,32},{56,40},{64,80... | collective-permute-start | bytes 1572872 | tf_op jit(solution)/shard_map/ppermute | solution.py:35
  70.7 2.1 %collective-permute-start.22 = (bf16[2,512,256]{2,1,0:T(8,128)(2,1)S(1)}, bf16[2,512,256]{2,1,0:T(8,128)(2,1)S(1)}, u32[]{:S(2)}, u32[]{:S(2)}) collective-permute-start(bf16[2,512,256]{2,1,0:T(8,128)(2,1)S(1)} %pad_maximum_fusion.1), channel_id=1, source_target_pairs={{0,48},{8,56},{16,32},{24,40},{32,16},{40,24},{48,0},{56,8},{64,11... | collective-permute-start | bytes 1572872 | tf_op jit(solution)/shard_map/ppermute | solution.py:35
  72.8 6.2 %collective-permute-done.18.refs_6_.refs_4_ = bf16[512,512]{1,0:T(8,128)(2,1)S(1)} collective-permute-done((bf16[512,512]{1,0:T(8,128)(2,1)S(1)}, bf16[512,512]{1,0:T(8,128)(2,1)S(1)}, u32[]{:S(2)}, u32[]{:S(2)}) %collective-permute-start.18) | collective-permute-done | bytes 524320 | tf_op jit(solution)/shard_map/ppermute | solution.py:27
  79.0 3.2 %collective-permute-start.16 = (bf16[512,512]{1,0:T(8,128)(2,1)S(1)}, bf16[512,512]{1,0:T(8,128)(2,1)S(1)}, u32[]{:S(2)}, u32[]{:S(2)}) collective-permute-start(bf16[512,512]{1,0:T(8,128)(2,1)S(1)} %collective-permute-done.13.refs_1_), channel_id=1, source_target_pairs={{0,7},{1,0},{2,1},{3,2},{4,3},{5,4},{6,5},{7,6},{64,71},{65,64},{6... | collective-permute-start | bytes 1572872 | tf_op jit(solution)/shard_map/ppermute | solution.py:27
  82.3 1.6 %collective-permute-start.23 = (bf16[512,256]{1,0:T(8,128)(2,1)S(1)}, bf16[512,256]{1,0:T(8,128)(2,1)S(1)}, u32[]{:S(2)}, u32[]{:S(2)}) collective-permute-start(bf16[512,256]{1,0:T(8,128)(2,1)S(1)} %slice_bitcast_fusion.1), channel_id=1, source_target_pairs={{0,16},{8,24},{16,0},{24,8},{32,48},{40,56},{48,32},{56,40},{64,80... | collective-permute-start | bytes 786440 | tf_op jit(solution)/shard_map/ppermute | solution.py:35
  83.9 2.2 %collective-permute-start.24 = (bf16[512,256]{1,0:T(8,128)(2,1)S(1)}, bf16[512,256]{1,0:T(8,128)(2,1)S(1)}, u32[]{:S(2)}, u32[]{:S(2)}) collective-permute-start(bf16[512,256]{1,0:T(8,128)(2,1)S(1)} %slice_bitcast_fusion), channel_id=1, source_target_pairs={{0,48},{8,56},{16,32},{24,40},{32,16},{40,24},{48,0},{56,8},{64,11... | collective-permute-start | bytes 786440 | tf_op jit(solution)/shard_map/ppermute | solution.py:35
  86.1 5.0 %collective-permute-done.19.refs_5_.refs_3_ = bf16[512,512]{1,0:T(8,128)(2,1)S(1)} collective-permute-done((bf16[512,512]{1,0:T(8,128)(2,1)S(1)}, bf16[512,512]{1,0:T(8,128)(2,1)S(1)}, u32[]{:S(2)}, u32[]{:S(2)}) %collective-permute-start.19) | collective-permute-done | bytes 524320 | tf_op jit(solution)/shard_map/ppermute | solution.py:27
  91.1 3.2 %collective-permute-start.17 = (bf16[512,512]{1,0:T(8,128)(2,1)S(1)}, bf16[512,512]{1,0:T(8,128)(2,1)S(1)}, u32[]{:S(2)}, u32[]{:S(2)}) collective-permute-start(bf16[512,512]{1,0:T(8,128)(2,1)S(1)} %collective-permute-done.16.refs_2_), channel_id=1, source_target_pairs={{0,7},{1,0},{2,1},{3,2},{4,3},{5,4},{6,5},{7,6},{64,71},{65,64},{6... | collective-permute-start | bytes 1572872 | tf_op jit(solution)/shard_map/ppermute | solution.py:27
  94.4 1.7 %shard_map.41.refs_2_ = f32[512,256]{1,0:T(8,128)S(1)} custom-call(s32[8]{0:T(128)S(1)} %fusion.order, bf16[8,512,256]{2,1,0:T(8,128)(2,1)S(1)} %constant_dynamic-update-slice_fusion.5.shots, bf16[512,512]{1,0:T(8,128)(2,1)S(1)} %bitcast.23, bf16[512,512]{1,0:T(8,128)(2,1)S(1)} %collective-permute-done.13.refs_1_, ...), custom_call_target="tpu_custom_call" | custom-call | flops 805306368 | bytes 4718592 | tf_op jit(solution)/shard_map/pallas_call | solution.py:114
  96.1 5.3 %collective-permute-done.20.refs_4_.refs_1_ = bf16[512,512]{1,0:T(8,128)(2,1)S(1)} collective-permute-done((bf16[512,512]{1,0:T(8,128)(2,1)S(1)}, bf16[512,512]{1,0:T(8,128)(2,1)S(1)}, u32[]{:S(2)}, u32[]{:S(2)}) %collective-permute-start.20) | collective-permute-done | bytes 524320 | tf_op jit(solution)/shard_map/ppermute | solution.py:27
  101.5 1.2 shard_map.42
  102.7 2.7 %collective-permute-start.28 = (bf16[512,256]{1,0:T(8,128)(2,1)S(1)}, bf16[512,256]{1,0:T(8,128)(2,1)S(1)}, u32[]{:S(2)}, u32[]{:S(2)}) collective-permute-start(bf16[512,256]{1,0:T(8,128)(2,1)S(1)} %get-tuple-element.31), channel_id=1, source_target_pairs={{0,80},{8,88},{16,64},{24,72},{32,112},{40,120},{48,96},{56,104},{... | collective-permute-start | bytes 786440 | tf_op jit(solution)/shard_map/ppermute | solution.py:35
  106.3 6.1 %collective-permute-done.25.refs_3_ = bf16[512,256]{1,0:T(8,128)(2,1)S(1)} collective-permute-done((bf16[512,256]{1,0:T(8,128)(2,1)S(1)}, bf16[512,256]{1,0:T(8,128)(2,1)S(1)}, u32[]{:S(2)}, u32[]{:S(2)}) %collective-permute-start.25) | collective-permute-done | bytes 262176 | tf_op jit(solution)/shard_map/ppermute | solution.py:35
  113.9 1.3 collective-permute-start.33
  115.1 5.6 %collective-permute-done.26.refs_6_ = bf16[512,256]{1,0:T(8,128)(2,1)S(1)} collective-permute-done((bf16[512,256]{1,0:T(8,128)(2,1)S(1)}, bf16[512,256]{1,0:T(8,128)(2,1)S(1)}, u32[]{:S(2)}, u32[]{:S(2)}) %collective-permute-start.26) | collective-permute-done | bytes 262176 | tf_op jit(solution)/shard_map/ppermute | solution.py:35
  121.3 1.2 collective-permute-done.29.refs_5_
  122.5 1.4 collective-permute-start.30
  124.2 1.8 %shard_map.43.refs_2_ = f32[512,256]{1,0:T(8,128)S(1)} custom-call(s32[8]{0:T(128)S(1)} %and_select_fusion.1.order, bf16[8,512,512]{2,1,0:T(8,128)(2,1)S(1)} %shard_map.40.operator, bf16[2,512,256]{2,1,0:T(8,128)(2,1)S(1)} %collective-permute-done.31.refs_0_, bf16[512,256]{1,0:T(8,128)(2,1)S(1)} %collective-permute-done.32.refs_1_, ...), custom_call_target="tpu_custom_call" | custom-call | flops 939524096 | bytes 5505024 | tf_op jit(solution)/shard_map/pallas_call | solution.py:176
  126.1 1.4 collective-permute-done.30.refs_1_
  128.5 1.7 %collective-permute-start.34 = (bf16[512,256]{1,0:T(8,128)(2,1)S(1)}, bf16[512,256]{1,0:T(8,128)(2,1)S(1)}, u32[]{:S(2)}, u32[]{:S(2)}) collective-permute-start(bf16[512,256]{1,0:T(8,128)(2,1)S(1)} %shard_map.44.refs_0_), channel_id=1, source_target_pairs={{0,48},{8,56},{16,32},{24,40},{32,16},{40,24},{48,0},{56,8},{64,11... | collective-permute-start | bytes 786440 | tf_op jit(solution)/shard_map/ppermute | solution.py:35
  130.9 5.6 %collective-permute-done.34.refs_3_ = bf16[512,256]{1,0:T(8,128)(2,1)S(1)} collective-permute-done((bf16[512,256]{1,0:T(8,128)(2,1)S(1)}, bf16[512,256]{1,0:T(8,128)(2,1)S(1)}, u32[]{:S(2)}, u32[]{:S(2)}) %collective-permute-start.34) | collective-permute-done | bytes 262176 | tf_op jit(solution)/shard_map/ppermute | solution.py:35
  136.4 1.3 collective-permute-start.35
  138.6 2.8 %collective-permute-start.41 = (bf16[512,256]{1,0:T(8,128)(2,1)S(1)}, bf16[512,256]{1,0:T(8,128)(2,1)S(1)}, u32[]{:S(2)}, u32[]{:S(2)}) collective-permute-start(bf16[512,256]{1,0:T(8,128)(2,1)S(1)} %collective-permute-done.40.refs_1_), channel_id=1, source_target_pairs={{0,16},{8,24},{16,0},{24,8},{32,48},{40,56},{48,32},{56,40},{64,80... | collective-permute-start | bytes 786440 | tf_op jit(solution)/shard_map/ppermute | solution.py:35
  141.4 1.4 collective-permute-done.35.refs_6_
  142.8 1.6 %collective-permute-start.36 = (bf16[256,256]{1,0:T(8,128)(2,1)S(1)}, bf16[256,256]{1,0:T(8,128)(2,1)S(1)}, u32[]{:S(2)}, u32[]{:S(2)}) collective-permute-start(bf16[256,256]{1,0:T(8,128)(2,1)S(1)} %slice.26), channel_id=1, source_target_pairs={{0,16},{8,24},{16,0},{24,8},{32,48},{40,56},{48,32},{56,40},{64,80... | collective-permute-start | bytes 393224 | tf_op jit(solution)/shard_map/ppermute | solution.py:35
  146.1 1.2 shard_map.37.operator
  147.4 1.8 %shard_map.45.refs_2_ = f32[512,256]{1,0:T(8,128)S(1)} custom-call(s32[8]{0:T(128)S(1)} %and_select_fusion.1.order, bf16[8,512,512]{2,1,0:T(8,128)(2,1)S(1)} %shard_map.37.operator, bf16[512,256]{1,0:T(8,128)(2,1)S(1)} %shard_map.44.refs_0_, bf16[512,256]{1,0:T(8,128)(2,1)S(1)} %collective-permute-done.40.refs_1_, ...), custom_call_target="tpu_custom_call" | custom-call | flops 939524096 | bytes 5505024 | tf_op jit(solution)/shard_map/pallas_call | solution.py:176
  149.2 1.1 collective-permute-done.39.refs_1_
  150.4 1.7 %shard_map.46 = bf16[512,256]{1,0:T(8,128)(2,1)} custom-call(s32[8]{0:T(128)S(1)} %and_select_fusion.1.order, bf16[8,512,512]{2,1,0:T(8,128)(2,1)S(1)} %shard_map.37.operator, bf16[256,256]{1,0:T(8,128)(2,1)S(1)} %collective-permute-done.36.refs_0_, bf16[256,256]{1,0:T(8,128)(2,1)S(1)} %collective-permute-done.39.refs_1_, f32[512,256]{1,0:T(8,128)S(1)} %shard_map.45.refs_2_), custom_call_target="tpu_custom_call" | custom-call | flops 134217728 | bytes 786432 | tf_op jit(solution)/shard_map/pallas_call | solution.py:176
  (71 shorter events, 13.0 us)
Async XLA Ops:
  0.0 18.0 %collective-permute-start = (bf16[512,512]{1,0:T(8,128)(2,1)}, bf16[512,512]{1,0:T(8,128)(2,1)S(1)}, u32[]{:S(2)}, u32[]{:S(2)}) collective-permute-start(bf16[512,512]{1,0:T(8,128)(2,1)} %bitcast.28), channel_id=1, source_target_pairs={{0,64},{8,72},{16,80},{24,88},{32,96},{40,104},{48,112},{56,120},{... | collective-permute-start | bytes 1572872 | tf_op jit(solution)/shard_map/ppermute | solution.py:35
  0.0 18.5 %collective-permute-start.10 = (bf16[512,512]{1,0:T(8,128)(2,1)}, bf16[512,512]{1,0:T(8,128)(2,1)S(1)}, u32[]{:S(2)}, u32[]{:S(2)}) collective-permute-start(bf16[512,512]{1,0:T(8,128)(2,1)} %bitcast.29), channel_id=1, source_target_pairs={{0,65},{1,66},{2,67},{3,68},{4,69},{5,70},{6,71},{7,64},{64,1},{65... | collective-permute-start | bytes 1572872 | tf_op jit(solution)/shard_map/ppermute | solution.py:27
  2.0 16.4 %collective-permute-start.1 = (bf16[512,512]{1,0:T(8,128)(2,1)}, bf16[512,512]{1,0:T(8,128)(2,1)S(1)}, u32[]{:S(2)}, u32[]{:S(2)}) collective-permute-start(bf16[512,512]{1,0:T(8,128)(2,1)} %bitcast.30), channel_id=1, source_target_pairs={{0,71},{1,64},{2,65},{3,66},{4,67},{5,68},{6,69},{7,70},{64,7},{65... | collective-permute-start | bytes 1572872 | tf_op jit(solution)/shard_map/ppermute | solution.py:27
  6.0 1.7 %collective-permute-start.2 = (bf16[512,256]{1,0:T(8,128)(2,1)}, bf16[512,256]{1,0:T(8,128)(2,1)S(1)}, u32[]{:S(2)}, u32[]{:S(2)}) collective-permute-start(bf16[512,256]{1,0:T(8,128)(2,1)} %bitcast.31), channel_id=1, source_target_pairs={{0,64},{8,72},{16,80},{24,88},{32,96},{40,104},{48,112},{56,120},{... | collective-permute-start | bytes 786440 | tf_op jit(solution)/shard_map/ppermute | solution.py:35
  6.1 8.2 %collective-permute-start.3 = (bf16[512,256]{1,0:T(8,128)(2,1)}, bf16[512,256]{1,0:T(8,128)(2,1)S(1)}, u32[]{:S(2)}, u32[]{:S(2)}) collective-permute-start(bf16[512,256]{1,0:T(8,128)(2,1)} %bitcast.32), channel_id=1, source_target_pairs={{0,72},{8,64},{16,88},{24,80},{32,104},{40,96},{48,120},{56,112},{... | collective-permute-start | bytes 786440 | tf_op jit(solution)/shard_map/ppermute | solution.py:35
  7.7 10.3 %copy-start.1 = (bf16[512,256]{1,0:T(8,128)(2,1)}, bf16[512,256]{1,0:T(8,128)(2,1)S(1)}, u32[]{:S(2)}) copy-start(bf16[512,256]{1,0:T(8,128)(2,1)S(1)} %collective-permute-done.2) | copy-start | bytes 786436
  14.4 17.2 %collective-permute-start.5 = (bf16[2,512,256]{2,1,0:T(8,128)(2,1)S(1)}, bf16[2,512,256]{2,1,0:T(8,128)(2,1)}, u32[]{:S(2)}, u32[]{:S(2)}) collective-permute-start(bf16[2,512,256]{2,1,0:T(8,128)(2,1)S(1)} %pad_maximum_fusion), channel_id=1, source_target_pairs={{0,16},{8,24},{16,0},{24,8},{32,48},{40,56},{48,32},{56,40},{64,80... | collective-permute-start | bytes 1572872 | tf_op jit(solution)/shard_map/ppermute | solution.py:35
  15.9 15.6 %collective-permute-start.6 = (bf16[2,512,256]{2,1,0:T(8,128)(2,1)S(1)}, bf16[2,512,256]{2,1,0:T(8,128)(2,1)}, u32[]{:S(2)}, u32[]{:S(2)}) collective-permute-start(bf16[2,512,256]{2,1,0:T(8,128)(2,1)S(1)} %pad_maximum_fusion), channel_id=1, source_target_pairs={{0,48},{8,56},{16,32},{24,40},{32,16},{40,24},{48,0},{56,8},{64,11... | collective-permute-start | bytes 1572872 | tf_op jit(solution)/shard_map/ppermute | solution.py:35
  18.5 15.2 %collective-permute-start.11 = (bf16[512,512]{1,0:T(8,128)(2,1)S(1)}, bf16[512,512]{1,0:T(8,128)(2,1)S(1)}, u32[]{:S(2)}, u32[]{:S(2)}) collective-permute-start(bf16[512,512]{1,0:T(8,128)(2,1)S(1)} %collective-permute-done.10.refs_7_.refs_6_), channel_id=1, source_target_pairs={{0,1},{1,2},{2,3},{3,4},{4,5},{5,6},{6,7},{7,0},{64,65},{65,66},{6... | collective-permute-start | bytes 1572872 | tf_op jit(solution)/shard_map/ppermute | solution.py:27
  18.5 15.2 %collective-permute-start.4 = (bf16[512,512]{1,0:T(8,128)(2,1)S(1)}, bf16[512,512]{1,0:T(8,128)(2,1)S(1)}, u32[]{:S(2)}, u32[]{:S(2)}) collective-permute-start(bf16[512,512]{1,0:T(8,128)(2,1)S(1)} %collective-permute-done.1.refs_1_), channel_id=1, source_target_pairs={{0,7},{1,0},{2,1},{3,2},{4,3},{5,4},{6,5},{7,6},{64,71},{65,64},{6... | collective-permute-start | bytes 1572872 | tf_op jit(solution)/shard_map/ppermute | solution.py:27
  31.5 13.8 %collective-permute-start.8 = (bf16[2,512,256]{2,1,0:T(8,128)(2,1)}, bf16[2,512,256]{2,1,0:T(8,128)(2,1)}, u32[]{:S(2)}, u32[]{:S(2)}) collective-permute-start(bf16[2,512,256]{2,1,0:T(8,128)(2,1)} %collective-permute-done.6), channel_id=1, source_target_pairs={{0,16},{8,24},{16,0},{24,8},{32,48},{40,56},{48,32},{56,40},{64,80... | collective-permute-start | bytes 1572872 | tf_op jit(solution)/shard_map/ppermute | solution.py:35
  33.6 14.3 %collective-permute-start.12 = (bf16[512,512]{1,0:T(8,128)(2,1)S(1)}, bf16[512,512]{1,0:T(8,128)(2,1)S(1)}, u32[]{:S(2)}, u32[]{:S(2)}) collective-permute-start(bf16[512,512]{1,0:T(8,128)(2,1)S(1)} %collective-permute-done.11.refs_6_.refs_5_), channel_id=1, source_target_pairs={{0,1},{1,2},{2,3},{3,4},{4,5},{5,6},{6,7},{7,0},{64,65},{65,66},{6... | collective-permute-start | bytes 1572872 | tf_op jit(solution)/shard_map/ppermute | solution.py:27
  33.6 14.3 %collective-permute-start.7 = (bf16[512,512]{1,0:T(8,128)(2,1)S(1)}, bf16[512,512]{1,0:T(8,128)(2,1)}, u32[]{:S(2)}, u32[]{:S(2)}) collective-permute-start(bf16[512,512]{1,0:T(8,128)(2,1)S(1)} %collective-permute-done.4.refs_2_), channel_id=1, source_target_pairs={{0,7},{1,0},{2,1},{3,2},{4,3},{5,4},{6,5},{7,6},{64,71},{65,64},{6... | collective-permute-start | bytes 1572872 | tf_op jit(solution)/shard_map/ppermute | solution.py:27
  48.0 13.6 %collective-permute-start.14 = (bf16[512,512]{1,0:T(8,128)(2,1)}, bf16[512,512]{1,0:T(8,128)(2,1)S(1)}, u32[]{:S(2)}, u32[]{:S(2)}) collective-permute-start(bf16[512,512]{1,0:T(8,128)(2,1)} %bitcast.21), channel_id=1, source_target_pairs={{0,1},{1,2},{2,3},{3,4},{4,5},{5,6},{6,7},{7,0},{64,65},{65,66},{6... | collective-permute-start | bytes 1572872 | tf_op jit(solution)/shard_map/ppermute | solution.py:27
  48.0 13.6 %collective-permute-start.9 = (bf16[512,512]{1,0:T(8,128)(2,1)}, bf16[512,512]{1,0:T(8,128)(2,1)S(1)}, u32[]{:S(2)}, u32[]{:S(2)}) collective-permute-start(bf16[512,512]{1,0:T(8,128)(2,1)} %collective-permute-done.7.refs_3_), channel_id=1, source_target_pairs={{0,7},{1,0},{2,1},{3,2},{4,3},{5,4},{6,5},{7,6},{64,71},{65,64},{6... | collective-permute-start | bytes 1572872 | tf_op jit(solution)/shard_map/ppermute | solution.py:27
  56.8 7.2 %copy-start = (bf16[1,512,512]{2,1,0:T(8,128)(2,1)S(1)}, bf16[1,512,512]{2,1,0:T(8,128)(2,1)}, u32[]{:S(2)}) copy-start(bf16[1,512,512]{2,1,0:T(8,128)(2,1)} %param.3) | copy-start | bytes 1572868
  62.6 6.5 %collective-permute-start.15 = (bf16[512,256]{1,0:T(8,128)(2,1)S(1)}, bf16[512,256]{1,0:T(8,128)(2,1)S(1)}, u32[]{:S(2)}, u32[]{:S(2)}) collective-permute-start(bf16[512,256]{1,0:T(8,128)(2,1)S(1)} %shard_map.39.refs_3_), channel_id=1, source_target_pairs={{0,8},{8,0},{16,24},{24,16},{32,40},{40,32},{48,56},{56,48},{64,72... | collective-permute-start | bytes 786440 | tf_op jit(solution)/shard_map/ppermute | solution.py:35
  64.0 15.0 %collective-permute-start.13 = (bf16[512,512]{1,0:T(8,128)(2,1)S(1)}, bf16[512,512]{1,0:T(8,128)(2,1)S(1)}, u32[]{:S(2)}, u32[]{:S(2)}) collective-permute-start(bf16[512,512]{1,0:T(8,128)(2,1)S(1)} %bitcast.22), channel_id=1, source_target_pairs={{0,7},{1,0},{2,1},{3,2},{4,3},{5,4},{6,5},{7,6},{64,71},{65,64},{6... | collective-permute-start | bytes 1572872 | tf_op jit(solution)/shard_map/ppermute | solution.py:27
  66.9 12.1 %collective-permute-start.18 = (bf16[512,512]{1,0:T(8,128)(2,1)S(1)}, bf16[512,512]{1,0:T(8,128)(2,1)S(1)}, u32[]{:S(2)}, u32[]{:S(2)}) collective-permute-start(bf16[512,512]{1,0:T(8,128)(2,1)S(1)} %collective-permute-done.14.refs_7_.refs_5_), channel_id=1, source_target_pairs={{0,1},{1,2},{2,3},{3,4},{4,5},{5,6},{6,7},{7,0},{64,65},{65,66},{6... | collective-permute-start | bytes 1572872 | tf_op jit(solution)/shard_map/ppermute | solution.py:27
  69.1 13.1 %collective-permute-start.21 = (bf16[2,512,256]{2,1,0:T(8,128)(2,1)S(1)}, bf16[2,512,256]{2,1,0:T(8,128)(2,1)S(1)}, u32[]{:S(2)}, u32[]{:S(2)}) collective-permute-start(bf16[2,512,256]{2,1,0:T(8,128)(2,1)S(1)} %pad_maximum_fusion.1), channel_id=1, source_target_pairs={{0,16},{8,24},{16,0},{24,8},{32,48},{40,56},{48,32},{56,40},{64,80... | collective-permute-start | bytes 1572872 | tf_op jit(solution)/shard_map/ppermute | solution.py:35
  70.7 11.6 %collective-permute-start.22 = (bf16[2,512,256]{2,1,0:T(8,128)(2,1)S(1)}, bf16[2,512,256]{2,1,0:T(8,128)(2,1)S(1)}, u32[]{:S(2)}, u32[]{:S(2)}) collective-permute-start(bf16[2,512,256]{2,1,0:T(8,128)(2,1)S(1)} %pad_maximum_fusion.1), channel_id=1, source_target_pairs={{0,48},{8,56},{16,32},{24,40},{32,16},{40,24},{48,0},{56,8},{64,11... | collective-permute-start | bytes 1572872 | tf_op jit(solution)/shard_map/ppermute | solution.py:35
  79.0 12.1 %collective-permute-start.19 = (bf16[512,512]{1,0:T(8,128)(2,1)S(1)}, bf16[512,512]{1,0:T(8,128)(2,1)S(1)}, u32[]{:S(2)}, u32[]{:S(2)}) collective-permute-start(bf16[512,512]{1,0:T(8,128)(2,1)S(1)} %collective-permute-done.18.refs_6_.refs_4_), channel_id=1, source_target_pairs={{0,1},{1,2},{2,3},{3,4},{4,5},{5,6},{6,7},{7,0},{64,65},{65,66},{6... | collective-permute-start | bytes 1572872 | tf_op jit(solution)/shard_map/ppermute | solution.py:27
  79.0 12.1 %collective-permute-start.16 = (bf16[512,512]{1,0:T(8,128)(2,1)S(1)}, bf16[512,512]{1,0:T(8,128)(2,1)S(1)}, u32[]{:S(2)}, u32[]{:S(2)}) collective-permute-start(bf16[512,512]{1,0:T(8,128)(2,1)S(1)} %collective-permute-done.13.refs_1_), channel_id=1, source_target_pairs={{0,7},{1,0},{2,1},{3,2},{4,3},{5,4},{6,5},{7,6},{64,71},{65,64},{6... | collective-permute-start | bytes 1572872 | tf_op jit(solution)/shard_map/ppermute | solution.py:27
  82.3 12.1 %collective-permute-start.23 = (bf16[512,256]{1,0:T(8,128)(2,1)S(1)}, bf16[512,256]{1,0:T(8,128)(2,1)S(1)}, u32[]{:S(2)}, u32[]{:S(2)}) collective-permute-start(bf16[512,256]{1,0:T(8,128)(2,1)S(1)} %slice_bitcast_fusion.1), channel_id=1, source_target_pairs={{0,16},{8,24},{16,0},{24,8},{32,48},{40,56},{48,32},{56,40},{64,80... | collective-permute-start | bytes 786440 | tf_op jit(solution)/shard_map/ppermute | solution.py:35
  83.9 10.5 %collective-permute-start.24 = (bf16[512,256]{1,0:T(8,128)(2,1)S(1)}, bf16[512,256]{1,0:T(8,128)(2,1)S(1)}, u32[]{:S(2)}, u32[]{:S(2)}) collective-permute-start(bf16[512,256]{1,0:T(8,128)(2,1)S(1)} %slice_bitcast_fusion), channel_id=1, source_target_pairs={{0,48},{8,56},{16,32},{24,40},{32,16},{40,24},{48,0},{56,8},{64,11... | collective-permute-start | bytes 786440 | tf_op jit(solution)/shard_map/ppermute | solution.py:35
  91.1 10.4 %collective-permute-start.20 = (bf16[512,512]{1,0:T(8,128)(2,1)S(1)}, bf16[512,512]{1,0:T(8,128)(2,1)S(1)}, u32[]{:S(2)}, u32[]{:S(2)}) collective-permute-start(bf16[512,512]{1,0:T(8,128)(2,1)S(1)} %collective-permute-done.19.refs_5_.refs_3_), channel_id=1, source_target_pairs={{0,1},{1,2},{2,3},{3,4},{4,5},{5,6},{6,7},{7,0},{64,65},{65,66},{6... | collective-permute-start | bytes 1572872 | tf_op jit(solution)/shard_map/ppermute | solution.py:27
  91.1 10.4 %collective-permute-start.17 = (bf16[512,512]{1,0:T(8,128)(2,1)S(1)}, bf16[512,512]{1,0:T(8,128)(2,1)S(1)}, u32[]{:S(2)}, u32[]{:S(2)}) collective-permute-start(bf16[512,512]{1,0:T(8,128)(2,1)S(1)} %collective-permute-done.16.refs_2_), channel_id=1, source_target_pairs={{0,7},{1,0},{2,1},{3,2},{4,3},{5,4},{6,5},{7,6},{64,71},{65,64},{6... | collective-permute-start | bytes 1572872 | tf_op jit(solution)/shard_map/ppermute | solution.py:27
  102.6 9.8 %collective-permute-start.25 = (bf16[512,256]{1,0:T(8,128)(2,1)S(1)}, bf16[512,256]{1,0:T(8,128)(2,1)S(1)}, u32[]{:S(2)}, u32[]{:S(2)}) collective-permute-start(bf16[512,256]{1,0:T(8,128)(2,1)S(1)} %get-tuple-element.31), channel_id=1, source_target_pairs={{0,112},{8,120},{16,96},{24,104},{32,80},{40,88},{48,64},{56,72},{... | collective-permute-start | bytes 786440 | tf_op jit(solution)/shard_map/ppermute | solution.py:35
  102.7 10.4 %collective-permute-start.28 = (bf16[512,256]{1,0:T(8,128)(2,1)S(1)}, bf16[512,256]{1,0:T(8,128)(2,1)S(1)}, u32[]{:S(2)}, u32[]{:S(2)}) collective-permute-start(bf16[512,256]{1,0:T(8,128)(2,1)S(1)} %get-tuple-element.31), channel_id=1, source_target_pairs={{0,80},{8,88},{16,64},{24,72},{32,112},{40,120},{48,96},{56,104},{... | collective-permute-start | bytes 786440 | tf_op jit(solution)/shard_map/ppermute | solution.py:35
  105.4 8.4 %collective-permute-start.32 = (bf16[512,256]{1,0:T(8,128)(2,1)S(1)}, bf16[512,256]{1,0:T(8,128)(2,1)S(1)}, u32[]{:S(2)}, u32[]{:S(2)}) collective-permute-start(bf16[512,256]{1,0:T(8,128)(2,1)S(1)} %get-tuple-element.31), channel_id=1, source_target_pairs={{0,72},{8,64},{16,88},{24,80},{32,104},{40,96},{48,120},{56,112},{... | collective-permute-start | bytes 786440 | tf_op jit(solution)/shard_map/ppermute | solution.py:35
  106.0 18.3 %collective-permute-start.31 = (bf16[2,512,256]{2,1,0:T(8,128)(2,1)S(1)}, bf16[2,512,256]{2,1,0:T(8,128)(2,1)S(1)}, u32[]{:S(2)}, u32[]{:S(2)}) collective-permute-start(bf16[2,512,256]{2,1,0:T(8,128)(2,1)S(1)} %get-tuple-element.32), channel_id=1, source_target_pairs={{0,64},{8,72},{16,80},{24,88},{32,96},{40,104},{48,112},{56,120},{... | collective-permute-start | bytes 1572872 | tf_op jit(solution)/shard_map/ppermute | solution.py:35
  112.4 8.3 %collective-permute-start.26 = (bf16[512,256]{1,0:T(8,128)(2,1)S(1)}, bf16[512,256]{1,0:T(8,128)(2,1)S(1)}, u32[]{:S(2)}, u32[]{:S(2)}) collective-permute-start(bf16[512,256]{1,0:T(8,128)(2,1)S(1)} %collective-permute-done.25.refs_3_), channel_id=1, source_target_pairs={{0,8},{8,0},{16,24},{24,16},{32,40},{40,32},{48,56},{56,48},{64,72... | collective-permute-start | bytes 786440 | tf_op jit(solution)/shard_map/ppermute | solution.py:35
  113.2 9.3 %collective-permute-start.29 = (bf16[512,256]{1,0:T(8,128)(2,1)S(1)}, bf16[512,256]{1,0:T(8,128)(2,1)S(1)}, u32[]{:S(2)}, u32[]{:S(2)}) collective-permute-start(bf16[512,256]{1,0:T(8,128)(2,1)S(1)} %collective-permute-done.28.refs_2_), channel_id=1, source_target_pairs={{0,48},{8,56},{16,32},{24,40},{32,16},{40,24},{48,0},{56,8},{64,11... | collective-permute-start | bytes 786440 | tf_op jit(solution)/shard_map/ppermute | solution.py:35
  113.9 10.4 %collective-permute-start.33 = (bf16[512,256]{1,0:T(8,128)(2,1)S(1)}, bf16[512,256]{1,0:T(8,128)(2,1)S(1)}, u32[]{:S(2)}, u32[]{:S(2)}) collective-permute-start(bf16[512,256]{1,0:T(8,128)(2,1)S(1)} %collective-permute-done.32.refs_1_), channel_id=1, source_target_pairs={{0,16},{8,24},{16,0},{24,8},{32,48},{40,56},{48,32},{56,40},{64,80... | collective-permute-start | bytes 786440 | tf_op jit(solution)/shard_map/ppermute | solution.py:35
  120.8 5.3 %collective-permute-start.27 = (bf16[256,256]{1,0:T(8,128)(2,1)S(1)}, bf16[256,256]{1,0:T(8,128)(2,1)S(1)}, u32[]{:S(2)}, u32[]{:S(2)}) collective-permute-start(bf16[256,256]{1,0:T(8,128)(2,1)S(1)} %slice.24), channel_id=1, source_target_pairs={{0,16},{8,24},{16,0},{24,8},{32,48},{40,56},{48,32},{56,40},{64,80... | collective-permute-start | bytes 393224 | tf_op jit(solution)/shard_map/ppermute | solution.py:35
  122.5 5.1 %collective-permute-start.30 = (bf16[256,256]{1,0:T(8,128)(2,1)S(1)}, bf16[256,256]{1,0:T(8,128)(2,1)S(1)}, u32[]{:S(2)}, u32[]{:S(2)}) collective-permute-start(bf16[256,256]{1,0:T(8,128)(2,1)S(1)} %slice.25), channel_id=1, source_target_pairs={{0,8},{8,0},{16,24},{24,16},{32,40},{40,32},{48,56},{56,48},{64,72... | collective-permute-start | bytes 393224 | tf_op jit(solution)/shard_map/ppermute | solution.py:35
  128.5 7.9 %collective-permute-start.34 = (bf16[512,256]{1,0:T(8,128)(2,1)S(1)}, bf16[512,256]{1,0:T(8,128)(2,1)S(1)}, u32[]{:S(2)}, u32[]{:S(2)}) collective-permute-start(bf16[512,256]{1,0:T(8,128)(2,1)S(1)} %shard_map.44.refs_0_), channel_id=1, source_target_pairs={{0,48},{8,56},{16,32},{24,40},{32,16},{40,24},{48,0},{56,8},{64,11... | collective-permute-start | bytes 786440 | tf_op jit(solution)/shard_map/ppermute | solution.py:35
  130.2 7.5 %collective-permute-start.37 = (bf16[512,256]{1,0:T(8,128)(2,1)S(1)}, bf16[512,256]{1,0:T(8,128)(2,1)S(1)}, u32[]{:S(2)}, u32[]{:S(2)}) collective-permute-start(bf16[512,256]{1,0:T(8,128)(2,1)S(1)} %shard_map.44.refs_0_), channel_id=1, source_target_pairs={{0,16},{8,24},{16,0},{24,8},{32,48},{40,56},{48,32},{56,40},{64,80... | collective-permute-start | bytes 786440 | tf_op jit(solution)/shard_map/ppermute | solution.py:35
  130.2 8.4 %collective-permute-start.40 = (bf16[512,256]{1,0:T(8,128)(2,1)S(1)}, bf16[512,256]{1,0:T(8,128)(2,1)S(1)}, u32[]{:S(2)}, u32[]{:S(2)}) collective-permute-start(bf16[512,256]{1,0:T(8,128)(2,1)S(1)} %shard_map.44.refs_0_), channel_id=1, source_target_pairs={{0,8},{8,0},{16,24},{24,16},{32,40},{40,32},{48,56},{56,48},{64,72... | collective-permute-start | bytes 786440 | tf_op jit(solution)/shard_map/ppermute | solution.py:35
  136.4 6.4 %collective-permute-start.35 = (bf16[512,256]{1,0:T(8,128)(2,1)S(1)}, bf16[512,256]{1,0:T(8,128)(2,1)S(1)}, u32[]{:S(2)}, u32[]{:S(2)}) collective-permute-start(bf16[512,256]{1,0:T(8,128)(2,1)S(1)} %collective-permute-done.34.refs_3_), channel_id=1, source_target_pairs={{0,8},{8,0},{16,24},{24,16},{32,40},{40,32},{48,56},{56,48},{64,72... | collective-permute-start | bytes 786440 | tf_op jit(solution)/shard_map/ppermute | solution.py:35
  137.7 7.6 %collective-permute-start.38 = (bf16[512,256]{1,0:T(8,128)(2,1)S(1)}, bf16[512,256]{1,0:T(8,128)(2,1)S(1)}, u32[]{:S(2)}, u32[]{:S(2)}) collective-permute-start(bf16[512,256]{1,0:T(8,128)(2,1)S(1)} %collective-permute-done.37.refs_2_), channel_id=1, source_target_pairs={{0,48},{8,56},{16,32},{24,40},{32,16},{40,24},{48,0},{56,8},{64,11... | collective-permute-start | bytes 786440 | tf_op jit(solution)/shard_map/ppermute | solution.py:35
  138.6 8.7 %collective-permute-start.41 = (bf16[512,256]{1,0:T(8,128)(2,1)S(1)}, bf16[512,256]{1,0:T(8,128)(2,1)S(1)}, u32[]{:S(2)}, u32[]{:S(2)}) collective-permute-start(bf16[512,256]{1,0:T(8,128)(2,1)S(1)} %collective-permute-done.40.refs_1_), channel_id=1, source_target_pairs={{0,16},{8,24},{16,0},{24,8},{32,48},{40,56},{48,32},{56,40},{64,80... | collective-permute-start | bytes 786440 | tf_op jit(solution)/shard_map/ppermute | solution.py:35
  142.8 6.4 %collective-permute-start.36 = (bf16[256,256]{1,0:T(8,128)(2,1)S(1)}, bf16[256,256]{1,0:T(8,128)(2,1)S(1)}, u32[]{:S(2)}, u32[]{:S(2)}) collective-permute-start(bf16[256,256]{1,0:T(8,128)(2,1)S(1)} %slice.26), channel_id=1, source_target_pairs={{0,16},{8,24},{16,0},{24,8},{32,48},{40,56},{48,32},{56,40},{64,80... | collective-permute-start | bytes 393224 | tf_op jit(solution)/shard_map/ppermute | solution.py:35
  145.3 5.1 %collective-permute-start.39 = (bf16[256,256]{1,0:T(8,128)(2,1)S(1)}, bf16[256,256]{1,0:T(8,128)(2,1)S(1)}, u32[]{:S(2)}, u32[]{:S(2)}) collective-permute-start(bf16[256,256]{1,0:T(8,128)(2,1)S(1)} %slice.27), channel_id=1, source_target_pairs={{0,8},{8,0},{16,24},{24,16},{32,40},{40,32},{48,56},{56,48},{64,72... | collective-permute-start | bytes 393224 | tf_op jit(solution)/shard_map/ppermute | solution.py:35
